TPU v7x, 256 devices: a whole 4x4x8 slice. The times are simulated.
256 devices in a mesh: src: 16 (over x, z_lo), rcv: 16 (over z_hi, y, core).
Axes of the slice: x: 4, y: 4, z: 8 (z_hi: 2, z_lo: 4; z = z_hi * 4 + z_lo), core: 2. Of those that a mesh axis runs over, the one named last changes fastest.
Arguments:
- reflection: bfloat16 [2, 8, 16384, 4096], P(None, None, 'src', 'rcv'), may hold values from -0.25 to 0.25
- focusing: bfloat16 [96, 4096, 128], P('src', 'rcv'), may hold values from -6 to 6
- direct: bfloat16 [96, 4096, 128], P('src', 'rcv'), may hold values from -6 to 6
- onset_source: int32 [96, 16384], P(None, 'src'), may hold values from 32 to 128
- onset_receiver: int32 [96, 4096], P('src', 'rcv'), may hold values from 32 to 128
Outputs:
- upgoing: bfloat16 [96, 16384, 128], P('rcv', 'src')
- refocused: float32 [96, 4096, 128], P('src', 'rcv')
All inputs are finite; a program needn't handle non-finite values.
Results may differ from a plain program's by a relative error of at most 0.022.
Values may be sent and summed in bfloat16 or wider, within the bound.
No kernel may reach another device: no remote copies, remote signals or barrier semaphores. Data moves between devices by JAX's collectives and lax.ppermute only.
A program may use at most 192 MiB of HBM per device.

v0:
```python
import functools
import math

import jax
import jax.numpy as jnp
import numpy as np
from jax import lax
from jax.experimental import pallas as pl
from jax.experimental.pallas import tpu as pltpu
from jax.sharding import PartitionSpec as P

NF = 8
NT = 128
NP = 6
PC = 3
CH = NP // PC
ROWS = 2 * NF * PC
BIN = 2 * PC
NS = 1024
NR = 256
BF = jnp.bfloat16
F32 = jnp.float32


def split(table):
    high = table.astype(BF)
    low = (table - high.astype(np.float32)).astype(BF)
    return high, low


def tables():
    k = np.arange(1, NF + 1)[:, None]
    t = np.arange(NT)[None, :]
    phase = 2.0 * math.pi / NT * ((k * t) % NT)
    return np.cos(phase).astype(np.float32), np.sin(phase).astype(np.float32)


def trace_table():
    cosines, sines = tables()
    return np.concatenate(split(np.stack([cosines, -sines], 1).reshape(2 * NF, NT)))


def spectra_table():
    cosines, sines = tables()
    full = np.zeros((PC, NF, PC, 2, NT), np.float32)
    for j in range(PC):
        full[j, :, j, 0] = cosines
        full[j, :, j, 1] = -sines
    return np.concatenate(split(full.reshape(PC, ROWS, NT)), axis=1)


def samples_table():
    cosines, sines = tables()
    full = np.zeros((PC, NT, NF, PC, 2), np.float32)
    for j in range(PC):
        full[j, :, :, j, 0] = 2.0 / NT * cosines.T
        full[j, :, :, j, 1] = -2.0 / NT * sines.T
    high, low = split(full.reshape(PC, NT, ROWS))
    return np.concatenate([high, high, low], axis=2)


def dot(a, b, ca=1, cb=0):
    return lax.dot_general(a, b, (((ca,), (cb,)), ((), ())), preferred_element_type=F32)


def hi_lo_hi(x, axis):
    high = x.astype(BF)
    low = (x - high.astype(F32)).astype(BF)
    return jnp.concatenate([high, low, high], axis=axis)


def place():
    src = lax.axis_index("src")
    rcv = lax.axis_index("rcv")
    return src // 4, src % 4, rcv // 8, (rcv // 2) % 4, rcv % 2


def call(kernel, out, name, mib=8, **kw):
    return pl.pallas_call(
        kernel,
        out_shape=out,
        name=name,
        compiler_params=pltpu.CompilerParams(vmem_limit_bytes=mib << 20),
        **kw,
    )


def cost(us):
    return pl.CostEstimate(flops=int(us * 1e9), bytes_accessed=1 << 16, transcendentals=0)


def window_of(k, tile):
    low = BIN * k // tile * tile
    high = -(-BIN * (k + 1) // tile) * tile
    return low, high


def merge(parts, t, tile):
    bins = sorted({(8 * t) // BIN, (8 * t + 7) // BIN})
    out = None
    for k in bins:
        value = parts[k][..., 8 * t - window_of(k, tile)[0] :, :][..., :8, :]
        if out is None:
            out = value
        else:
            row = lax.broadcasted_iota(jnp.int32, value.shape, value.ndim - 2) + 8 * t
            out = jnp.where(row < BIN * k, out, value)
    return out


def spectra_kernel(f_ref, t_ref, o_ref):
    rows = []
    for j in range(NP):
        both = dot(t_ref[...], f_ref[j], 1, 1)
        rows.append(both[: 2 * NF] + both[2 * NF :])
    r = lax.broadcasted_iota(jnp.int32, (CH * ROWS, CH * ROWS), 0)
    q = (r * 43) >> 8
    rest = r - BIN * q
    source = ((q >> 3) * PC + (rest >> 1)) * 16 + (q & 7) * 2 + (rest & 1)
    move = (lax.broadcasted_iota(jnp.int32, r.shape, 1) == source).astype(F32).astype(BF)
    o_ref[...] = dot(move, jnp.concatenate(rows, axis=0).astype(BF)).astype(BF)


def swap_rows(x):
    even = lax.broadcasted_iota(jnp.int32, x.shape, 0) % 2 == 0
    n = x.shape[0]
    return jnp.where(even, -pltpu.roll(x, n - 1, 0), pltpu.roll(x, 1, 0))


def conv_kernel(f0, f1, f2, f3, r_ref, give, keep, l1, l2):
    x, zl, zh, y, c = place()
    for dx, ref in enumerate((f0, f1, f2, f3)):
        for dz in range(4):
            xb = lax.rem(x + 4 - dx, 4)
            zb = zl ^ dz
            yb = lax.rem(xb, 2) * 2 + zb // 2
            to = lax.rem(zb + c, 2) * 8 + lax.rem(yb + 4 - y, 4) * 2 + lax.rem(xb // 2 + zh, 2)
            rows = ref[dz].astype(F32)
            l1[to] = rows
            l2[to] = swap_rows(rows)

    sb = 256

    def step(i, carry):
        g, at = i // 4, pl.ds(pl.multiple_of(lax.rem(i, 4) * sb, sb), sb)
        parts = {}
        for k in range(4):
            low, high = window_of(k, 8)
            n = 16 * (high - low)
            rows = pl.ds(pl.multiple_of(g * 24, 8) + low, high - low)
            a1 = l1[:, rows].reshape(n, NR).astype(BF)
            a2 = l2[:, rows].reshape(n, NR).astype(BF)
            v = dot(a1, r_ref[0, 4 * g + k, at, :], 1, 1) + dot(a2, r_ref[1, 4 * g + k, at, :], 1, 1)
            parts[k] = v.reshape(16, high - low, sb)
        out = jnp.concatenate([merge(parts, t, 8) for t in range(3)], axis=1).astype(BF)
        keep[:, g, :, at] = out[:8]
        give[:, g, :, at] = out[8:]
        return carry

    lax.fori_loop(0, 2 * NS // sb, step, 0)


def convolve(pieces, reflection):
    give, keep = call(
        conv_kernel,
        [jax.ShapeDtypeStruct((8, 2, ROWS // 2, NS), BF)] * 2,
        "conv",
        in_specs=[pl.BlockSpec(memory_space=pltpu.VMEM)] * 5,
        scratch_shapes=[pltpu.VMEM((16, ROWS, NR), F32)] * 2,
        cost_estimate=cost(4),
    )(*pieces, reflection)
    return give.reshape(4, 2, ROWS, NS), keep.reshape(4, 2, ROWS, NS)


def window_kernel(p0, p1, p2, p3, r_ref, on_ref, a_ref, t_ref, w_ref, up_ref):
    steps = lax.broadcasted_iota(jnp.int32, (NT, NS), 0)

    def half(i, carry):
        e = 1 - i
        total = (p0[e].astype(F32) + p1[e].astype(F32)) + (p2[e].astype(F32) + p3[e].astype(F32))
        u = hi_lo_hi(total + r_ref[i].astype(F32), 0)
        acc = jnp.zeros((2 * ROWS, NS), F32)
        for j in range(PC):
            field = dot(a_ref[j], u)
            field = jnp.where(steps < on_ref[e, j : j + 1, :], field, 0.0).astype(BF)
            up_ref[j] = field
            acc += dot(t_ref[j], field)
        w_ref[e] = (acc[:ROWS] + acc[ROWS:]).astype(BF)
        return carry

    lax.fori_loop(0, 2, half, 0)


def flip_kernel(a_ref, b_ref, o_ref):
    for i, ref in enumerate((a_ref, b_ref)):
        for j in range(PC):
            o_ref[i * PC + j] = ref[j].T


def load_kernel(r_hbm, o_ref, sem):
    copies = [
        pltpu.make_async_copy(r_hbm.at[part, k], o_ref.at[part, k], sem.at[part, k])
        for k in range(NF)
        for part in range(2)
    ]
    for copy in copies:
        copy.start()
    for copy in copies:
        copy.wait()


def corr_kernel(w0, w1, w2, w3, v0, v1, v2, v3, r_ref, o0, o1, o2, o3, out, acc):
    x, zl, zh, y, c = place()
    refs = (w0, w1, w2, w3, v0, v1, v2, v3)
    row = lax.broadcasted_iota(jnp.int32, (256, NR), 0)
    even = row % 2 == 0

    def step(i, carry):
        for n in range(2):
            p = 2 * i + n
            t = (p >= 3).astype(jnp.int32) + (p >= 7).astype(jnp.int32)
            k = p - t
            at = pl.ds(pl.multiple_of(16 * t, 16), 16)
            m = jnp.concatenate([w[e, at] for w in refs for e in range(2)], axis=0)
            q = dot(m, r_ref[1, k])
            g = dot(m, r_ref[0, k]) + jnp.where(even, pltpu.roll(q, 255, 0), -pltpu.roll(q, 1, 0))
            mine = (row % 16 + 16 * t >= BIN * k) & (row % 16 + 16 * t < BIN * k + BIN)
            acc[t] = jnp.where(mine, g, acc[t])
        return carry

    lax.fori_loop(0, 5, step, 0)
    for i in range(16):
        other, d, e = i // 8, i // 2 % 4, i % 2
        yb = lax.rem(y + 4 - d, 4)
        xb = lax.rem(zh + e, 2) * 2 + yb // 2
        zb = lax.rem(yb, 2) * 2 + lax.rem(c + other, 2)
        out[lax.rem(xb + 4 - x, 4), zb ^ zl] = jnp.concatenate([acc[t, 16 * i : 16 * i + 16] for t in range(3)], axis=0).astype(BF)
    for d, ref in enumerate((o0, o1, o2, o3)):
        ref[...] = out[d]


def correlate(waves, reflection):
    return call(
        corr_kernel,
        [jax.ShapeDtypeStruct((4, ROWS, NR), BF)] * 4,
        "corr",
        in_specs=[pl.BlockSpec(memory_space=pltpu.VMEM)] * 9,
        scratch_shapes=[pltpu.VMEM((4, 4, ROWS, NR), BF), pltpu.VMEM((3, 256, NR), F32)],
        cost_estimate=cost(4),
        mib=16,
    )(*waves, reflection)


def sum_kernel(*refs):
    ins, (keep, *gives) = refs[: 4 * CH], refs[4 * CH :]
    for h in range(CH):
        g = ins[4 * h : 4 * h + 4]
        total = (g[0][...].astype(F32) + g[1][...].astype(F32)) + (g[2][...].astype(F32) + g[3][...].astype(F32))
        keep[h] = total[0]
        for d, give in enumerate(gives):
            give[h] = total[d + 1].astype(BF)


def refocus_kernel(g0, g1, g2, g3, d_ref, on_ref, a_ref, o_ref):
    steps = lax.broadcasted_iota(jnp.int32, (NR, NT), 1)
    for h in range(CH):
        g = (g0[h] + g1[h].astype(F32)) + (g2[h].astype(F32) + g3[h].astype(F32))
        gt = hi_lo_hi(g.T, 1)
        for i in range(PC):
            j = h * PC + i
            field = dot(gt, a_ref[i], 1, 1)
            field = jnp.where(steps < on_ref[:, j : j + 1], field, 0.0)
            o_ref[j] = d_ref[j].astype(F32) + field


def send(value, axis, to):
    return lax.ppermute(value, axis, [(i, to(i)) for i in range(16)])


def to_x(d):
    return lambda i: (i // 4 + d) % 4 * 4 + i % 4


def to_zl(d):
    return lambda i: i ^ d


def to_y(d):
    return lambda i: i // 8 * 8 + (i // 2 % 4 + d) % 4 * 2 + i % 2


def to_zh(i):
    return (i + 8) % 16


def to_core(i):
    return i ^ 1


def together(*lists):
    flat = lax.optimization_barrier(tuple(v for values in lists for v in values))
    out, at = [], 0
    for values in lists:
        out.append(list(flat[at : at + len(values)]))
        at += len(values)
    return out


def on_device(reflection, focusing, direct, onset_source, onset_receiver):
    t_spec = jnp.asarray(spectra_table())
    t_samp = jnp.asarray(samples_table())

    spectra = call(spectra_kernel, jax.ShapeDtypeStruct((CH * ROWS, NR), BF), "spectra")(
        focusing, jnp.asarray(trace_table())
    )
    rcv = lax.axis_index("rcv")
    near_far = [lax.dynamic_slice_in_dim(onset_source, r * NP, NP, 0) for r in (rcv, rcv ^ 8)]
    onsets = [jnp.stack([o[h * PC : (h + 1) * PC] for o in near_far]) for h in range(CH)]
    near = [spectra] + [send(spectra, "src", to_zl(d)) for d in (1, 2, 3)]
    stacks = [jnp.stack([n[h * ROWS : (h + 1) * ROWS] for n in near]) for h in range(CH)]
    [reflection], stacks[:1] = together([reflection], stacks[:1])
    pieces = [[stacks[0]] + [send(stacks[0], "src", to_x(d)) for d in (1, 2, 3)]]
    held = call(
        load_kernel,
        pltpu.VMEM((2, NF, NS, NR), BF),
        "load",
        in_specs=[pl.BlockSpec(memory_space=pltpu.HBM)],
        out_specs=pl.BlockSpec(memory_space=pltpu.VMEM),
        scratch_shapes=[pltpu.SemaphoreType.DMA((2, NF))],
        cost_estimate=cost(3),
        mib=50,
    )(reflection)

    def summed(give, keep):
        got = send(give, "rcv", to_core)
        return [(keep[d].astype(F32) + got[d].astype(F32)).astype(BF) for d in range(4)]

    def over_y(both):
        return [both[0]] + [send(both[d], "rcv", to_y(d)) for d in (1, 2, 3)]

    def half_sum(both):
        return ((both[0].astype(F32) + both[1].astype(F32)) + (both[2].astype(F32) + both[3].astype(F32))).astype(BF)

    def window(both, half, h):
        return call(
            window_kernel,
            (jax.ShapeDtypeStruct((2, ROWS, NS), BF), jax.ShapeDtypeStruct((PC, NT, NS), BF)),
            "window",
            cost_estimate=cost(2),
        )(*both, half, onsets[h], t_samp, t_spec)

    give_a, keep_a = convolve(pieces[0], held)
    [second], [keep_a] = together([stacks[1]], [keep_a])
    pieces.append([second] + [send(second, "src", to_x(d)) for d in (1, 2, 3)])
    sum_a = summed(give_a, keep_a)
    both_a = over_y(sum_a)
    pieces[1][1:], both_a[1:2] = together(pieces[1][1:], both_a[1:2])
    sum_b = summed(*convolve(pieces[1], held))
    both_a[1:], sum_b = together(both_a[1:], sum_b)
    both_b = over_y(sum_b)
    half_a = send(half_sum(both_a), "rcv", to_zh)
    half_b = send(half_sum(both_b), "rcv", to_zh)
    [half_a], both_b = together([half_a], both_b)
    wave_a, field_a = window(both_a, half_a, 0)
    wave_b, field_b = window(both_b, half_b, 1)
    own_a = over_y([wave_a] * 4)
    own_b = over_y([wave_b] * 4)
    upgoing = call(
        flip_kernel, jax.ShapeDtypeStruct((NP, NS, NT), BF), "flip", cost_estimate=cost(2)
    )(field_a, field_b)
    parts = []
    own_a[:1], [upgoing] = together(own_a[:1], [upgoing])

    def over_core(own):
        return [*own, *[send(w, "rcv", to_core) for w in own]]

    def over_x(back):
        return [back[0]] + [send(back[d], "src", to_x(d)) for d in (1, 2, 3)]

    parts_a = over_x(correlate(over_core(own_a), held))
    own_b[1:], parts_a = together(own_b[1:], parts_a)
    parts = parts_a + over_x(correlate(over_core(own_b), held))

    keep, *gives = call(
        sum_kernel,
        [jax.ShapeDtypeStruct((CH, ROWS, NR), F32)] + [jax.ShapeDtypeStruct((CH, ROWS, NR), BF)] * 3,
        "sum_x",
    )(*parts)
    last = [keep] + [send(gives[d - 1], "src", to_zl(d)) for d in (1, 2, 3)]
    refocused = call(refocus_kernel, jax.ShapeDtypeStruct((NP, NR, NT), F32), "refocus")(
        *last, direct, onset_receiver.T, t_samp
    )
    return (upgoing, refocused)


def solution(mesh):
    in_specs = (
        P(None, None, "src", "rcv"),
        P("src", "rcv", None),
        P("src", "rcv", None),
        P(None, "src"),
        P("src", "rcv"),
    )
    out_specs = (P("rcv", "src", None), P("src", "rcv", None))
    return jax.shard_map(
        on_device, mesh=mesh, in_specs=in_specs, out_specs=out_specs, check_vma=False
    )
```

profile of v0, /device:TPU:8, one launch (start us, length us, event | category | flops | bytes accessed | tf_op | source)
XLA Modules:
  0.0 134.9 jit_solution(9679014086564527312)
XLA Ops:
  2.7 4.7 %collective-permute-start.2 = (bf16[96,256]{1,0:T(8,128)(2,1)S(1)}, bf16[96,256]{1,0:T(8,128)(2,1)S(1)}, u32[]{:S(2)}, u32[]{:S(2)}) collective-permute-start(bf16[96,256]{1,0:T(8,128)(2,1)S(1)} %spectra.1), channel_id=1, source_target_pairs={{0,48},{16,32},{32,16},{48,0},{64,112},{80,96},{96,80},{112,64},{1... | collective-permute-start | bytes 147464 | tf_op jit(solution)/shard_map/ppermute | solution.py:277
  8.1 1.8 %collective-permute-done.2 = bf16[96,256]{1,0:T(8,128)(2,1)S(1)} collective-permute-done((bf16[96,256]{1,0:T(8,128)(2,1)S(1)}, bf16[96,256]{1,0:T(8,128)(2,1)S(1)}, u32[]{:S(2)}, u32[]{:S(2)}) %collective-permute-start.2) | collective-permute-done | bytes 49184 | tf_op jit(solution)/shard_map/ppermute | solution.py:277
  9.8 2.5 %collective-permute-done.1 = bf16[96,256]{1,0:T(8,128)(2,1)S(1)} collective-permute-done((bf16[96,256]{1,0:T(8,128)(2,1)S(1)}, bf16[96,256]{1,0:T(8,128)(2,1)S(1)}, u32[]{:S(2)}, u32[]{:S(2)}) %collective-permute-start.1) | collective-permute-done | bytes 49184 | tf_op jit(solution)/shard_map/ppermute | solution.py:277
  14.0 2.7 %collective-permute-start.4 = (bf16[4,48,256]{2,1,0:T(8,128)(2,1)S(1)}, bf16[4,48,256]{2,1,0:T(8,128)(2,1)S(1)}, u32[]{:S(2)}, u32[]{:S(2)}) collective-permute-start(bf16[4,48,256]{2,1,0:T(8,128)(2,1)S(1)} %get-tuple-element.51.f0), channel_id=1, source_target_pairs={{0,128},{16,144},{32,160},{48,176},{64,192},{80,208},{96,224},{112... | collective-permute-start | bytes 294920 | tf_op jit(solution)/shard_map/ppermute | solution.py:277
  18.2 3.5 %load.1.r_ref = bf16[2,8,1024,256]{3,2,1,0:T(8,128)(2,1)S(1)} custom-call(bf16[2,8,1024,256]{3,2,1,0:T(8,128)(2,1)} %r_hbm), custom_call_target="tpu_custom_call" | custom-call | flops 3000000000 | bytes 65536 | tf_op jit(solution)/shard_map/load/pallas_call | solution.py:323
  21.7 4.2 %conv.2 = (bf16[8,2,24,1024]{3,2,1,0:T(8,128)(2,1)S(1)}, bf16[8,2,24,1024]{3,2,1,0:T(8,128)(2,1)S(1)}) custom-call(bf16[4,48,256]{2,1,0:T(8,128)(2,1)S(1)} %get-tuple-element.51.f0, bf16[4,48,256]{2,1,0:T(8,128)(2,1)S(1)} %collective-permute-done.3.f1, bf16[4,48,256]{2,1,0:T(8,128)(2,1)S(1)} %collective-permute-done.4.f2, ...), custom_call_target="tpu_custom_call" | custom-call | flops 4000000000 | bytes 65536 | tf_op jit(solution)/shard_map/conv/pallas_call | solution.py:164
  26.0 2.3 %collective-permute-done.6 = bf16[4,2,48,1024]{3,2,1,0:T(8,128)(2,1)S(1)} collective-permute-done((bf16[4,2,48,1024]{3,2,1,0:T(8,128)(2,1)S(1)}, bf16[4,2,48,1024]{3,2,1,0:T(8,128)(2,1)S(1)}, u32[]{:S(2)}, u32[]{:S(2)}) %collective-permute-start.6) | collective-permute-done | bytes 786464 | tf_op jit(solution)/shard_map/ppermute | solution.py:277
  30.8 3.1 %collective-permute-start.8 = (bf16[4,48,256]{2,1,0:T(8,128)(2,1)S(1)}, bf16[4,48,256]{2,1,0:T(8,128)(2,1)S(1)}, u32[]{:S(2)}, u32[]{:S(2)}) collective-permute-start(bf16[4,48,256]{2,1,0:T(8,128)(2,1)S(1)} %get-tuple-element.56.f0), channel_id=1, source_target_pairs={{0,128},{16,144},{32,160},{48,176},{64,192},{80,208},{96,224},{112... | collective-permute-start | bytes 294920 | tf_op jit(solution)/shard_map/ppermute | solution.py:277
  34.4 2.3 %collective-permute-done.7.f1 = bf16[4,48,256]{2,1,0:T(8,128)(2,1)S(1)} collective-permute-done((bf16[4,48,256]{2,1,0:T(8,128)(2,1)S(1)}, bf16[4,48,256]{2,1,0:T(8,128)(2,1)S(1)}, u32[]{:S(2)}, u32[]{:S(2)}) %collective-permute-start.7) | collective-permute-done | bytes 98336 | tf_op jit(solution)/shard_map/ppermute | solution.py:277
  36.7 1.8 %collective-permute-done.8.f2 = bf16[4,48,256]{2,1,0:T(8,128)(2,1)S(1)} collective-permute-done((bf16[4,48,256]{2,1,0:T(8,128)(2,1)S(1)}, bf16[4,48,256]{2,1,0:T(8,128)(2,1)S(1)}, u32[]{:S(2)}, u32[]{:S(2)}) %collective-permute-start.8) | collective-permute-done | bytes 98336 | tf_op jit(solution)/shard_map/ppermute | solution.py:277
  39.0 4.2 %conv.3 = (bf16[8,2,24,1024]{3,2,1,0:T(8,128)(2,1)S(1)}, bf16[8,2,24,1024]{3,2,1,0:T(8,128)(2,1)S(1)}) custom-call(bf16[4,48,256]{2,1,0:T(8,128)(2,1)S(1)} %get-tuple-element.56.f0, bf16[4,48,256]{2,1,0:T(8,128)(2,1)S(1)} %collective-permute-done.7.f1, bf16[4,48,256]{2,1,0:T(8,128)(2,1)S(1)} %collective-permute-done.8.f2, ...), custom_call_target="tpu_custom_call" | custom-call | flops 4000000000 | bytes 65536 | tf_op jit(solution)/shard_map/conv/pallas_call | solution.py:164
  45.3 2.4 %collective-permute-start.12 = (bf16[2,48,1024]{2,1,0:T(8,128)(2,1)S(1)}, bf16[2,48,1024]{2,1,0:T(8,128)(2,1)S(1)}, u32[]{:S(2)}, u32[]{:S(2)}) collective-permute-start(bf16[2,48,1024]{2,1,0:T(8,128)(2,1)S(1)} %get-tuple-element.102), channel_id=1, source_target_pairs={{0,6},{1,7},{2,0},{3,1},{4,2},{5,3},{6,4},{7,5},{8,14},{9,15},{10,... | collective-permute-start | bytes 589832 | tf_op jit(solution)/shard_map/ppermute | solution.py:277
  49.3 4.3 %collective-permute-done.11.p2 = bf16[2,48,1024]{2,1,0:T(8,128)(2,1)S(1)} collective-permute-done((bf16[2,48,1024]{2,1,0:T(8,128)(2,1)S(1)}, bf16[2,48,1024]{2,1,0:T(8,128)(2,1)S(1)}, u32[]{:S(2)}, u32[]{:S(2)}) %collective-permute-start.11) | collective-permute-done | bytes 196640 | tf_op jit(solution)/shard_map/ppermute | solution.py:277
  53.6 2.9 %collective-permute-done.12.p3 = bf16[2,48,1024]{2,1,0:T(8,128)(2,1)S(1)} collective-permute-done((bf16[2,48,1024]{2,1,0:T(8,128)(2,1)S(1)}, bf16[2,48,1024]{2,1,0:T(8,128)(2,1)S(1)}, u32[]{:S(2)}, u32[]{:S(2)}) %collective-permute-start.12) | collective-permute-done | bytes 196640 | tf_op jit(solution)/shard_map/ppermute | solution.py:277
  58.9 2.0 %collective-permute-start.17 = (bf16[2,48,1024]{2,1,0:T(8,128)(2,1)S(1)}, bf16[2,48,1024]{2,1,0:T(8,128)(2,1)S(1)}, u32[]{:S(2)}, u32[]{:S(2)}) collective-permute-start(bf16[2,48,1024]{2,1,0:T(8,128)(2,1)S(1)} %get-tuple-element.69), channel_id=1, source_target_pairs={{0,6},{1,7},{2,0},{3,1},{4,2},{5,3},{6,4},{7,5},{8,14},{9,15},{10,... | collective-permute-start | bytes 589832 | tf_op jit(solution)/shard_map/ppermute | solution.py:277
  62.0 5.4 %collective-permute-start.14 = (bf16[2,48,1024]{2,1,0:T(8,128)(2,1)S(1)}, bf16[2,48,1024]{2,1,0:T(8,128)(2,1)S(1)}, u32[]{:S(2)}, u32[]{:S(2)}) collective-permute-start(bf16[2,48,1024]{2,1,0:T(8,128)(2,1)S(1)} %get-tuple-element.100), channel_id=1, source_target_pairs={{0,8},{1,9},{2,10},{3,11},{4,12},{5,13},{6,14},{7,15},{8,0},{9,1},... | collective-permute-start | bytes 589832 | tf_op jit(solution)/shard_map/ppermute | solution.py:277
  67.4 1.7 %collective-permute-done.17.p3 = bf16[2,48,1024]{2,1,0:T(8,128)(2,1)S(1)} collective-permute-done((bf16[2,48,1024]{2,1,0:T(8,128)(2,1)S(1)}, bf16[2,48,1024]{2,1,0:T(8,128)(2,1)S(1)}, u32[]{:S(2)}, u32[]{:S(2)}) %collective-permute-start.17) | collective-permute-done | bytes 196640 | tf_op jit(solution)/shard_map/ppermute | solution.py:277
  69.2 5.4 %collective-permute-start.18 = (bf16[2,48,1024]{2,1,0:T(8,128)(2,1)S(1)}, bf16[2,48,1024]{2,1,0:T(8,128)(2,1)S(1)}, u32[]{:S(2)}, u32[]{:S(2)}) collective-permute-start(bf16[2,48,1024]{2,1,0:T(8,128)(2,1)S(1)} %add_convert_fusion), channel_id=1, source_target_pairs={{0,8},{1,9},{2,10},{3,11},{4,12},{5,13},{6,14},{7,15},{8,0},{9,1},... | collective-permute-start | bytes 589832 | tf_op jit(solution)/shard_map/ppermute | solution.py:277
  80.7 4.0 %collective-permute-done.18.r_ref = bf16[2,48,1024]{2,1,0:T(8,128)(2,1)S(1)} collective-permute-done((bf16[2,48,1024]{2,1,0:T(8,128)(2,1)S(1)}, bf16[2,48,1024]{2,1,0:T(8,128)(2,1)S(1)}, u32[]{:S(2)}, u32[]{:S(2)}) %collective-permute-start.18) | collective-permute-done | bytes 196640 | tf_op jit(solution)/shard_map/ppermute | solution.py:277
  89.0 2.2 %collective-permute-start.19 = (bf16[2,48,1024]{2,1,0:T(8,128)(2,1)S(1)}, bf16[2,48,1024]{2,1,0:T(8,128)(2,1)S(1)}, u32[]{:S(2)}, u32[]{:S(2)}) collective-permute-start(bf16[2,48,1024]{2,1,0:T(8,128)(2,1)S(1)} %get-tuple-element.79.w0), channel_id=1, source_target_pairs={{0,2},{1,3},{2,4},{3,5},{4,6},{5,7},{6,0},{7,1},{8,10},{9,11},{10,... | collective-permute-start | bytes 589832 | tf_op jit(solution)/shard_map/ppermute | solution.py:277
  91.2 1.7 %collective-permute-start.20 = (bf16[2,48,1024]{2,1,0:T(8,128)(2,1)S(1)}, bf16[2,48,1024]{2,1,0:T(8,128)(2,1)S(1)}, u32[]{:S(2)}, u32[]{:S(2)}) collective-permute-start(bf16[2,48,1024]{2,1,0:T(8,128)(2,1)S(1)} %get-tuple-element.79.w0), channel_id=1, source_target_pairs={{0,4},{1,5},{2,6},{3,7},{4,0},{5,1},{6,2},{7,3},{8,12},{9,13},{10,... | collective-permute-start | bytes 589832 | tf_op jit(solution)/shard_map/ppermute | solution.py:277
  92.9 2.2 %collective-permute-start.21 = (bf16[2,48,1024]{2,1,0:T(8,128)(2,1)S(1)}, bf16[2,48,1024]{2,1,0:T(8,128)(2,1)S(1)}, u32[]{:S(2)}, u32[]{:S(2)}) collective-permute-start(bf16[2,48,1024]{2,1,0:T(8,128)(2,1)S(1)} %get-tuple-element.79.w0), channel_id=1, source_target_pairs={{0,6},{1,7},{2,0},{3,1},{4,2},{5,3},{6,4},{7,5},{8,14},{9,15},{10,... | collective-permute-start | bytes 589832 | tf_op jit(solution)/shard_map/ppermute | solution.py:277
  95.2 3.9 %corr.2 = (bf16[4,48,256]{2,1,0:T(8,128)(2,1)S(1)}, bf16[4,48,256]{2,1,0:T(8,128)(2,1)S(1)}, bf16[4,48,256]{2,1,0:T(8,128)(2,1)S(1)}, bf16[4,48,256]{2,1,0:T(8,128)(2,1)S(1)}) custom-call(bf16[2,48,1024]{2,1,0:T(8,128)(2,1)S(1)} %get-tuple-element.80.w0, bf16[2,48,1024]{2,1,0:T(8,128)(2,1)S(1)} %collective-permute-done.22.w1, ...), custom_call_target="tpu_custom_call" | custom-call | flops 4000000000 | bytes 65536 | tf_op jit(solution)/shard_map/corr/pallas_call | solution.py:243
  99.3 3.7 %collective-permute-start.30 = (bf16[4,48,256]{2,1,0:T(8,128)(2,1)S(1)}, bf16[4,48,256]{2,1,0:T(8,128)(2,1)S(1)}, u32[]{:S(2)}, u32[]{:S(2)}) collective-permute-start(bf16[4,48,256]{2,1,0:T(8,128)(2,1)S(1)} %get-tuple-element.83), channel_id=1, source_target_pairs={{0,128},{16,144},{32,160},{48,176},{64,192},{80,208},{96,224},{112... | collective-permute-start | bytes 294920 | tf_op jit(solution)/shard_map/ppermute | solution.py:277
  103.6 2.4 %collective-permute-done.29.refs_1_ = bf16[4,48,256]{2,1,0:T(8,128)(2,1)S(1)} collective-permute-done((bf16[4,48,256]{2,1,0:T(8,128)(2,1)S(1)}, bf16[4,48,256]{2,1,0:T(8,128)(2,1)S(1)}, u32[]{:S(2)}, u32[]{:S(2)}) %collective-permute-start.29) | collective-permute-done | bytes 98336 | tf_op jit(solution)/shard_map/ppermute | solution.py:277
  109.6 3.9 %corr.3 = (bf16[4,48,256]{2,1,0:T(8,128)(2,1)S(1)}, bf16[4,48,256]{2,1,0:T(8,128)(2,1)S(1)}, bf16[4,48,256]{2,1,0:T(8,128)(2,1)S(1)}, bf16[4,48,256]{2,1,0:T(8,128)(2,1)S(1)}) custom-call(bf16[2,48,1024]{2,1,0:T(8,128)(2,1)S(1)} %get-tuple-element.79.w0, bf16[2,48,1024]{2,1,0:T(8,128)(2,1)S(1)} %collective-permute-done.19.w1, ...), custom_call_target="tpu_custom_call" | custom-call | flops 4000000000 | bytes 65536 | tf_op jit(solution)/shard_map/corr/pallas_call | solution.py:243
  113.8 3.3 %collective-permute-start.37 = (bf16[4,48,256]{2,1,0:T(8,128)(2,1)S(1)}, bf16[4,48,256]{2,1,0:T(8,128)(2,1)S(1)}, u32[]{:S(2)}, u32[]{:S(2)}) collective-permute-start(bf16[4,48,256]{2,1,0:T(8,128)(2,1)S(1)} %get-tuple-element.94), channel_id=1, source_target_pairs={{0,128},{16,144},{32,160},{48,176},{64,192},{80,208},{96,224},{112... | collective-permute-start | bytes 294920 | tf_op jit(solution)/shard_map/ppermute | solution.py:277
  117.7 2.4 %collective-permute-done.36.refs_5_ = bf16[4,48,256]{2,1,0:T(8,128)(2,1)S(1)} collective-permute-done((bf16[4,48,256]{2,1,0:T(8,128)(2,1)S(1)}, bf16[4,48,256]{2,1,0:T(8,128)(2,1)S(1)}, u32[]{:S(2)}, u32[]{:S(2)}) %collective-permute-start.36) | collective-permute-done | bytes 98336 | tf_op jit(solution)/shard_map/ppermute | solution.py:277
  120.2 2.0 %collective-permute-done.37.refs_6_ = bf16[4,48,256]{2,1,0:T(8,128)(2,1)S(1)} collective-permute-done((bf16[4,48,256]{2,1,0:T(8,128)(2,1)S(1)}, bf16[4,48,256]{2,1,0:T(8,128)(2,1)S(1)}, u32[]{:S(2)}, u32[]{:S(2)}) %collective-permute-start.37) | collective-permute-done | bytes 98336 | tf_op jit(solution)/shard_map/ppermute | solution.py:277
  122.5 2.6 %collective-permute-start.39 = (bf16[2,48,256]{2,1,0:T(8,128)(2,1)S(1)}, bf16[2,48,256]{2,1,0:T(8,128)(2,1)S(1)}, u32[]{:S(2)}, u32[]{:S(2)}) collective-permute-start(bf16[2,48,256]{2,1,0:T(8,128)(2,1)S(1)} %get-tuple-element.97), channel_id=1, source_target_pairs={{0,16},{16,0},{32,48},{48,32},{64,80},{80,64},{96,112},{112,96},{1... | collective-permute-start | bytes 147464 | tf_op jit(solution)/shard_map/ppermute | solution.py:277
  125.1 2.4 %collective-permute-start.40 = (bf16[2,48,256]{2,1,0:T(8,128)(2,1)S(1)}, bf16[2,48,256]{2,1,0:T(8,128)(2,1)S(1)}, u32[]{:S(2)}, u32[]{:S(2)}) collective-permute-start(bf16[2,48,256]{2,1,0:T(8,128)(2,1)S(1)} %get-tuple-element.98), channel_id=1, source_target_pairs={{0,32},{16,48},{32,0},{48,16},{64,96},{80,112},{96,64},{112,80},{1... | collective-permute-start | bytes 147464 | tf_op jit(solution)/shard_map/ppermute | solution.py:277
  130.5 2.9 %collective-permute-done.41.g3 = bf16[2,48,256]{2,1,0:T(8,128)(2,1)S(1)} collective-permute-done((bf16[2,48,256]{2,1,0:T(8,128)(2,1)S(1)}, bf16[2,48,256]{2,1,0:T(8,128)(2,1)S(1)}, u32[]{:S(2)}, u32[]{:S(2)}) %collective-permute-start.41) | collective-permute-done | bytes 49184 | tf_op jit(solution)/shard_map/ppermute | solution.py:277
  (98 shorter events, 37.2 us)
Async XLA Ops:
  2.7 7.2 %collective-permute-start.2 = (bf16[96,256]{1,0:T(8,128)(2,1)S(1)}, bf16[96,256]{1,0:T(8,128)(2,1)S(1)}, u32[]{:S(2)}, u32[]{:S(2)}) collective-permute-start(bf16[96,256]{1,0:T(8,128)(2,1)S(1)} %spectra.1), channel_id=1, source_target_pairs={{0,48},{16,32},{32,16},{48,0},{64,112},{80,96},{96,80},{112,64},{1... | collective-permute-start | bytes 147464 | tf_op jit(solution)/shard_map/ppermute | solution.py:277
  7.4 5.0 %collective-permute-start = (bf16[96,256]{1,0:T(8,128)(2,1)S(1)}, bf16[96,256]{1,0:T(8,128)(2,1)S(1)}, u32[]{:S(2)}, u32[]{:S(2)}) collective-permute-start(bf16[96,256]{1,0:T(8,128)(2,1)S(1)} %spectra.1), channel_id=1, source_target_pairs={{0,16},{16,0},{32,48},{48,32},{64,80},{80,64},{96,112},{112,96},{1... | collective-permute-start | bytes 147464 | tf_op jit(solution)/shard_map/ppermute | solution.py:277
  12.4 9.3 %collective-permute-start.3 = (bf16[4,48,256]{2,1,0:T(8,128)(2,1)S(1)}, bf16[4,48,256]{2,1,0:T(8,128)(2,1)S(1)}, u32[]{:S(2)}, u32[]{:S(2)}) collective-permute-start(bf16[4,48,256]{2,1,0:T(8,128)(2,1)S(1)} %get-tuple-element.51.f0), channel_id=1, source_target_pairs={{0,64},{16,80},{32,96},{48,112},{64,128},{80,144},{96,160},{112,17... | collective-permute-start | bytes 294920 | tf_op jit(solution)/shard_map/ppermute | solution.py:277
  14.0 7.7 %collective-permute-start.4 = (bf16[4,48,256]{2,1,0:T(8,128)(2,1)S(1)}, bf16[4,48,256]{2,1,0:T(8,128)(2,1)S(1)}, u32[]{:S(2)}, u32[]{:S(2)}) collective-permute-start(bf16[4,48,256]{2,1,0:T(8,128)(2,1)S(1)} %get-tuple-element.51.f0), channel_id=1, source_target_pairs={{0,128},{16,144},{32,160},{48,176},{64,192},{80,208},{96,224},{112... | collective-permute-start | bytes 294920 | tf_op jit(solution)/shard_map/ppermute | solution.py:277
  28.5 10.4 %collective-permute-start.10 = (bf16[2,48,1024]{2,1,0:T(8,128)(2,1)S(1)}, bf16[2,48,1024]{2,1,0:T(8,128)(2,1)S(1)}, u32[]{:S(2)}, u32[]{:S(2)}) collective-permute-start(bf16[2,48,1024]{2,1,0:T(8,128)(2,1)S(1)} %get-tuple-element.104), channel_id=1, source_target_pairs={{0,2},{1,3},{2,4},{3,5},{4,6},{5,7},{6,0},{7,1},{8,10},{9,11},{10,... | collective-permute-start | bytes 589832 | tf_op jit(solution)/shard_map/ppermute | solution.py:277
  30.2 6.5 %collective-permute-start.7 = (bf16[4,48,256]{2,1,0:T(8,128)(2,1)S(1)}, bf16[4,48,256]{2,1,0:T(8,128)(2,1)S(1)}, u32[]{:S(2)}, u32[]{:S(2)}) collective-permute-start(bf16[4,48,256]{2,1,0:T(8,128)(2,1)S(1)} %get-tuple-element.56.f0), channel_id=1, source_target_pairs={{0,64},{16,80},{32,96},{48,112},{64,128},{80,144},{96,160},{112,17... | collective-permute-start | bytes 294920 | tf_op jit(solution)/shard_map/ppermute | solution.py:277
  30.8 7.8 %collective-permute-start.8 = (bf16[4,48,256]{2,1,0:T(8,128)(2,1)S(1)}, bf16[4,48,256]{2,1,0:T(8,128)(2,1)S(1)}, u32[]{:S(2)}, u32[]{:S(2)}) collective-permute-start(bf16[4,48,256]{2,1,0:T(8,128)(2,1)S(1)} %get-tuple-element.56.f0), channel_id=1, source_target_pairs={{0,128},{16,144},{32,160},{48,176},{64,192},{80,208},{96,224},{112... | collective-permute-start | bytes 294920 | tf_op jit(solution)/shard_map/ppermute | solution.py:277
  33.9 5.0 %collective-permute-start.9 = (bf16[4,48,256]{2,1,0:T(8,128)(2,1)S(1)}, bf16[4,48,256]{2,1,0:T(8,128)(2,1)S(1)}, u32[]{:S(2)}, u32[]{:S(2)}) collective-permute-start(bf16[4,48,256]{2,1,0:T(8,128)(2,1)S(1)} %get-tuple-element.56.f0), channel_id=1, source_target_pairs={{0,192},{16,208},{32,224},{48,240},{64,0},{80,16},{96,32},{112,48}... | collective-permute-start | bytes 294920 | tf_op jit(solution)/shard_map/ppermute | solution.py:277
  44.3 9.3 %collective-permute-start.11 = (bf16[2,48,1024]{2,1,0:T(8,128)(2,1)S(1)}, bf16[2,48,1024]{2,1,0:T(8,128)(2,1)S(1)}, u32[]{:S(2)}, u32[]{:S(2)}) collective-permute-start(bf16[2,48,1024]{2,1,0:T(8,128)(2,1)S(1)} %get-tuple-element.103), channel_id=1, source_target_pairs={{0,4},{1,5},{2,6},{3,7},{4,0},{5,1},{6,2},{7,3},{8,12},{9,13},{10,... | collective-permute-start | bytes 589832 | tf_op jit(solution)/shard_map/ppermute | solution.py:277
  45.3 11.2 %collective-permute-start.12 = (bf16[2,48,1024]{2,1,0:T(8,128)(2,1)S(1)}, bf16[2,48,1024]{2,1,0:T(8,128)(2,1)S(1)}, u32[]{:S(2)}, u32[]{:S(2)}) collective-permute-start(bf16[2,48,1024]{2,1,0:T(8,128)(2,1)S(1)} %get-tuple-element.102), channel_id=1, source_target_pairs={{0,6},{1,7},{2,0},{3,1},{4,2},{5,3},{6,4},{7,5},{8,14},{9,15},{10,... | collective-permute-start | bytes 589832 | tf_op jit(solution)/shard_map/ppermute | solution.py:277
  56.5 10.9 %collective-permute-start.15 = (bf16[2,48,1024]{2,1,0:T(8,128)(2,1)S(1)}, bf16[2,48,1024]{2,1,0:T(8,128)(2,1)S(1)}, u32[]{:S(2)}, u32[]{:S(2)}) collective-permute-start(bf16[2,48,1024]{2,1,0:T(8,128)(2,1)S(1)} %get-tuple-element.67), channel_id=1, source_target_pairs={{0,2},{1,3},{2,4},{3,5},{4,6},{5,7},{6,0},{7,1},{8,10},{9,11},{10,... | collective-permute-start | bytes 589832 | tf_op jit(solution)/shard_map/ppermute | solution.py:277
  58.0 9.4 %collective-permute-start.16 = (bf16[2,48,1024]{2,1,0:T(8,128)(2,1)S(1)}, bf16[2,48,1024]{2,1,0:T(8,128)(2,1)S(1)}, u32[]{:S(2)}, u32[]{:S(2)}) collective-permute-start(bf16[2,48,1024]{2,1,0:T(8,128)(2,1)S(1)} %get-tuple-element.68), channel_id=1, source_target_pairs={{0,4},{1,5},{2,6},{3,7},{4,0},{5,1},{6,2},{7,3},{8,12},{9,13},{10,... | collective-permute-start | bytes 589832 | tf_op jit(solution)/shard_map/ppermute | solution.py:277
  58.9 10.2 %collective-permute-start.17 = (bf16[2,48,1024]{2,1,0:T(8,128)(2,1)S(1)}, bf16[2,48,1024]{2,1,0:T(8,128)(2,1)S(1)}, u32[]{:S(2)}, u32[]{:S(2)}) collective-permute-start(bf16[2,48,1024]{2,1,0:T(8,128)(2,1)S(1)} %get-tuple-element.69), channel_id=1, source_target_pairs={{0,6},{1,7},{2,0},{3,1},{4,2},{5,3},{6,4},{7,5},{8,14},{9,15},{10,... | collective-permute-start | bytes 589832 | tf_op jit(solution)/shard_map/ppermute | solution.py:277
  62.0 12.6 %collective-permute-start.14 = (bf16[2,48,1024]{2,1,0:T(8,128)(2,1)S(1)}, bf16[2,48,1024]{2,1,0:T(8,128)(2,1)S(1)}, u32[]{:S(2)}, u32[]{:S(2)}) collective-permute-start(bf16[2,48,1024]{2,1,0:T(8,128)(2,1)S(1)} %get-tuple-element.100), channel_id=1, source_target_pairs={{0,8},{1,9},{2,10},{3,11},{4,12},{5,13},{6,14},{7,15},{8,0},{9,1},... | collective-permute-start | bytes 589832 | tf_op jit(solution)/shard_map/ppermute | solution.py:277
  69.2 15.6 %collective-permute-start.18 = (bf16[2,48,1024]{2,1,0:T(8,128)(2,1)S(1)}, bf16[2,48,1024]{2,1,0:T(8,128)(2,1)S(1)}, u32[]{:S(2)}, u32[]{:S(2)}) collective-permute-start(bf16[2,48,1024]{2,1,0:T(8,128)(2,1)S(1)} %add_convert_fusion), channel_id=1, source_target_pairs={{0,8},{1,9},{2,10},{3,11},{4,12},{5,13},{6,14},{7,15},{8,0},{9,1},... | collective-permute-start | bytes 589832 | tf_op jit(solution)/shard_map/ppermute | solution.py:277
  76.3 11.7 %collective-permute-start.22 = (bf16[2,48,1024]{2,1,0:T(8,128)(2,1)S(1)}, bf16[2,48,1024]{2,1,0:T(8,128)(2,1)S(1)}, u32[]{:S(2)}, u32[]{:S(2)}) collective-permute-start(bf16[2,48,1024]{2,1,0:T(8,128)(2,1)S(1)} %get-tuple-element.80.w0), channel_id=1, source_target_pairs={{0,2},{1,3},{2,4},{3,5},{4,6},{5,7},{6,0},{7,1},{8,10},{9,11},{10,... | collective-permute-start | bytes 589832 | tf_op jit(solution)/shard_map/ppermute | solution.py:277
  77.8 10.8 %collective-permute-start.23 = (bf16[2,48,1024]{2,1,0:T(8,128)(2,1)S(1)}, bf16[2,48,1024]{2,1,0:T(8,128)(2,1)S(1)}, u32[]{:S(2)}, u32[]{:S(2)}) collective-permute-start(bf16[2,48,1024]{2,1,0:T(8,128)(2,1)S(1)} %get-tuple-element.80.w0), channel_id=1, source_target_pairs={{0,4},{1,5},{2,6},{3,7},{4,0},{5,1},{6,2},{7,3},{8,12},{9,13},{10,... | collective-permute-start | bytes 589832 | tf_op jit(solution)/shard_map/ppermute | solution.py:277
  79.3 9.3 %collective-permute-start.24 = (bf16[2,48,1024]{2,1,0:T(8,128)(2,1)S(1)}, bf16[2,48,1024]{2,1,0:T(8,128)(2,1)S(1)}, u32[]{:S(2)}, u32[]{:S(2)}) collective-permute-start(bf16[2,48,1024]{2,1,0:T(8,128)(2,1)S(1)} %get-tuple-element.80.w0), channel_id=1, source_target_pairs={{0,6},{1,7},{2,0},{3,1},{4,2},{5,3},{6,4},{7,5},{8,14},{9,15},{10,... | collective-permute-start | bytes 589832 | tf_op jit(solution)/shard_map/ppermute | solution.py:277
  88.5 6.6 %collective-permute-start.27 = (bf16[2,48,1024]{2,1,0:T(8,128)(2,1)S(1)}, bf16[2,48,1024]{2,1,0:T(8,128)(2,1)S(1)}, u32[]{:S(2)}, u32[]{:S(2)}) collective-permute-start(bf16[2,48,1024]{2,1,0:T(8,128)(2,1)S(1)} %collective-permute-done.23.w2), channel_id=1, source_target_pairs={{0,1},{1,0},{2,3},{3,2},{4,5},{5,4},{6,7},{7,6},{8,9},{9,8},{10,11... | collective-permute-start | bytes 589832 | tf_op jit(solution)/shard_map/ppermute | solution.py:277
  88.6 6.5 %collective-permute-start.28 = (bf16[2,48,1024]{2,1,0:T(8,128)(2,1)S(1)}, bf16[2,48,1024]{2,1,0:T(8,128)(2,1)S(1)}, u32[]{:S(2)}, u32[]{:S(2)}) collective-permute-start(bf16[2,48,1024]{2,1,0:T(8,128)(2,1)S(1)} %collective-permute-done.24.w3), channel_id=1, source_target_pairs={{0,1},{1,0},{2,3},{3,2},{4,5},{5,4},{6,7},{7,6},{8,9},{9,8},{10,11... | collective-permute-start | bytes 589832 | tf_op jit(solution)/shard_map/ppermute | solution.py:277
  89.0 14.0 %collective-permute-start.19 = (bf16[2,48,1024]{2,1,0:T(8,128)(2,1)S(1)}, bf16[2,48,1024]{2,1,0:T(8,128)(2,1)S(1)}, u32[]{:S(2)}, u32[]{:S(2)}) collective-permute-start(bf16[2,48,1024]{2,1,0:T(8,128)(2,1)S(1)} %get-tuple-element.79.w0), channel_id=1, source_target_pairs={{0,2},{1,3},{2,4},{3,5},{4,6},{5,7},{6,0},{7,1},{8,10},{9,11},{10,... | collective-permute-start | bytes 589832 | tf_op jit(solution)/shard_map/ppermute | solution.py:277
  91.2 11.8 %collective-permute-start.20 = (bf16[2,48,1024]{2,1,0:T(8,128)(2,1)S(1)}, bf16[2,48,1024]{2,1,0:T(8,128)(2,1)S(1)}, u32[]{:S(2)}, u32[]{:S(2)}) collective-permute-start(bf16[2,48,1024]{2,1,0:T(8,128)(2,1)S(1)} %get-tuple-element.79.w0), channel_id=1, source_target_pairs={{0,4},{1,5},{2,6},{3,7},{4,0},{5,1},{6,2},{7,3},{8,12},{9,13},{10,... | collective-permute-start | bytes 589832 | tf_op jit(solution)/shard_map/ppermute | solution.py:277
  92.9 10.7 %collective-permute-start.21 = (bf16[2,48,1024]{2,1,0:T(8,128)(2,1)S(1)}, bf16[2,48,1024]{2,1,0:T(8,128)(2,1)S(1)}, u32[]{:S(2)}, u32[]{:S(2)}) collective-permute-start(bf16[2,48,1024]{2,1,0:T(8,128)(2,1)S(1)} %get-tuple-element.79.w0), channel_id=1, source_target_pairs={{0,6},{1,7},{2,0},{3,1},{4,2},{5,3},{6,4},{7,5},{8,14},{9,15},{10,... | collective-permute-start | bytes 589832 | tf_op jit(solution)/shard_map/ppermute | solution.py:277
  99.1 6.9 %collective-permute-start.29 = (bf16[4,48,256]{2,1,0:T(8,128)(2,1)S(1)}, bf16[4,48,256]{2,1,0:T(8,128)(2,1)S(1)}, u32[]{:S(2)}, u32[]{:S(2)}) collective-permute-start(bf16[4,48,256]{2,1,0:T(8,128)(2,1)S(1)} %get-tuple-element.82), channel_id=1, source_target_pairs={{0,64},{16,80},{32,96},{48,112},{64,128},{80,144},{96,160},{112,17... | collective-permute-start | bytes 294920 | tf_op jit(solution)/shard_map/ppermute | solution.py:277
  99.3 7.7 %collective-permute-start.30 = (bf16[4,48,256]{2,1,0:T(8,128)(2,1)S(1)}, bf16[4,48,256]{2,1,0:T(8,128)(2,1)S(1)}, u32[]{:S(2)}, u32[]{:S(2)}) collective-permute-start(bf16[4,48,256]{2,1,0:T(8,128)(2,1)S(1)} %get-tuple-element.83), channel_id=1, source_target_pairs={{0,128},{16,144},{32,160},{48,176},{64,192},{80,208},{96,224},{112... | collective-permute-start | bytes 294920 | tf_op jit(solution)/shard_map/ppermute | solution.py:277
  103.0 5.1 %collective-permute-start.32 = (bf16[2,48,1024]{2,1,0:T(8,128)(2,1)S(1)}, bf16[2,48,1024]{2,1,0:T(8,128)(2,1)S(1)}, u32[]{:S(2)}, u32[]{:S(2)}) collective-permute-start(bf16[2,48,1024]{2,1,0:T(8,128)(2,1)S(1)} %get-tuple-element.79.w0), channel_id=1, source_target_pairs={{0,1},{1,0},{2,3},{3,2},{4,5},{5,4},{6,7},{7,6},{8,9},{9,8},{10,11... | collective-permute-start | bytes 589832 | tf_op jit(solution)/shard_map/ppermute | solution.py:277
  113.5 6.6 %collective-permute-start.36 = (bf16[4,48,256]{2,1,0:T(8,128)(2,1)S(1)}, bf16[4,48,256]{2,1,0:T(8,128)(2,1)S(1)}, u32[]{:S(2)}, u32[]{:S(2)}) collective-permute-start(bf16[4,48,256]{2,1,0:T(8,128)(2,1)S(1)} %get-tuple-element.93), channel_id=1, source_target_pairs={{0,64},{16,80},{32,96},{48,112},{64,128},{80,144},{96,160},{112,17... | collective-permute-start | bytes 294920 | tf_op jit(solution)/shard_map/ppermute | solution.py:277
  113.8 8.3 %collective-permute-start.37 = (bf16[4,48,256]{2,1,0:T(8,128)(2,1)S(1)}, bf16[4,48,256]{2,1,0:T(8,128)(2,1)S(1)}, u32[]{:S(2)}, u32[]{:S(2)}) collective-permute-start(bf16[4,48,256]{2,1,0:T(8,128)(2,1)S(1)} %get-tuple-element.94), channel_id=1, source_target_pairs={{0,128},{16,144},{32,160},{48,176},{64,192},{80,208},{96,224},{112... | collective-permute-start | bytes 294920 | tf_op jit(solution)/shard_map/ppermute | solution.py:277
  117.1 5.3 %collective-permute-start.38 = (bf16[4,48,256]{2,1,0:T(8,128)(2,1)S(1)}, bf16[4,48,256]{2,1,0:T(8,128)(2,1)S(1)}, u32[]{:S(2)}, u32[]{:S(2)}) collective-permute-start(bf16[4,48,256]{2,1,0:T(8,128)(2,1)S(1)} %get-tuple-element.95), channel_id=1, source_target_pairs={{0,192},{16,208},{32,224},{48,240},{64,0},{80,16},{96,32},{112,48}... | collective-permute-start | bytes 294920 | tf_op jit(solution)/shard_map/ppermute | solution.py:277
  122.5 6.5 %collective-permute-start.39 = (bf16[2,48,256]{2,1,0:T(8,128)(2,1)S(1)}, bf16[2,48,256]{2,1,0:T(8,128)(2,1)S(1)}, u32[]{:S(2)}, u32[]{:S(2)}) collective-permute-start(bf16[2,48,256]{2,1,0:T(8,128)(2,1)S(1)} %get-tuple-element.97), channel_id=1, source_target_pairs={{0,16},{16,0},{32,48},{48,32},{64,80},{80,64},{96,112},{112,96},{1... | collective-permute-start | bytes 147464 | tf_op jit(solution)/shard_map/ppermute | solution.py:277
  125.1 5.4 %collective-permute-start.40 = (bf16[2,48,256]{2,1,0:T(8,128)(2,1)S(1)}, bf16[2,48,256]{2,1,0:T(8,128)(2,1)S(1)}, u32[]{:S(2)}, u32[]{:S(2)}) collective-permute-start(bf16[2,48,256]{2,1,0:T(8,128)(2,1)S(1)} %get-tuple-element.98), channel_id=1, source_target_pairs={{0,32},{16,48},{32,0},{48,16},{64,96},{80,112},{96,64},{112,80},{1... | collective-permute-start | bytes 147464 | tf_op jit(solution)/shard_map/ppermute | solution.py:277
  127.5 6.0 %collective-permute-start.41 = (bf16[2,48,256]{2,1,0:T(8,128)(2,1)S(1)}, bf16[2,48,256]{2,1,0:T(8,128)(2,1)S(1)}, u32[]{:S(2)}, u32[]{:S(2)}) collective-permute-start(bf16[2,48,256]{2,1,0:T(8,128)(2,1)S(1)} %get-tuple-element.99), channel_id=1, source_target_pairs={{0,48},{16,32},{32,16},{48,0},{64,112},{80,96},{96,80},{112,64},{1... | collective-permute-start | bytes 147464 | tf_op jit(solution)/shard_map/ppermute | solution.py:277
  (20 other events, 268.2 us)
where the time goes:
time: 135 us
  starting transfers between devices  62.4 us (46%)
  waiting for transfers between devices  39.2 us (29%)
  Pallas kernels  26.4 us (20%)
  other arithmetic  3 us (2%)
  local copies, waits for them, and re-layouts  2.9 us (2%)
    ppermute x42, starting transfers between devices, send(): return lax.ppermute(value, axis, [(i, to(i)) for i in range(16)])  62.4 us
    ppermute x42, waiting for transfers between devices, send(): return lax.ppermute(value, axis, [(i, to(i)) for i in range(16)])  39.2 us
    pallas_call x2, Pallas kernels, convolve(): call(conv_kernel, [jax.ShapeDtypeStruct((8, 2, ROWS // 2, NS), BF)] * 2,...  8.37 us
    pallas_call x2, Pallas kernels, correlate(): call(corr_kernel, [jax.ShapeDtypeStruct((4, ROWS, NR), BF)] * 4, 'corr',...  7.74 us
    pallas_call x1, Pallas kernels, on_device(): call(load_kernel, pltpu.VMEM((2, NF, NS, NR), BF), 'load', in_specs=[pl.B...  3.51 us
    pallas_call x2, Pallas kernels, window(): call(window_kernel, (jax.ShapeDtypeStruct((2, ROWS, NS), BF), jax.ShapeDt...  3.22 us
  transfers between devices with their start and end apart: 42, of which 22 were waited for; matrix products, arithmetic and copies ran while one was open for 3% of the time, Pallas kernels for 9%

commit v1 on v0

--- a/solution.py
+++ b/solution.py
@@ -80,7 +80,7 @@
         kernel,
         out_shape=out,
         name=name,
-        compiler_params=pltpu.CompilerParams(vmem_limit_bytes=mib << 20),
+        compiler_params=pltpu.CompilerParams(vmem_limit_bytes=int(mib * 2**20)),
         **kw,
     )
 
@@ -108,7 +108,13 @@
     return out
 
 
-def spectra_kernel(f_ref, t_ref, o_ref):
+def spectra_kernel(f_hbm, t_hbm, o_ref, f_ref, t_ref, sem):
+    copies = [pltpu.make_async_copy(f_hbm.at[j], f_ref.at[j], sem.at[j]) for j in range(NP)]
+    copies.append(pltpu.make_async_copy(t_hbm, t_ref, sem.at[NP]))
+    for copy in copies:
+        copy.start()
+    for copy in copies:
+        copy.wait()
     rows = []
     for j in range(NP):
         both = dot(t_ref[...], f_ref[j], 1, 1)
@@ -209,15 +215,16 @@
         copy.wait()
 
 
-def corr_kernel(w0, w1, w2, w3, v0, v1, v2, v3, r_ref, o0, o1, o2, o3, out, acc):
+def corr_kernel(w0, w1, w2, w3, v0, v1, v2, v3, r_ref, *rest):
+    *firsts, o0, o1, o2, o3, out, acc = rest
     x, zl, zh, y, c = place()
     refs = (w0, w1, w2, w3, v0, v1, v2, v3)
     row = lax.broadcasted_iota(jnp.int32, (256, NR), 0)
     even = row % 2 == 0
 
     def step(i, carry):
-        for n in range(2):
-            p = 2 * i + n
+        for n in range(5):
+            p = 5 * i + n
             t = (p >= 3).astype(jnp.int32) + (p >= 7).astype(jnp.int32)
             k = p - t
             at = pl.ds(pl.multiple_of(16 * t, 16), 16)
@@ -228,7 +235,7 @@
             acc[t] = jnp.where(mine, g, acc[t])
         return carry
 
-    lax.fori_loop(0, 5, step, 0)
+    lax.fori_loop(0, 2, step, 0)
     for i in range(16):
         other, d, e = i // 8, i // 2 % 4, i % 2
         yb = lax.rem(y + 4 - d, 4)
@@ -236,26 +243,29 @@
         zb = lax.rem(yb, 2) * 2 + lax.rem(c + other, 2)
         out[lax.rem(xb + 4 - x, 4), zb ^ zl] = jnp.concatenate([acc[t, 16 * i : 16 * i + 16] for t in range(3)], axis=0).astype(BF)
     for d, ref in enumerate((o0, o1, o2, o3)):
-        ref[...] = out[d]
-
-
-def correlate(waves, reflection):
+        if firsts:
+            ref[0] = firsts[d][...]
+            ref[1] = out[d]
+        else:
+            ref[...] = out[d]
+
+
+def correlate(waves, reflection, firsts=()):
+    shape = (4, ROWS, NR) if not firsts else (2, 4, ROWS, NR)
     return call(
         corr_kernel,
-        [jax.ShapeDtypeStruct((4, ROWS, NR), BF)] * 4,
+        [jax.ShapeDtypeStruct(shape, BF)] * 4,
         "corr",
-        in_specs=[pl.BlockSpec(memory_space=pltpu.VMEM)] * 9,
+        in_specs=[pl.BlockSpec(memory_space=pltpu.VMEM)] * (9 + len(firsts)),
         scratch_shapes=[pltpu.VMEM((4, 4, ROWS, NR), BF), pltpu.VMEM((3, 256, NR), F32)],
         cost_estimate=cost(4),
         mib=16,
-    )(*waves, reflection)
-
-
-def sum_kernel(*refs):
-    ins, (keep, *gives) = refs[: 4 * CH], refs[4 * CH :]
+    )(*waves, reflection, *firsts)
+
+
+def sum_kernel(g0, g1, g2, g3, keep, *gives):
     for h in range(CH):
-        g = ins[4 * h : 4 * h + 4]
-        total = (g[0][...].astype(F32) + g[1][...].astype(F32)) + (g[2][...].astype(F32) + g[3][...].astype(F32))
+        total = (g0[h].astype(F32) + g1[h].astype(F32)) + (g2[h].astype(F32) + g3[h].astype(F32))
         keep[h] = total[0]
         for d, give in enumerate(gives):
             give[h] = total[d + 1].astype(BF)
@@ -310,16 +320,21 @@
     t_spec = jnp.asarray(spectra_table())
     t_samp = jnp.asarray(samples_table())
 
-    spectra = call(spectra_kernel, jax.ShapeDtypeStruct((CH * ROWS, NR), BF), "spectra")(
+    spectra = call(spectra_kernel, pltpu.VMEM((CH * ROWS, NR), BF), "spectra", mib=62,
+        out_specs=pl.BlockSpec(memory_space=pltpu.VMEM),
+        in_specs=[pl.BlockSpec(memory_space=pltpu.HBM)] * 2,
+        scratch_shapes=[
+            pltpu.VMEM((NP, NR, NT), BF),
+            pltpu.VMEM((4 * NF, NT), BF),
+            pltpu.SemaphoreType.DMA((NP + 1,)),
+        ],
+    )(
         focusing, jnp.asarray(trace_table())
     )
     rcv = lax.axis_index("rcv")
     near_far = [lax.dynamic_slice_in_dim(onset_source, r * NP, NP, 0) for r in (rcv, rcv ^ 8)]
     onsets = [jnp.stack([o[h * PC : (h + 1) * PC] for o in near_far]) for h in range(CH)]
-    near = [spectra] + [send(spectra, "src", to_zl(d)) for d in (1, 2, 3)]
-    stacks = [jnp.stack([n[h * ROWS : (h + 1) * ROWS] for n in near]) for h in range(CH)]
-    [reflection], stacks[:1] = together([reflection], stacks[:1])
-    pieces = [[stacks[0]] + [send(stacks[0], "src", to_x(d)) for d in (1, 2, 3)]]
+    near = [send(spectra, "src", to_zl(d)) for d in (1, 2, 3)]
     held = call(
         load_kernel,
         pltpu.VMEM((2, NF, NS, NR), BF),
@@ -330,6 +345,10 @@
         cost_estimate=cost(3),
         mib=50,
     )(reflection)
+    near, [spectra, held] = together(near, [spectra, held])
+    near = [spectra, *near]
+    stacks = [jnp.stack([n[h * ROWS : (h + 1) * ROWS] for n in near]) for h in range(CH)]
+    pieces = [[stacks[0]] + [send(stacks[0], "src", to_x(d)) for d in (1, 2, 3)]]
 
     def summed(give, keep):
         got = send(give, "rcv", to_core)
@@ -353,8 +372,8 @@
     [second], [keep_a] = together([stacks[1]], [keep_a])
     pieces.append([second] + [send(second, "src", to_x(d)) for d in (1, 2, 3)])
     sum_a = summed(give_a, keep_a)
+    pieces[1][1:], sum_a = together(pieces[1][1:], sum_a)
     both_a = over_y(sum_a)
-    pieces[1][1:], both_a[1:2] = together(pieces[1][1:], both_a[1:2])
     sum_b = summed(*convolve(pieces[1], held))
     both_a[1:], sum_b = together(both_a[1:], sum_b)
     both_b = over_y(sum_b)
@@ -377,9 +396,9 @@
     def over_x(back):
         return [back[0]] + [send(back[d], "src", to_x(d)) for d in (1, 2, 3)]
 
-    parts_a = over_x(correlate(over_core(own_a), held))
-    own_b[1:], parts_a = together(own_b[1:], parts_a)
-    parts = parts_a + over_x(correlate(over_core(own_b), held))
+    back_a = list(correlate(over_core(own_a), held))
+    own_b[1:], back_a = together(own_b[1:], back_a)
+    parts = over_x(correlate(over_core(own_b), held, back_a))
 
     keep, *gives = call(
         sum_kernel,

time: 135 us -> 129 us (0.956)
  starting transfers between devices: 62.4 us -> 53.4 us
  waiting for transfers between devices: 39.2 us -> 45.5 us
  other arithmetic: 3 us -> 0.94 us
  local copies, waits for them, and re-layouts: 2.9 us -> 1.21 us
    ppermute x42 -> x39, starting transfers between devices: 62.4 us -> 53.4 us  [send(): return lax.ppermute(value, axis, [(i, to(i)) for i in range(16)])]
    ppermute x42 -> x39, waiting for transfers between devices: 39.2 us -> 45.5 us  [send(): return lax.ppermute(value, axis, [(i, to(i)) for i in range(16)])]
    unnamed x21 -> x15, local copies, waits for them, and re-layouts: 1.86 us -> 0.17 us
  transfers between devices with their start and end apart: 42 -> 39, of which waited for: 22 -> 22; matrix products, arithmetic and copies ran while one was open for 3% -> 2% of each run, Pallas kernels for 9% -> 9%
where the time goes in v1:
time: 129 us
  starting transfers between devices  53.4 us (41%)
  waiting for transfers between devices  45.5 us (35%)
  Pallas kernels  26.6 us (21%)
    ppermute x39, starting transfers between devices, send(): return lax.ppermute(value, axis, [(i, to(i)) for i in range(16)])  53.4 us
    ppermute x39, waiting for transfers between devices, send(): return lax.ppermute(value, axis, [(i, to(i)) for i in range(16)])  45.5 us
    pallas_call x2, Pallas kernels, convolve(): call(conv_kernel, [jax.ShapeDtypeStruct((8, 2, ROWS // 2, NS), BF)] * 2,...  8.37 us
    pallas_call x2, Pallas kernels, correlate(): call(corr_kernel, [jax.ShapeDtypeStruct(shape, BF)] * 4, 'corr', in_specs...  6.87 us
    pallas_call x1, Pallas kernels, on_device(): call(load_kernel, pltpu.VMEM((2, NF, NS, NR), BF), 'load', in_specs=[pl.B...  3.51 us
    pallas_call x2, Pallas kernels, window(): call(window_kernel, (jax.ShapeDtypeStruct((2, ROWS, NS), BF), jax.ShapeDt...  3.24 us
  transfers between devices with their start and end apart: 39, of which 22 were waited for; matrix products, arithmetic and copies ran while one was open for 2% of the time, Pallas kernels for 9%

profile of v1, /device:TPU:8, one launch (start us, length us, event | category | flops | bytes accessed | tf_op | source)
XLA Modules:
  0.0 128.7 jit_solution(15771952321917994579)
XLA Ops:
  2.1 2.0 %collective-permute-start = (bf16[96,256]{1,0:T(8,128)(2,1)S(1)}, bf16[96,256]{1,0:T(8,128)(2,1)S(1)}, u32[]{:S(2)}, u32[]{:S(2)}) collective-permute-start(bf16[96,256]{1,0:T(8,128)(2,1)S(1)} %spectra.1), channel_id=1, source_target_pairs={{0,16},{16,0},{32,48},{48,32},{64,80},{80,64},{96,112},{112,96},{1... | collective-permute-start | bytes 147464 | tf_op jit(solution)/shard_map/ppermute | solution.py:287
  4.1 3.3 %collective-permute-start.1 = (bf16[96,256]{1,0:T(8,128)(2,1)S(1)}, bf16[96,256]{1,0:T(8,128)(2,1)S(1)}, u32[]{:S(2)}, u32[]{:S(2)}) collective-permute-start(bf16[96,256]{1,0:T(8,128)(2,1)S(1)} %spectra.1), channel_id=1, source_target_pairs={{0,32},{16,48},{32,0},{48,16},{64,96},{80,112},{96,64},{112,80},{1... | collective-permute-start | bytes 147464 | tf_op jit(solution)/shard_map/ppermute | solution.py:287
  7.3 3.5 %load.1.r_ref = bf16[2,8,1024,256]{3,2,1,0:T(8,128)(2,1)S(1)} custom-call(bf16[2,8,1024,256]{3,2,1,0:T(8,128)(2,1)} %r_hbm.1), custom_call_target="tpu_custom_call" | custom-call | flops 3000000000 | bytes 65536 | tf_op jit(solution)/shard_map/load/pallas_call | solution.py:338
  10.9 2.3 %collective-permute-done.2 = bf16[96,256]{1,0:T(8,128)(2,1)S(1)} collective-permute-done((bf16[96,256]{1,0:T(8,128)(2,1)S(1)}, bf16[96,256]{1,0:T(8,128)(2,1)S(1)}, u32[]{:S(2)}, u32[]{:S(2)}) %collective-permute-start.2) | collective-permute-done | bytes 49184 | tf_op jit(solution)/shard_map/ppermute | solution.py:287
  14.9 2.7 %collective-permute-start.4 = (bf16[4,48,256]{2,1,0:T(8,128)(2,1)S(1)}, bf16[4,48,256]{2,1,0:T(8,128)(2,1)S(1)}, u32[]{:S(2)}, u32[]{:S(2)}) collective-permute-start(bf16[4,48,256]{2,1,0:T(8,128)(2,1)S(1)} %pad_maximum_fusion.1.f0), channel_id=1, source_target_pairs={{0,128},{16,144},{32,160},{48,176},{64,192},{80,208},{96,224},{112... | collective-permute-start | bytes 294920 | tf_op jit(solution)/shard_map/ppermute | solution.py:287
  19.4 1.8 %collective-permute-done.4.f2 = bf16[4,48,256]{2,1,0:T(8,128)(2,1)S(1)} collective-permute-done((bf16[4,48,256]{2,1,0:T(8,128)(2,1)S(1)}, bf16[4,48,256]{2,1,0:T(8,128)(2,1)S(1)}, u32[]{:S(2)}, u32[]{:S(2)}) %collective-permute-start.4) | collective-permute-done | bytes 98336 | tf_op jit(solution)/shard_map/ppermute | solution.py:287
  22.2 4.2 %conv.2 = (bf16[8,2,24,1024]{3,2,1,0:T(8,128)(2,1)S(1)}, bf16[8,2,24,1024]{3,2,1,0:T(8,128)(2,1)S(1)}) custom-call(bf16[4,48,256]{2,1,0:T(8,128)(2,1)S(1)} %pad_maximum_fusion.1.f0, bf16[4,48,256]{2,1,0:T(8,128)(2,1)S(1)} %collective-permute-done.3.f1, bf16[4,48,256]{2,1,0:T(8,128)(2,1)S(1)} %collective-permute-done.4.f2, ...), custom_call_target="tpu_custom_call" | custom-call | flops 4000000000 | bytes 65536 | tf_op jit(solution)/shard_map/conv/pallas_call | solution.py:170
  27.5 3.2 %collective-permute-start.7 = (bf16[4,48,256]{2,1,0:T(8,128)(2,1)S(1)}, bf16[4,48,256]{2,1,0:T(8,128)(2,1)S(1)}, u32[]{:S(2)}, u32[]{:S(2)}) collective-permute-start(bf16[4,48,256]{2,1,0:T(8,128)(2,1)S(1)} %pad_maximum_fusion.f0), channel_id=1, source_target_pairs={{0,128},{16,144},{32,160},{48,176},{64,192},{80,208},{96,224},{112... | collective-permute-start | bytes 294920 | tf_op jit(solution)/shard_map/ppermute | solution.py:287
  33.0 3.0 %collective-permute-done.7.f2 = bf16[4,48,256]{2,1,0:T(8,128)(2,1)S(1)} collective-permute-done((bf16[4,48,256]{2,1,0:T(8,128)(2,1)S(1)}, bf16[4,48,256]{2,1,0:T(8,128)(2,1)S(1)}, u32[]{:S(2)}, u32[]{:S(2)}) %collective-permute-start.7) | collective-permute-done | bytes 98336 | tf_op jit(solution)/shard_map/ppermute | solution.py:287
  36.0 4.2 %conv.3 = (bf16[8,2,24,1024]{3,2,1,0:T(8,128)(2,1)S(1)}, bf16[8,2,24,1024]{3,2,1,0:T(8,128)(2,1)S(1)}) custom-call(bf16[4,48,256]{2,1,0:T(8,128)(2,1)S(1)} %pad_maximum_fusion.f0, bf16[4,48,256]{2,1,0:T(8,128)(2,1)S(1)} %collective-permute-done.6.f1, bf16[4,48,256]{2,1,0:T(8,128)(2,1)S(1)} %collective-permute-done.7.f2, ...), custom_call_target="tpu_custom_call" | custom-call | flops 4000000000 | bytes 65536 | tf_op jit(solution)/shard_map/conv/pallas_call | solution.py:170
  41.3 1.7 %collective-permute-start.10 = (bf16[2,48,1024]{2,1,0:T(8,128)(2,1)S(1)}, bf16[2,48,1024]{2,1,0:T(8,128)(2,1)S(1)}, u32[]{:S(2)}, u32[]{:S(2)}) collective-permute-start(bf16[2,48,1024]{2,1,0:T(8,128)(2,1)S(1)} %get-tuple-element.67), channel_id=1, source_target_pairs={{0,2},{1,3},{2,4},{3,5},{4,6},{5,7},{6,0},{7,1},{8,10},{9,11},{10,... | collective-permute-start | bytes 589832 | tf_op jit(solution)/shard_map/ppermute | solution.py:287
  43.9 2.4 %collective-permute-start.12 = (bf16[2,48,1024]{2,1,0:T(8,128)(2,1)S(1)}, bf16[2,48,1024]{2,1,0:T(8,128)(2,1)S(1)}, u32[]{:S(2)}, u32[]{:S(2)}) collective-permute-start(bf16[2,48,1024]{2,1,0:T(8,128)(2,1)S(1)} %get-tuple-element.69), channel_id=1, source_target_pairs={{0,6},{1,7},{2,0},{3,1},{4,2},{5,3},{6,4},{7,5},{8,14},{9,15},{10,... | collective-permute-start | bytes 589832 | tf_op jit(solution)/shard_map/ppermute | solution.py:287
  46.7 2.3 %collective-permute-done.10.p1 = bf16[2,48,1024]{2,1,0:T(8,128)(2,1)S(1)} collective-permute-done((bf16[2,48,1024]{2,1,0:T(8,128)(2,1)S(1)}, bf16[2,48,1024]{2,1,0:T(8,128)(2,1)S(1)}, u32[]{:S(2)}, u32[]{:S(2)}) %collective-permute-start.10) | collective-permute-done | bytes 196640 | tf_op jit(solution)/shard_map/ppermute | solution.py:287
  49.1 3.2 %collective-permute-done.11.p2 = bf16[2,48,1024]{2,1,0:T(8,128)(2,1)S(1)} collective-permute-done((bf16[2,48,1024]{2,1,0:T(8,128)(2,1)S(1)}, bf16[2,48,1024]{2,1,0:T(8,128)(2,1)S(1)}, u32[]{:S(2)}, u32[]{:S(2)}) %collective-permute-start.11) | collective-permute-done | bytes 196640 | tf_op jit(solution)/shard_map/ppermute | solution.py:287
  52.2 2.7 %collective-permute-done.12.p3 = bf16[2,48,1024]{2,1,0:T(8,128)(2,1)S(1)} collective-permute-done((bf16[2,48,1024]{2,1,0:T(8,128)(2,1)S(1)}, bf16[2,48,1024]{2,1,0:T(8,128)(2,1)S(1)}, u32[]{:S(2)}, u32[]{:S(2)}) %collective-permute-start.12) | collective-permute-done | bytes 196640 | tf_op jit(solution)/shard_map/ppermute | solution.py:287
  59.5 4.6 %collective-permute-start.14 = (bf16[2,48,1024]{2,1,0:T(8,128)(2,1)S(1)}, bf16[2,48,1024]{2,1,0:T(8,128)(2,1)S(1)}, u32[]{:S(2)}, u32[]{:S(2)}) collective-permute-start(bf16[2,48,1024]{2,1,0:T(8,128)(2,1)S(1)} %add_convert_fusion.1), channel_id=1, source_target_pairs={{0,8},{1,9},{2,10},{3,11},{4,12},{5,13},{6,14},{7,15},{8,0},{9,1},... | collective-permute-start | bytes 589832 | tf_op jit(solution)/shard_map/ppermute | solution.py:287
  65.6 2.3 %collective-permute-done.17.p3 = bf16[2,48,1024]{2,1,0:T(8,128)(2,1)S(1)} collective-permute-done((bf16[2,48,1024]{2,1,0:T(8,128)(2,1)S(1)}, bf16[2,48,1024]{2,1,0:T(8,128)(2,1)S(1)}, u32[]{:S(2)}, u32[]{:S(2)}) %collective-permute-start.17) | collective-permute-done | bytes 196640 | tf_op jit(solution)/shard_map/ppermute | solution.py:287
  68.0 4.6 %collective-permute-start.18 = (bf16[2,48,1024]{2,1,0:T(8,128)(2,1)S(1)}, bf16[2,48,1024]{2,1,0:T(8,128)(2,1)S(1)}, u32[]{:S(2)}, u32[]{:S(2)}) collective-permute-start(bf16[2,48,1024]{2,1,0:T(8,128)(2,1)S(1)} %add_convert_fusion), channel_id=1, source_target_pairs={{0,8},{1,9},{2,10},{3,11},{4,12},{5,13},{6,14},{7,15},{8,0},{9,1},... | collective-permute-start | bytes 589832 | tf_op jit(solution)/shard_map/ppermute | solution.py:287
  75.0 2.0 %collective-permute-start.23 = (bf16[2,48,1024]{2,1,0:T(8,128)(2,1)S(1)}, bf16[2,48,1024]{2,1,0:T(8,128)(2,1)S(1)}, u32[]{:S(2)}, u32[]{:S(2)}) collective-permute-start(bf16[2,48,1024]{2,1,0:T(8,128)(2,1)S(1)} %get-tuple-element.92.w0), channel_id=1, source_target_pairs={{0,4},{1,5},{2,6},{3,7},{4,0},{5,1},{6,2},{7,3},{8,12},{9,13},{10,... | collective-permute-start | bytes 589832 | tf_op jit(solution)/shard_map/ppermute | solution.py:287
  77.0 1.8 %collective-permute-start.24 = (bf16[2,48,1024]{2,1,0:T(8,128)(2,1)S(1)}, bf16[2,48,1024]{2,1,0:T(8,128)(2,1)S(1)}, u32[]{:S(2)}, u32[]{:S(2)}) collective-permute-start(bf16[2,48,1024]{2,1,0:T(8,128)(2,1)S(1)} %get-tuple-element.92.w0), channel_id=1, source_target_pairs={{0,6},{1,7},{2,0},{3,1},{4,2},{5,3},{6,4},{7,5},{8,14},{9,15},{10,... | collective-permute-start | bytes 589832 | tf_op jit(solution)/shard_map/ppermute | solution.py:287
  78.8 3.0 %collective-permute-done.18.r_ref = bf16[2,48,1024]{2,1,0:T(8,128)(2,1)S(1)} collective-permute-done((bf16[2,48,1024]{2,1,0:T(8,128)(2,1)S(1)}, bf16[2,48,1024]{2,1,0:T(8,128)(2,1)S(1)}, u32[]{:S(2)}, u32[]{:S(2)}) %collective-permute-start.18) | collective-permute-done | bytes 196640 | tf_op jit(solution)/shard_map/ppermute | solution.py:287
  87.3 2.5 %collective-permute-start.20 = (bf16[2,48,1024]{2,1,0:T(8,128)(2,1)S(1)}, bf16[2,48,1024]{2,1,0:T(8,128)(2,1)S(1)}, u32[]{:S(2)}, u32[]{:S(2)}) collective-permute-start(bf16[2,48,1024]{2,1,0:T(8,128)(2,1)S(1)} %get-tuple-element.91.w0), channel_id=1, source_target_pairs={{0,4},{1,5},{2,6},{3,7},{4,0},{5,1},{6,2},{7,3},{8,12},{9,13},{10,... | collective-permute-start | bytes 589832 | tf_op jit(solution)/shard_map/ppermute | solution.py:287
  90.9 3.4 %corr.2 = (bf16[4,48,256]{2,1,0:T(8,128)(2,1)S(1)}, bf16[4,48,256]{2,1,0:T(8,128)(2,1)S(1)}, bf16[4,48,256]{2,1,0:T(8,128)(2,1)S(1)}, bf16[4,48,256]{2,1,0:T(8,128)(2,1)S(1)}) custom-call(bf16[2,48,1024]{2,1,0:T(8,128)(2,1)S(1)} %get-tuple-element.92.w0, bf16[2,48,1024]{2,1,0:T(8,128)(2,1)S(1)} %collective-permute-done.22.w1, ...), custom_call_target="tpu_custom_call" | custom-call | flops 4000000000 | bytes 65536 | tf_op jit(solution)/shard_map/corr/pallas_call | solution.py:255
  94.4 2.2 %collective-permute-done.20.w2 = bf16[2,48,1024]{2,1,0:T(8,128)(2,1)S(1)} collective-permute-done((bf16[2,48,1024]{2,1,0:T(8,128)(2,1)S(1)}, bf16[2,48,1024]{2,1,0:T(8,128)(2,1)S(1)}, u32[]{:S(2)}, u32[]{:S(2)}) %collective-permute-start.20) | collective-permute-done | bytes 196640 | tf_op jit(solution)/shard_map/ppermute | solution.py:287
  96.6 3.5 %collective-permute-done.21.w3 = bf16[2,48,1024]{2,1,0:T(8,128)(2,1)S(1)} collective-permute-done((bf16[2,48,1024]{2,1,0:T(8,128)(2,1)S(1)}, bf16[2,48,1024]{2,1,0:T(8,128)(2,1)S(1)}, u32[]{:S(2)}, u32[]{:S(2)}) %collective-permute-start.21) | collective-permute-done | bytes 196640 | tf_op jit(solution)/shard_map/ppermute | solution.py:287
  102.1 3.4 %corr.3 = (bf16[2,4,48,256]{3,2,1,0:T(8,128)(2,1)S(1)}, bf16[2,4,48,256]{3,2,1,0:T(8,128)(2,1)S(1)}, bf16[2,4,48,256]{3,2,1,0:T(8,128)(2,1)S(1)}, bf16[2,4,48,256]{3,2,1,0:T(8,128)(2,1)S(1)}) custom-call(bf16[2,48,1024]{2,1,0:T(8,128)(2,1)S(1)} %get-tuple-element.91.w0, bf16[2,48,1024]{2,1,0:T(8,128)(2,1)S(1)} %collective-permute-done.19.w1, ...), custom_call_target="tpu_custom_call" | custom-call | flops 4000000000 | bytes 65536 | tf_op jit(solution)/shard_map/corr/pallas_call | solution.py:255
  106.6 2.8 %collective-permute-start.34 = (bf16[2,4,48,256]{3,2,1,0:T(8,128)(2,1)S(1)}, bf16[2,4,48,256]{3,2,1,0:T(8,128)(2,1)S(1)}, u32[]{:S(2)}, u32[]{:S(2)}) collective-permute-start(bf16[2,4,48,256]{3,2,1,0:T(8,128)(2,1)S(1)} %get-tuple-element.106), channel_id=1, source_target_pairs={{0,128},{16,144},{32,160},{48,176},{64,192},{80,208},{96,224},{112... | collective-permute-start | bytes 589832 | tf_op jit(solution)/shard_map/ppermute | solution.py:287
  109.9 4.1 %collective-permute-done.33.g1 = bf16[2,4,48,256]{3,2,1,0:T(8,128)(2,1)S(1)} collective-permute-done((bf16[2,4,48,256]{3,2,1,0:T(8,128)(2,1)S(1)}, bf16[2,4,48,256]{3,2,1,0:T(8,128)(2,1)S(1)}, u32[]{:S(2)}, u32[]{:S(2)}) %collective-permute-start.33) | collective-permute-done | bytes 196640 | tf_op jit(solution)/shard_map/ppermute | solution.py:287
  113.9 4.7 %collective-permute-done.34.g2 = bf16[2,4,48,256]{3,2,1,0:T(8,128)(2,1)S(1)} collective-permute-done((bf16[2,4,48,256]{3,2,1,0:T(8,128)(2,1)S(1)}, bf16[2,4,48,256]{3,2,1,0:T(8,128)(2,1)S(1)}, u32[]{:S(2)}, u32[]{:S(2)}) %collective-permute-start.34) | collective-permute-done | bytes 196640 | tf_op jit(solution)/shard_map/ppermute | solution.py:287
  118.9 2.4 %collective-permute-start.37 = (bf16[2,48,256]{2,1,0:T(8,128)(2,1)S(1)}, bf16[2,48,256]{2,1,0:T(8,128)(2,1)S(1)}, u32[]{:S(2)}, u32[]{:S(2)}) collective-permute-start(bf16[2,48,256]{2,1,0:T(8,128)(2,1)S(1)} %get-tuple-element.110), channel_id=1, source_target_pairs={{0,32},{16,48},{32,0},{48,16},{64,96},{80,112},{96,64},{112,80},{1... | collective-permute-start | bytes 147464 | tf_op jit(solution)/shard_map/ppermute | solution.py:287
  121.3 1.9 %collective-permute-start.38 = (bf16[2,48,256]{2,1,0:T(8,128)(2,1)S(1)}, bf16[2,48,256]{2,1,0:T(8,128)(2,1)S(1)}, u32[]{:S(2)}, u32[]{:S(2)}) collective-permute-start(bf16[2,48,256]{2,1,0:T(8,128)(2,1)S(1)} %get-tuple-element.111), channel_id=1, source_target_pairs={{0,48},{16,32},{32,16},{48,0},{64,112},{80,96},{96,80},{112,64},{1... | collective-permute-start | bytes 147464 | tf_op jit(solution)/shard_map/ppermute | solution.py:287
  124.1 3.1 %collective-permute-done.38.g3 = bf16[2,48,256]{2,1,0:T(8,128)(2,1)S(1)} collective-permute-done((bf16[2,48,256]{2,1,0:T(8,128)(2,1)S(1)}, bf16[2,48,256]{2,1,0:T(8,128)(2,1)S(1)}, u32[]{:S(2)}, u32[]{:S(2)}) %collective-permute-start.38) | collective-permute-done | bytes 49184 | tf_op jit(solution)/shard_map/ppermute | solution.py:287
  (85 shorter events, 32.9 us)
Async XLA Ops:
  2.1 8.8 %collective-permute-start = (bf16[96,256]{1,0:T(8,128)(2,1)S(1)}, bf16[96,256]{1,0:T(8,128)(2,1)S(1)}, u32[]{:S(2)}, u32[]{:S(2)}) collective-permute-start(bf16[96,256]{1,0:T(8,128)(2,1)S(1)} %spectra.1), channel_id=1, source_target_pairs={{0,16},{16,0},{32,48},{48,32},{64,80},{80,64},{96,112},{112,96},{1... | collective-permute-start | bytes 147464 | tf_op jit(solution)/shard_map/ppermute | solution.py:287
  4.1 6.8 %collective-permute-start.1 = (bf16[96,256]{1,0:T(8,128)(2,1)S(1)}, bf16[96,256]{1,0:T(8,128)(2,1)S(1)}, u32[]{:S(2)}, u32[]{:S(2)}) collective-permute-start(bf16[96,256]{1,0:T(8,128)(2,1)S(1)} %spectra.1), channel_id=1, source_target_pairs={{0,32},{16,48},{32,0},{48,16},{64,96},{80,112},{96,64},{112,80},{1... | collective-permute-start | bytes 147464 | tf_op jit(solution)/shard_map/ppermute | solution.py:287
  7.3 5.9 %collective-permute-start.2 = (bf16[96,256]{1,0:T(8,128)(2,1)S(1)}, bf16[96,256]{1,0:T(8,128)(2,1)S(1)}, u32[]{:S(2)}, u32[]{:S(2)}) collective-permute-start(bf16[96,256]{1,0:T(8,128)(2,1)S(1)} %spectra.1), channel_id=1, source_target_pairs={{0,48},{16,32},{32,16},{48,0},{64,112},{80,96},{96,80},{112,64},{1... | collective-permute-start | bytes 147464 | tf_op jit(solution)/shard_map/ppermute | solution.py:287
  13.3 6.2 %collective-permute-start.3 = (bf16[4,48,256]{2,1,0:T(8,128)(2,1)S(1)}, bf16[4,48,256]{2,1,0:T(8,128)(2,1)S(1)}, u32[]{:S(2)}, u32[]{:S(2)}) collective-permute-start(bf16[4,48,256]{2,1,0:T(8,128)(2,1)S(1)} %pad_maximum_fusion.1.f0), channel_id=1, source_target_pairs={{0,64},{16,80},{32,96},{48,112},{64,128},{80,144},{96,160},{112,17... | collective-permute-start | bytes 294920 | tf_op jit(solution)/shard_map/ppermute | solution.py:287
  14.9 6.4 %collective-permute-start.4 = (bf16[4,48,256]{2,1,0:T(8,128)(2,1)S(1)}, bf16[4,48,256]{2,1,0:T(8,128)(2,1)S(1)}, u32[]{:S(2)}, u32[]{:S(2)}) collective-permute-start(bf16[4,48,256]{2,1,0:T(8,128)(2,1)S(1)} %pad_maximum_fusion.1.f0), channel_id=1, source_target_pairs={{0,128},{16,144},{32,160},{48,176},{64,192},{80,208},{96,224},{112... | collective-permute-start | bytes 294920 | tf_op jit(solution)/shard_map/ppermute | solution.py:287
  26.4 4.8 %collective-permute-start.9 = (bf16[4,2,48,1024]{3,2,1,0:T(8,128)(2,1)S(1)}, bf16[4,2,48,1024]{3,2,1,0:T(8,128)(2,1)S(1)}, u32[]{:S(2)}, u32[]{:S(2)}) collective-permute-start(bf16[4,2,48,1024]{3,2,1,0:T(8,128)(2,1)S(1)} %bitcast.73), channel_id=1, source_target_pairs={{0,1},{1,0},{2,3},{3,2},{4,5},{5,4},{6,7},{7,6},{8,9},{9,8},{10,11... | collective-permute-start | bytes 2359304 | tf_op jit(solution)/shard_map/ppermute | solution.py:287
  26.5 6.5 %collective-permute-start.6 = (bf16[4,48,256]{2,1,0:T(8,128)(2,1)S(1)}, bf16[4,48,256]{2,1,0:T(8,128)(2,1)S(1)}, u32[]{:S(2)}, u32[]{:S(2)}) collective-permute-start(bf16[4,48,256]{2,1,0:T(8,128)(2,1)S(1)} %pad_maximum_fusion.f0), channel_id=1, source_target_pairs={{0,64},{16,80},{32,96},{48,112},{64,128},{80,144},{96,160},{112,17... | collective-permute-start | bytes 294920 | tf_op jit(solution)/shard_map/ppermute | solution.py:287
  27.5 8.5 %collective-permute-start.7 = (bf16[4,48,256]{2,1,0:T(8,128)(2,1)S(1)}, bf16[4,48,256]{2,1,0:T(8,128)(2,1)S(1)}, u32[]{:S(2)}, u32[]{:S(2)}) collective-permute-start(bf16[4,48,256]{2,1,0:T(8,128)(2,1)S(1)} %pad_maximum_fusion.f0), channel_id=1, source_target_pairs={{0,128},{16,144},{32,160},{48,176},{64,192},{80,208},{96,224},{112... | collective-permute-start | bytes 294920 | tf_op jit(solution)/shard_map/ppermute | solution.py:287
  30.7 5.3 %collective-permute-start.8 = (bf16[4,48,256]{2,1,0:T(8,128)(2,1)S(1)}, bf16[4,48,256]{2,1,0:T(8,128)(2,1)S(1)}, u32[]{:S(2)}, u32[]{:S(2)}) collective-permute-start(bf16[4,48,256]{2,1,0:T(8,128)(2,1)S(1)} %pad_maximum_fusion.f0), channel_id=1, source_target_pairs={{0,192},{16,208},{32,224},{48,240},{64,0},{80,16},{96,32},{112,48}... | collective-permute-start | bytes 294920 | tf_op jit(solution)/shard_map/ppermute | solution.py:287
  40.2 6.2 %collective-permute-start.13 = (bf16[4,2,48,1024]{3,2,1,0:T(8,128)(2,1)S(1)}, bf16[4,2,48,1024]{3,2,1,0:T(8,128)(2,1)S(1)}, u32[]{:S(2)}, u32[]{:S(2)}) collective-permute-start(bf16[4,2,48,1024]{3,2,1,0:T(8,128)(2,1)S(1)} %bitcast.72), channel_id=1, source_target_pairs={{0,1},{1,0},{2,3},{3,2},{4,5},{5,4},{6,7},{7,6},{8,9},{9,8},{10,11... | collective-permute-start | bytes 2359304 | tf_op jit(solution)/shard_map/ppermute | solution.py:287
  41.3 7.8 %collective-permute-start.10 = (bf16[2,48,1024]{2,1,0:T(8,128)(2,1)S(1)}, bf16[2,48,1024]{2,1,0:T(8,128)(2,1)S(1)}, u32[]{:S(2)}, u32[]{:S(2)}) collective-permute-start(bf16[2,48,1024]{2,1,0:T(8,128)(2,1)S(1)} %get-tuple-element.67), channel_id=1, source_target_pairs={{0,2},{1,3},{2,4},{3,5},{4,6},{5,7},{6,0},{7,1},{8,10},{9,11},{10,... | collective-permute-start | bytes 589832 | tf_op jit(solution)/shard_map/ppermute | solution.py:287
  42.9 9.3 %collective-permute-start.11 = (bf16[2,48,1024]{2,1,0:T(8,128)(2,1)S(1)}, bf16[2,48,1024]{2,1,0:T(8,128)(2,1)S(1)}, u32[]{:S(2)}, u32[]{:S(2)}) collective-permute-start(bf16[2,48,1024]{2,1,0:T(8,128)(2,1)S(1)} %get-tuple-element.68), channel_id=1, source_target_pairs={{0,4},{1,5},{2,6},{3,7},{4,0},{5,1},{6,2},{7,3},{8,12},{9,13},{10,... | collective-permute-start | bytes 589832 | tf_op jit(solution)/shard_map/ppermute | solution.py:287
  43.9 11.1 %collective-permute-start.12 = (bf16[2,48,1024]{2,1,0:T(8,128)(2,1)S(1)}, bf16[2,48,1024]{2,1,0:T(8,128)(2,1)S(1)}, u32[]{:S(2)}, u32[]{:S(2)}) collective-permute-start(bf16[2,48,1024]{2,1,0:T(8,128)(2,1)S(1)} %get-tuple-element.69), channel_id=1, source_target_pairs={{0,6},{1,7},{2,0},{3,1},{4,2},{5,3},{6,4},{7,5},{8,14},{9,15},{10,... | collective-permute-start | bytes 589832 | tf_op jit(solution)/shard_map/ppermute | solution.py:287
  55.0 9.1 %collective-permute-start.15 = (bf16[2,48,1024]{2,1,0:T(8,128)(2,1)S(1)}, bf16[2,48,1024]{2,1,0:T(8,128)(2,1)S(1)}, u32[]{:S(2)}, u32[]{:S(2)}) collective-permute-start(bf16[2,48,1024]{2,1,0:T(8,128)(2,1)S(1)} %get-tuple-element.79), channel_id=1, source_target_pairs={{0,2},{1,3},{2,4},{3,5},{4,6},{5,7},{6,0},{7,1},{8,10},{9,11},{10,... | collective-permute-start | bytes 589832 | tf_op jit(solution)/shard_map/ppermute | solution.py:287
  56.3 9.4 %collective-permute-start.16 = (bf16[2,48,1024]{2,1,0:T(8,128)(2,1)S(1)}, bf16[2,48,1024]{2,1,0:T(8,128)(2,1)S(1)}, u32[]{:S(2)}, u32[]{:S(2)}) collective-permute-start(bf16[2,48,1024]{2,1,0:T(8,128)(2,1)S(1)} %get-tuple-element.80), channel_id=1, source_target_pairs={{0,4},{1,5},{2,6},{3,7},{4,0},{5,1},{6,2},{7,3},{8,12},{9,13},{10,... | collective-permute-start | bytes 589832 | tf_op jit(solution)/shard_map/ppermute | solution.py:287
  57.8 10.1 %collective-permute-start.17 = (bf16[2,48,1024]{2,1,0:T(8,128)(2,1)S(1)}, bf16[2,48,1024]{2,1,0:T(8,128)(2,1)S(1)}, u32[]{:S(2)}, u32[]{:S(2)}) collective-permute-start(bf16[2,48,1024]{2,1,0:T(8,128)(2,1)S(1)} %get-tuple-element.81), channel_id=1, source_target_pairs={{0,6},{1,7},{2,0},{3,1},{4,2},{5,3},{6,4},{7,5},{8,14},{9,15},{10,... | collective-permute-start | bytes 589832 | tf_op jit(solution)/shard_map/ppermute | solution.py:287
  59.5 13.1 %collective-permute-start.14 = (bf16[2,48,1024]{2,1,0:T(8,128)(2,1)S(1)}, bf16[2,48,1024]{2,1,0:T(8,128)(2,1)S(1)}, u32[]{:S(2)}, u32[]{:S(2)}) collective-permute-start(bf16[2,48,1024]{2,1,0:T(8,128)(2,1)S(1)} %add_convert_fusion.1), channel_id=1, source_target_pairs={{0,8},{1,9},{2,10},{3,11},{4,12},{5,13},{6,14},{7,15},{8,0},{9,1},... | collective-permute-start | bytes 589832 | tf_op jit(solution)/shard_map/ppermute | solution.py:287
  68.0 13.9 %collective-permute-start.18 = (bf16[2,48,1024]{2,1,0:T(8,128)(2,1)S(1)}, bf16[2,48,1024]{2,1,0:T(8,128)(2,1)S(1)}, u32[]{:S(2)}, u32[]{:S(2)}) collective-permute-start(bf16[2,48,1024]{2,1,0:T(8,128)(2,1)S(1)} %add_convert_fusion), channel_id=1, source_target_pairs={{0,8},{1,9},{2,10},{3,11},{4,12},{5,13},{6,14},{7,15},{8,0},{9,1},... | collective-permute-start | bytes 589832 | tf_op jit(solution)/shard_map/ppermute | solution.py:287
  74.3 10.8 %collective-permute-start.22 = (bf16[2,48,1024]{2,1,0:T(8,128)(2,1)S(1)}, bf16[2,48,1024]{2,1,0:T(8,128)(2,1)S(1)}, u32[]{:S(2)}, u32[]{:S(2)}) collective-permute-start(bf16[2,48,1024]{2,1,0:T(8,128)(2,1)S(1)} %get-tuple-element.92.w0), channel_id=1, source_target_pairs={{0,2},{1,3},{2,4},{3,5},{4,6},{5,7},{6,0},{7,1},{8,10},{9,11},{10,... | collective-permute-start | bytes 589832 | tf_op jit(solution)/shard_map/ppermute | solution.py:287
  75.0 10.7 %collective-permute-start.23 = (bf16[2,48,1024]{2,1,0:T(8,128)(2,1)S(1)}, bf16[2,48,1024]{2,1,0:T(8,128)(2,1)S(1)}, u32[]{:S(2)}, u32[]{:S(2)}) collective-permute-start(bf16[2,48,1024]{2,1,0:T(8,128)(2,1)S(1)} %get-tuple-element.92.w0), channel_id=1, source_target_pairs={{0,4},{1,5},{2,6},{3,7},{4,0},{5,1},{6,2},{7,3},{8,12},{9,13},{10,... | collective-permute-start | bytes 589832 | tf_op jit(solution)/shard_map/ppermute | solution.py:287
  77.0 9.4 %collective-permute-start.24 = (bf16[2,48,1024]{2,1,0:T(8,128)(2,1)S(1)}, bf16[2,48,1024]{2,1,0:T(8,128)(2,1)S(1)}, u32[]{:S(2)}, u32[]{:S(2)}) collective-permute-start(bf16[2,48,1024]{2,1,0:T(8,128)(2,1)S(1)} %get-tuple-element.92.w0), channel_id=1, source_target_pairs={{0,6},{1,7},{2,0},{3,1},{4,2},{5,3},{6,4},{7,5},{8,14},{9,15},{10,... | collective-permute-start | bytes 589832 | tf_op jit(solution)/shard_map/ppermute | solution.py:287
  85.1 4.7 %collective-permute-start.26 = (bf16[2,48,1024]{2,1,0:T(8,128)(2,1)S(1)}, bf16[2,48,1024]{2,1,0:T(8,128)(2,1)S(1)}, u32[]{:S(2)}, u32[]{:S(2)}) collective-permute-start(bf16[2,48,1024]{2,1,0:T(8,128)(2,1)S(1)} %collective-permute-done.22.w1), channel_id=1, source_target_pairs={{0,1},{1,0},{2,3},{3,2},{4,5},{5,4},{6,7},{7,6},{8,9},{9,8},{10,11... | collective-permute-start | bytes 589832 | tf_op jit(solution)/shard_map/ppermute | solution.py:287
  85.6 5.2 %collective-permute-start.27 = (bf16[2,48,1024]{2,1,0:T(8,128)(2,1)S(1)}, bf16[2,48,1024]{2,1,0:T(8,128)(2,1)S(1)}, u32[]{:S(2)}, u32[]{:S(2)}) collective-permute-start(bf16[2,48,1024]{2,1,0:T(8,128)(2,1)S(1)} %collective-permute-done.23.w2), channel_id=1, source_target_pairs={{0,1},{1,0},{2,3},{3,2},{4,5},{5,4},{6,7},{7,6},{8,9},{9,8},{10,11... | collective-permute-start | bytes 589832 | tf_op jit(solution)/shard_map/ppermute | solution.py:287
  86.4 7.9 %collective-permute-start.19 = (bf16[2,48,1024]{2,1,0:T(8,128)(2,1)S(1)}, bf16[2,48,1024]{2,1,0:T(8,128)(2,1)S(1)}, u32[]{:S(2)}, u32[]{:S(2)}) collective-permute-start(bf16[2,48,1024]{2,1,0:T(8,128)(2,1)S(1)} %get-tuple-element.91.w0), channel_id=1, source_target_pairs={{0,2},{1,3},{2,4},{3,5},{4,6},{5,7},{6,0},{7,1},{8,10},{9,11},{10,... | collective-permute-start | bytes 589832 | tf_op jit(solution)/shard_map/ppermute | solution.py:287
  87.3 9.3 %collective-permute-start.20 = (bf16[2,48,1024]{2,1,0:T(8,128)(2,1)S(1)}, bf16[2,48,1024]{2,1,0:T(8,128)(2,1)S(1)}, u32[]{:S(2)}, u32[]{:S(2)}) collective-permute-start(bf16[2,48,1024]{2,1,0:T(8,128)(2,1)S(1)} %get-tuple-element.91.w0), channel_id=1, source_target_pairs={{0,4},{1,5},{2,6},{3,7},{4,0},{5,1},{6,2},{7,3},{8,12},{9,13},{10,... | collective-permute-start | bytes 589832 | tf_op jit(solution)/shard_map/ppermute | solution.py:287
  89.8 10.3 %collective-permute-start.21 = (bf16[2,48,1024]{2,1,0:T(8,128)(2,1)S(1)}, bf16[2,48,1024]{2,1,0:T(8,128)(2,1)S(1)}, u32[]{:S(2)}, u32[]{:S(2)}) collective-permute-start(bf16[2,48,1024]{2,1,0:T(8,128)(2,1)S(1)} %get-tuple-element.91.w0), channel_id=1, source_target_pairs={{0,6},{1,7},{2,0},{3,1},{4,2},{5,3},{6,4},{7,5},{8,14},{9,15},{10,... | collective-permute-start | bytes 589832 | tf_op jit(solution)/shard_map/ppermute | solution.py:287
  90.9 9.7 %collective-permute-start.29 = (bf16[2,48,1024]{2,1,0:T(8,128)(2,1)S(1)}, bf16[2,48,1024]{2,1,0:T(8,128)(2,1)S(1)}, u32[]{:S(2)}, u32[]{:S(2)}) collective-permute-start(bf16[2,48,1024]{2,1,0:T(8,128)(2,1)S(1)} %get-tuple-element.91.w0), channel_id=1, source_target_pairs={{0,1},{1,0},{2,3},{3,2},{4,5},{5,4},{6,7},{7,6},{8,9},{9,8},{10,11... | collective-permute-start | bytes 589832 | tf_op jit(solution)/shard_map/ppermute | solution.py:287
  105.5 8.4 %collective-permute-start.33 = (bf16[2,4,48,256]{3,2,1,0:T(8,128)(2,1)S(1)}, bf16[2,4,48,256]{3,2,1,0:T(8,128)(2,1)S(1)}, u32[]{:S(2)}, u32[]{:S(2)}) collective-permute-start(bf16[2,4,48,256]{3,2,1,0:T(8,128)(2,1)S(1)} %get-tuple-element.105), channel_id=1, source_target_pairs={{0,64},{16,80},{32,96},{48,112},{64,128},{80,144},{96,160},{112,17... | collective-permute-start | bytes 589832 | tf_op jit(solution)/shard_map/ppermute | solution.py:287
  106.6 12.0 %collective-permute-start.34 = (bf16[2,4,48,256]{3,2,1,0:T(8,128)(2,1)S(1)}, bf16[2,4,48,256]{3,2,1,0:T(8,128)(2,1)S(1)}, u32[]{:S(2)}, u32[]{:S(2)}) collective-permute-start(bf16[2,4,48,256]{3,2,1,0:T(8,128)(2,1)S(1)} %get-tuple-element.106), channel_id=1, source_target_pairs={{0,128},{16,144},{32,160},{48,176},{64,192},{80,208},{96,224},{112... | collective-permute-start | bytes 589832 | tf_op jit(solution)/shard_map/ppermute | solution.py:287
  109.4 9.3 %collective-permute-start.35 = (bf16[2,4,48,256]{3,2,1,0:T(8,128)(2,1)S(1)}, bf16[2,4,48,256]{3,2,1,0:T(8,128)(2,1)S(1)}, u32[]{:S(2)}, u32[]{:S(2)}) collective-permute-start(bf16[2,4,48,256]{3,2,1,0:T(8,128)(2,1)S(1)} %get-tuple-element.107), channel_id=1, source_target_pairs={{0,192},{16,208},{32,224},{48,240},{64,0},{80,16},{96,32},{112,48}... | collective-permute-start | bytes 589832 | tf_op jit(solution)/shard_map/ppermute | solution.py:287
  118.9 5.3 %collective-permute-start.37 = (bf16[2,48,256]{2,1,0:T(8,128)(2,1)S(1)}, bf16[2,48,256]{2,1,0:T(8,128)(2,1)S(1)}, u32[]{:S(2)}, u32[]{:S(2)}) collective-permute-start(bf16[2,48,256]{2,1,0:T(8,128)(2,1)S(1)} %get-tuple-element.110), channel_id=1, source_target_pairs={{0,32},{16,48},{32,0},{48,16},{64,96},{80,112},{96,64},{112,80},{1... | collective-permute-start | bytes 147464 | tf_op jit(solution)/shard_map/ppermute | solution.py:287
  121.3 5.9 %collective-permute-start.38 = (bf16[2,48,256]{2,1,0:T(8,128)(2,1)S(1)}, bf16[2,48,256]{2,1,0:T(8,128)(2,1)S(1)}, u32[]{:S(2)}, u32[]{:S(2)}) collective-permute-start(bf16[2,48,256]{2,1,0:T(8,128)(2,1)S(1)} %get-tuple-element.111), channel_id=1, source_target_pairs={{0,48},{16,32},{32,16},{48,0},{64,112},{80,96},{96,80},{112,64},{1... | collective-permute-start | bytes 147464 | tf_op jit(solution)/shard_map/ppermute | solution.py:287
  (14 other events, 215.5 us)

commit v2 on v1

--- a/solution.py
+++ b/solution.py
@@ -133,7 +133,7 @@
     return jnp.where(even, -pltpu.roll(x, n - 1, 0), pltpu.roll(x, 1, 0))
 
 
-def conv_kernel(f0, f1, f2, f3, r_ref, give, keep, l1, l2):
+def conv_kernel(chunk, f0, f1, f2, f3, r_ref, give, keep, l1, l2):
     x, zl, zh, y, c = place()
     for dx, ref in enumerate((f0, f1, f2, f3)):
         for dz in range(4):
@@ -141,7 +141,7 @@
             zb = zl ^ dz
             yb = lax.rem(xb, 2) * 2 + zb // 2
             to = lax.rem(zb + c, 2) * 8 + lax.rem(yb + 4 - y, 4) * 2 + lax.rem(xb // 2 + zh, 2)
-            rows = ref[dz].astype(F32)
+            rows = ref[dz, chunk * ROWS : (chunk + 1) * ROWS].astype(F32)
             l1[to] = rows
             l2[to] = swap_rows(rows)
 
@@ -166,11 +166,11 @@
     lax.fori_loop(0, 2 * NS // sb, step, 0)
 
 
-def convolve(pieces, reflection):
+def convolve(pieces, reflection, chunk):
     give, keep = call(
-        conv_kernel,
+        functools.partial(conv_kernel, chunk),
         [jax.ShapeDtypeStruct((8, 2, ROWS // 2, NS), BF)] * 2,
-        "conv",
+        f"conv{chunk}",
         in_specs=[pl.BlockSpec(memory_space=pltpu.VMEM)] * 5,
         scratch_shapes=[pltpu.VMEM((16, ROWS, NR), F32)] * 2,
         cost_estimate=cost(4),
@@ -178,17 +178,18 @@
     return give.reshape(4, 2, ROWS, NS), keep.reshape(4, 2, ROWS, NS)
 
 
-def window_kernel(p0, p1, p2, p3, r_ref, on_ref, a_ref, t_ref, w_ref, up_ref):
+def window_kernel(chunk, p0, p1, p2, p3, r_ref, on_ref, a_ref, t_ref, w_ref, up_ref):
     steps = lax.broadcasted_iota(jnp.int32, (NT, NS), 0)
 
     def half(i, carry):
         e = 1 - i
+        first = lax.rem(lax.axis_index("rcv") + 8 * e, 16) * NP + chunk * PC
         total = (p0[e].astype(F32) + p1[e].astype(F32)) + (p2[e].astype(F32) + p3[e].astype(F32))
         u = hi_lo_hi(total + r_ref[i].astype(F32), 0)
         acc = jnp.zeros((2 * ROWS, NS), F32)
         for j in range(PC):
             field = dot(a_ref[j], u)
-            field = jnp.where(steps < on_ref[e, j : j + 1, :], field, 0.0).astype(BF)
+            field = jnp.where(steps < on_ref[pl.ds(first + j, 1), :], field, 0.0).astype(BF)
             up_ref[j] = field
             acc += dot(t_ref[j], field)
         w_ref[e] = (acc[:ROWS] + acc[ROWS:]).astype(BF)
@@ -215,8 +216,7 @@
         copy.wait()
 
 
-def corr_kernel(w0, w1, w2, w3, v0, v1, v2, v3, r_ref, *rest):
-    *firsts, o0, o1, o2, o3, out, acc = rest
+def corr_kernel(w0, w1, w2, w3, v0, v1, v2, v3, r_ref, o0, o1, o2, o3, out, acc):
     x, zl, zh, y, c = place()
     refs = (w0, w1, w2, w3, v0, v1, v2, v3)
     row = lax.broadcasted_iota(jnp.int32, (256, NR), 0)
@@ -243,29 +243,26 @@
         zb = lax.rem(yb, 2) * 2 + lax.rem(c + other, 2)
         out[lax.rem(xb + 4 - x, 4), zb ^ zl] = jnp.concatenate([acc[t, 16 * i : 16 * i + 16] for t in range(3)], axis=0).astype(BF)
     for d, ref in enumerate((o0, o1, o2, o3)):
-        if firsts:
-            ref[0] = firsts[d][...]
-            ref[1] = out[d]
-        else:
-            ref[...] = out[d]
-
-
-def correlate(waves, reflection, firsts=()):
-    shape = (4, ROWS, NR) if not firsts else (2, 4, ROWS, NR)
+        ref[...] = out[d]
+
+
+def correlate(waves, reflection):
     return call(
         corr_kernel,
-        [jax.ShapeDtypeStruct(shape, BF)] * 4,
+        [jax.ShapeDtypeStruct((4, ROWS, NR), BF)] * 4,
         "corr",
-        in_specs=[pl.BlockSpec(memory_space=pltpu.VMEM)] * (9 + len(firsts)),
+        in_specs=[pl.BlockSpec(memory_space=pltpu.VMEM)] * 9,
         scratch_shapes=[pltpu.VMEM((4, 4, ROWS, NR), BF), pltpu.VMEM((3, 256, NR), F32)],
         cost_estimate=cost(4),
         mib=16,
-    )(*waves, reflection, *firsts)
-
-
-def sum_kernel(g0, g1, g2, g3, keep, *gives):
+    )(*waves, reflection)
+
+
+def sum_kernel(*refs):
+    ins, (keep, *gives) = refs[: 4 * CH], refs[4 * CH :]
     for h in range(CH):
-        total = (g0[h].astype(F32) + g1[h].astype(F32)) + (g2[h].astype(F32) + g3[h].astype(F32))
+        g = ins[4 * h : 4 * h + 4]
+        total = (g[0][...].astype(F32) + g[1][...].astype(F32)) + (g[2][...].astype(F32) + g[3][...].astype(F32))
         keep[h] = total[0]
         for d, give in enumerate(gives):
             give[h] = total[d + 1].astype(BF)
@@ -331,9 +328,6 @@
     )(
         focusing, jnp.asarray(trace_table())
     )
-    rcv = lax.axis_index("rcv")
-    near_far = [lax.dynamic_slice_in_dim(onset_source, r * NP, NP, 0) for r in (rcv, rcv ^ 8)]
-    onsets = [jnp.stack([o[h * PC : (h + 1) * PC] for o in near_far]) for h in range(CH)]
     near = [send(spectra, "src", to_zl(d)) for d in (1, 2, 3)]
     held = call(
         load_kernel,
@@ -346,9 +340,8 @@
         mib=50,
     )(reflection)
     near, [spectra, held] = together(near, [spectra, held])
-    near = [spectra, *near]
-    stacks = [jnp.stack([n[h * ROWS : (h + 1) * ROWS] for n in near]) for h in range(CH)]
-    pieces = [[stacks[0]] + [send(stacks[0], "src", to_x(d)) for d in (1, 2, 3)]]
+    stack = jnp.stack([spectra, *near])
+    pieces = [stack] + [send(stack, "src", to_x(d)) for d in (1, 2, 3)]
 
     def summed(give, keep):
         got = send(give, "rcv", to_core)
@@ -362,19 +355,15 @@
 
     def window(both, half, h):
         return call(
-            window_kernel,
+            functools.partial(window_kernel, h),
             (jax.ShapeDtypeStruct((2, ROWS, NS), BF), jax.ShapeDtypeStruct((PC, NT, NS), BF)),
-            "window",
+            f"window{h}",
             cost_estimate=cost(2),
-        )(*both, half, onsets[h], t_samp, t_spec)
-
-    give_a, keep_a = convolve(pieces[0], held)
-    [second], [keep_a] = together([stacks[1]], [keep_a])
-    pieces.append([second] + [send(second, "src", to_x(d)) for d in (1, 2, 3)])
-    sum_a = summed(give_a, keep_a)
-    pieces[1][1:], sum_a = together(pieces[1][1:], sum_a)
+        )(*both, half, onset_source, t_samp, t_spec)
+
+    sum_a = summed(*convolve(pieces, held, 0))
     both_a = over_y(sum_a)
-    sum_b = summed(*convolve(pieces[1], held))
+    sum_b = summed(*convolve(pieces, held, 1))
     both_a[1:], sum_b = together(both_a[1:], sum_b)
     both_b = over_y(sum_b)
     half_a = send(half_sum(both_a), "rcv", to_zh)
@@ -396,9 +385,10 @@
     def over_x(back):
         return [back[0]] + [send(back[d], "src", to_x(d)) for d in (1, 2, 3)]
 
-    back_a = list(correlate(over_core(own_a), held))
-    own_b[1:], back_a = together(own_b[1:], back_a)
-    parts = over_x(correlate(over_core(own_b), held, back_a))
+    parts_a = over_x(correlate(over_core(own_a), held))
+    own_b[1:3], parts_a[:1] = together(own_b[1:3], parts_a[:1])
+    own_b[3:], parts_a[2:3] = together(own_b[3:], parts_a[2:3])
+    parts = parts_a + over_x(correlate(over_core(own_b), held))
 
     keep, *gives = call(
         sum_kernel,

time: 129 us -> 120 us (0.930)
  waiting for transfers between devices: 45.5 us -> 34.8 us
  starting transfers between devices: 53.4 us -> 55.8 us
    ppermute x39, waiting for transfers between devices: 45.5 us -> 34.8 us  [send(): return lax.ppermute(value, axis, [(i, to(i)) for i in range(16)])]
    ppermute x39, starting transfers between devices: 53.4 us -> 55.8 us  [send(): return lax.ppermute(value, axis, [(i, to(i)) for i in range(16)])]
  transfers between devices with their start and end apart: 39 -> 39, of which waited for: 22 -> 16; matrix products, arithmetic and copies ran while one was open for 2% -> 1% of each run, Pallas kernels for 9% -> 16%
where the time goes in v2:
time: 120 us; the launch traced here: 119 us
  starting transfers between devices  55.8 us (46%)
  waiting for transfers between devices  34.8 us (29%)
  Pallas kernels  26.4 us (22%)
    ppermute x39, starting transfers between devices, send(): return lax.ppermute(value, axis, [(i, to(i)) for i in range(16)])  55.8 us
    ppermute x39, waiting for transfers between devices, send(): return lax.ppermute(value, axis, [(i, to(i)) for i in range(16)])  34.8 us
    pallas_call x2, Pallas kernels, convolve(): call(functools.partial(conv_kernel, chunk), [jax.ShapeDtypeStruct((8, 2,...  8.36 us
    pallas_call x2, Pallas kernels, correlate(): call(corr_kernel, [jax.ShapeDtypeStruct((4, ROWS, NR), BF)] * 4, 'corr',...  6.65 us
    pallas_call x1, Pallas kernels, on_device(): call(load_kernel, pltpu.VMEM((2, NF, NS, NR), BF), 'load', in_specs=[pl.B...  3.51 us
    pallas_call x2, Pallas kernels, window(): call(functools.partial(window_kernel, h), (jax.ShapeDtypeStruct((2, ROWS,...  3.27 us
  transfers between devices with their start and end apart: 39, of which 16 were waited for; matrix products, arithmetic and copies ran while one was open for 1% of the time, Pallas kernels for 16%

profile of v2, /device:TPU:8, one launch (start us, length us, event | category | flops | bytes accessed | tf_op | source)
XLA Modules:
  0.0 119.1 jit_solution(345366656681681614)
XLA Ops:
  2.1 2.0 %collective-permute-start = (bf16[96,256]{1,0:T(8,128)(2,1)S(1)}, bf16[96,256]{1,0:T(8,128)(2,1)S(1)}, u32[]{:S(2)}, u32[]{:S(2)}) collective-permute-start(bf16[96,256]{1,0:T(8,128)(2,1)S(1)} %spectra.1), channel_id=1, source_target_pairs={{0,16},{16,0},{32,48},{48,32},{64,80},{80,64},{96,112},{112,96},{1... | collective-permute-start | bytes 147464 | tf_op jit(solution)/shard_map/ppermute | solution.py:284
  4.1 3.3 %collective-permute-start.1 = (bf16[96,256]{1,0:T(8,128)(2,1)S(1)}, bf16[96,256]{1,0:T(8,128)(2,1)S(1)}, u32[]{:S(2)}, u32[]{:S(2)}) collective-permute-start(bf16[96,256]{1,0:T(8,128)(2,1)S(1)} %spectra.1), channel_id=1, source_target_pairs={{0,32},{16,48},{32,0},{48,16},{64,96},{80,112},{96,64},{112,80},{1... | collective-permute-start | bytes 147464 | tf_op jit(solution)/shard_map/ppermute | solution.py:284
  7.3 3.5 %load.1.r_ref = bf16[2,8,1024,256]{3,2,1,0:T(8,128)(2,1)S(1)} custom-call(bf16[2,8,1024,256]{3,2,1,0:T(8,128)(2,1)} %r_hbm.1), custom_call_target="tpu_custom_call" | custom-call | flops 3000000000 | bytes 65536 | tf_op jit(solution)/shard_map/load/pallas_call | solution.py:332
  10.9 2.3 %collective-permute-done.2 = bf16[96,256]{1,0:T(8,128)(2,1)S(1)} collective-permute-done((bf16[96,256]{1,0:T(8,128)(2,1)S(1)}, bf16[96,256]{1,0:T(8,128)(2,1)S(1)}, u32[]{:S(2)}, u32[]{:S(2)}) %collective-permute-start.2) | collective-permute-done | bytes 49184 | tf_op jit(solution)/shard_map/ppermute | solution.py:284
  14.8 2.7 %collective-permute-start.4 = (bf16[4,96,256]{2,1,0:T(8,128)(2,1)S(1)}, bf16[4,96,256]{2,1,0:T(8,128)(2,1)S(1)}, u32[]{:S(2)}, u32[]{:S(2)}) collective-permute-start(bf16[4,96,256]{2,1,0:T(8,128)(2,1)S(1)} %pad_maximum_fusion.f0), channel_id=1, source_target_pairs={{0,128},{16,144},{32,160},{48,176},{64,192},{80,208},{96,224},{112... | collective-permute-start | bytes 589832 | tf_op jit(solution)/shard_map/ppermute | solution.py:284
  19.0 3.3 %collective-permute-done.3.f1 = bf16[4,96,256]{2,1,0:T(8,128)(2,1)S(1)} collective-permute-done((bf16[4,96,256]{2,1,0:T(8,128)(2,1)S(1)}, bf16[4,96,256]{2,1,0:T(8,128)(2,1)S(1)}, u32[]{:S(2)}, u32[]{:S(2)}) %collective-permute-start.3) | collective-permute-done | bytes 196640 | tf_op jit(solution)/shard_map/ppermute | solution.py:284
  22.3 2.4 %collective-permute-done.4.f2 = bf16[4,96,256]{2,1,0:T(8,128)(2,1)S(1)} collective-permute-done((bf16[4,96,256]{2,1,0:T(8,128)(2,1)S(1)}, bf16[4,96,256]{2,1,0:T(8,128)(2,1)S(1)}, u32[]{:S(2)}, u32[]{:S(2)}) %collective-permute-start.4) | collective-permute-done | bytes 196640 | tf_op jit(solution)/shard_map/ppermute | solution.py:284
  24.7 4.2 %conv0.1 = (bf16[8,2,24,1024]{3,2,1,0:T(8,128)(2,1)S(1)}, bf16[8,2,24,1024]{3,2,1,0:T(8,128)(2,1)S(1)}) custom-call(bf16[4,96,256]{2,1,0:T(8,128)(2,1)S(1)} %pad_maximum_fusion.f0, bf16[4,96,256]{2,1,0:T(8,128)(2,1)S(1)} %collective-permute-done.3.f1, bf16[4,96,256]{2,1,0:T(8,128)(2,1)S(1)} %collective-permute-done.4.f2, ...), custom_call_target="tpu_custom_call" | custom-call | flops 4000000000 | bytes 65536 | tf_op jit(solution)/shard_map/conv0/pallas_call | solution.py:170
  29.0 4.2 %conv1.1 = (bf16[8,2,24,1024]{3,2,1,0:T(8,128)(2,1)S(1)}, bf16[8,2,24,1024]{3,2,1,0:T(8,128)(2,1)S(1)}) custom-call(bf16[4,96,256]{2,1,0:T(8,128)(2,1)S(1)} %pad_maximum_fusion.f0, bf16[4,96,256]{2,1,0:T(8,128)(2,1)S(1)} %collective-permute-done.3.f1, bf16[4,96,256]{2,1,0:T(8,128)(2,1)S(1)} %collective-permute-done.4.f2, ...), custom_call_target="tpu_custom_call" | custom-call | flops 4000000000 | bytes 65536 | tf_op jit(solution)/shard_map/conv1/pallas_call | solution.py:170
  34.2 1.7 %collective-permute-start.7 = (bf16[2,48,1024]{2,1,0:T(8,128)(2,1)S(1)}, bf16[2,48,1024]{2,1,0:T(8,128)(2,1)S(1)}, u32[]{:S(2)}, u32[]{:S(2)}) collective-permute-start(bf16[2,48,1024]{2,1,0:T(8,128)(2,1)S(1)} %get-tuple-element.106), channel_id=1, source_target_pairs={{0,2},{1,3},{2,4},{3,5},{4,6},{5,7},{6,0},{7,1},{8,10},{9,11},{10,... | collective-permute-start | bytes 589832 | tf_op jit(solution)/shard_map/ppermute | solution.py:284
  36.8 2.4 %collective-permute-start.9 = (bf16[2,48,1024]{2,1,0:T(8,128)(2,1)S(1)}, bf16[2,48,1024]{2,1,0:T(8,128)(2,1)S(1)}, u32[]{:S(2)}, u32[]{:S(2)}) collective-permute-start(bf16[2,48,1024]{2,1,0:T(8,128)(2,1)S(1)} %get-tuple-element.104), channel_id=1, source_target_pairs={{0,6},{1,7},{2,0},{3,1},{4,2},{5,3},{6,4},{7,5},{8,14},{9,15},{10,... | collective-permute-start | bytes 589832 | tf_op jit(solution)/shard_map/ppermute | solution.py:284
  39.5 2.5 %collective-permute-done.7.p1 = bf16[2,48,1024]{2,1,0:T(8,128)(2,1)S(1)} collective-permute-done((bf16[2,48,1024]{2,1,0:T(8,128)(2,1)S(1)}, bf16[2,48,1024]{2,1,0:T(8,128)(2,1)S(1)}, u32[]{:S(2)}, u32[]{:S(2)}) %collective-permute-start.7) | collective-permute-done | bytes 196640 | tf_op jit(solution)/shard_map/ppermute | solution.py:284
  42.0 3.1 %collective-permute-done.8.p2 = bf16[2,48,1024]{2,1,0:T(8,128)(2,1)S(1)} collective-permute-done((bf16[2,48,1024]{2,1,0:T(8,128)(2,1)S(1)}, bf16[2,48,1024]{2,1,0:T(8,128)(2,1)S(1)}, u32[]{:S(2)}, u32[]{:S(2)}) %collective-permute-start.8) | collective-permute-done | bytes 196640 | tf_op jit(solution)/shard_map/ppermute | solution.py:284
  45.1 2.3 %collective-permute-done.9.p3 = bf16[2,48,1024]{2,1,0:T(8,128)(2,1)S(1)} collective-permute-done((bf16[2,48,1024]{2,1,0:T(8,128)(2,1)S(1)}, bf16[2,48,1024]{2,1,0:T(8,128)(2,1)S(1)}, u32[]{:S(2)}, u32[]{:S(2)}) %collective-permute-start.9) | collective-permute-done | bytes 196640 | tf_op jit(solution)/shard_map/ppermute | solution.py:284
  52.0 5.0 %collective-permute-start.11 = (bf16[2,48,1024]{2,1,0:T(8,128)(2,1)S(1)}, bf16[2,48,1024]{2,1,0:T(8,128)(2,1)S(1)}, u32[]{:S(2)}, u32[]{:S(2)}) collective-permute-start(bf16[2,48,1024]{2,1,0:T(8,128)(2,1)S(1)} %get-tuple-element.90), channel_id=1, source_target_pairs={{0,8},{1,9},{2,10},{3,11},{4,12},{5,13},{6,14},{7,15},{8,0},{9,1},... | collective-permute-start | bytes 589832 | tf_op jit(solution)/shard_map/ppermute | solution.py:284
  57.8 2.0 %collective-permute-done.14.p3 = bf16[2,48,1024]{2,1,0:T(8,128)(2,1)S(1)} collective-permute-done((bf16[2,48,1024]{2,1,0:T(8,128)(2,1)S(1)}, bf16[2,48,1024]{2,1,0:T(8,128)(2,1)S(1)}, u32[]{:S(2)}, u32[]{:S(2)}) %collective-permute-start.14) | collective-permute-done | bytes 196640 | tf_op jit(solution)/shard_map/ppermute | solution.py:284
  60.0 5.2 %collective-permute-start.15 = (bf16[2,48,1024]{2,1,0:T(8,128)(2,1)S(1)}, bf16[2,48,1024]{2,1,0:T(8,128)(2,1)S(1)}, u32[]{:S(2)}, u32[]{:S(2)}) collective-permute-start(bf16[2,48,1024]{2,1,0:T(8,128)(2,1)S(1)} %add_convert_fusion), channel_id=1, source_target_pairs={{0,8},{1,9},{2,10},{3,11},{4,12},{5,13},{6,14},{7,15},{8,0},{9,1},... | collective-permute-start | bytes 589832 | tf_op jit(solution)/shard_map/ppermute | solution.py:284
  65.2 1.6 %window0.1 = (bf16[2,48,1024]{2,1,0:T(8,128)(2,1)S(1)}, bf16[3,128,1024]{2,1,0:T(8,128)(2,1)S(1)}) custom-call(bf16[2,48,1024]{2,1,0:T(8,128)(2,1)S(1)} %get-tuple-element.91.p0, bf16[2,48,1024]{2,1,0:T(8,128)(2,1)S(1)} %collective-permute-done.7.p1, bf16[2,48,1024]{2,1,0:T(8,128)(2,1)S(1)} %collective-permute-done.8.p2, ...), custom_call_target="tpu_custom_call" | custom-call | flops 2000000000 | bytes 65536 | tf_op jit(solution)/shard_map/window0/pallas_call | solution.py:357
  67.5 2.4 %collective-permute-start.19 = (bf16[2,48,1024]{2,1,0:T(8,128)(2,1)S(1)}, bf16[2,48,1024]{2,1,0:T(8,128)(2,1)S(1)}, u32[]{:S(2)}, u32[]{:S(2)}) collective-permute-start(bf16[2,48,1024]{2,1,0:T(8,128)(2,1)S(1)} %get-tuple-element.72.w0), channel_id=1, source_target_pairs={{0,4},{1,5},{2,6},{3,7},{4,0},{5,1},{6,2},{7,3},{8,12},{9,13},{10,... | collective-permute-start | bytes 589832 | tf_op jit(solution)/shard_map/ppermute | solution.py:284
  71.4 4.4 %collective-permute-done.15.r_ref = bf16[2,48,1024]{2,1,0:T(8,128)(2,1)S(1)} collective-permute-done((bf16[2,48,1024]{2,1,0:T(8,128)(2,1)S(1)}, bf16[2,48,1024]{2,1,0:T(8,128)(2,1)S(1)}, u32[]{:S(2)}, u32[]{:S(2)}) %collective-permute-start.15) | collective-permute-done | bytes 196640 | tf_op jit(solution)/shard_map/ppermute | solution.py:284
  75.8 1.6 %window1.1 = (bf16[2,48,1024]{2,1,0:T(8,128)(2,1)S(1)}, bf16[3,128,1024]{2,1,0:T(8,128)(2,1)S(1)}) custom-call(bf16[2,48,1024]{2,1,0:T(8,128)(2,1)S(1)} %get-tuple-element.65.p0, bf16[2,48,1024]{2,1,0:T(8,128)(2,1)S(1)} %collective-permute-done.12.p1, bf16[2,48,1024]{2,1,0:T(8,128)(2,1)S(1)} %collective-permute-done.13.p2, ...), custom_call_target="tpu_custom_call" | custom-call | flops 2000000000 | bytes 65536 | tf_op jit(solution)/shard_map/window1/pallas_call | solution.py:357
  82.1 2.2 %collective-permute-start.17 = (bf16[2,48,1024]{2,1,0:T(8,128)(2,1)S(1)}, bf16[2,48,1024]{2,1,0:T(8,128)(2,1)S(1)}, u32[]{:S(2)}, u32[]{:S(2)}) collective-permute-start(bf16[2,48,1024]{2,1,0:T(8,128)(2,1)S(1)} %get-tuple-element.71.w0), channel_id=1, source_target_pairs={{0,4},{1,5},{2,6},{3,7},{4,0},{5,1},{6,2},{7,3},{8,12},{9,13},{10,... | collective-permute-start | bytes 589832 | tf_op jit(solution)/shard_map/ppermute | solution.py:284
  84.3 3.3 %corr.2 = (bf16[4,48,256]{2,1,0:T(8,128)(2,1)S(1)}, bf16[4,48,256]{2,1,0:T(8,128)(2,1)S(1)}, bf16[4,48,256]{2,1,0:T(8,128)(2,1)S(1)}, bf16[4,48,256]{2,1,0:T(8,128)(2,1)S(1)}) custom-call(bf16[2,48,1024]{2,1,0:T(8,128)(2,1)S(1)} %get-tuple-element.72.w0, bf16[2,48,1024]{2,1,0:T(8,128)(2,1)S(1)} %collective-permute-done.18.w1, ...), custom_call_target="tpu_custom_call" | custom-call | flops 4000000000 | bytes 65536 | tf_op jit(solution)/shard_map/corr/pallas_call | solution.py:250
  87.6 2.7 %collective-permute-start.27 = (bf16[4,48,256]{2,1,0:T(8,128)(2,1)S(1)}, bf16[4,48,256]{2,1,0:T(8,128)(2,1)S(1)}, u32[]{:S(2)}, u32[]{:S(2)}) collective-permute-start(bf16[4,48,256]{2,1,0:T(8,128)(2,1)S(1)} %get-tuple-element.76), channel_id=1, source_target_pairs={{0,128},{16,144},{32,160},{48,176},{64,192},{80,208},{96,224},{112... | collective-permute-start | bytes 294920 | tf_op jit(solution)/shard_map/ppermute | solution.py:284
  91.4 2.4 %collective-permute-done.27.refs_2_ = bf16[4,48,256]{2,1,0:T(8,128)(2,1)S(1)} collective-permute-done((bf16[4,48,256]{2,1,0:T(8,128)(2,1)S(1)}, bf16[4,48,256]{2,1,0:T(8,128)(2,1)S(1)}, u32[]{:S(2)}, u32[]{:S(2)}) %collective-permute-start.27) | collective-permute-done | bytes 98336 | tf_op jit(solution)/shard_map/ppermute | solution.py:284
  95.2 1.9 %collective-permute-start.28 = (bf16[4,48,256]{2,1,0:T(8,128)(2,1)S(1)}, bf16[4,48,256]{2,1,0:T(8,128)(2,1)S(1)}, u32[]{:S(2)}, u32[]{:S(2)}) collective-permute-start(bf16[4,48,256]{2,1,0:T(8,128)(2,1)S(1)} %get-tuple-element.78), channel_id=1, source_target_pairs={{0,192},{16,208},{32,224},{48,240},{64,0},{80,16},{96,32},{112,48}... | collective-permute-start | bytes 294920 | tf_op jit(solution)/shard_map/ppermute | solution.py:284
  97.1 3.3 %corr.3 = (bf16[4,48,256]{2,1,0:T(8,128)(2,1)S(1)}, bf16[4,48,256]{2,1,0:T(8,128)(2,1)S(1)}, bf16[4,48,256]{2,1,0:T(8,128)(2,1)S(1)}, bf16[4,48,256]{2,1,0:T(8,128)(2,1)S(1)}) custom-call(bf16[2,48,1024]{2,1,0:T(8,128)(2,1)S(1)} %get-tuple-element.71.w0, bf16[2,48,1024]{2,1,0:T(8,128)(2,1)S(1)} %collective-permute-done.16.w1, ...), custom_call_target="tpu_custom_call" | custom-call | flops 4000000000 | bytes 65536 | tf_op jit(solution)/shard_map/corr/pallas_call | solution.py:250
  100.7 2.4 %collective-permute-start.34 = (bf16[4,48,256]{2,1,0:T(8,128)(2,1)S(1)}, bf16[4,48,256]{2,1,0:T(8,128)(2,1)S(1)}, u32[]{:S(2)}, u32[]{:S(2)}) collective-permute-start(bf16[4,48,256]{2,1,0:T(8,128)(2,1)S(1)} %get-tuple-element.84), channel_id=1, source_target_pairs={{0,128},{16,144},{32,160},{48,176},{64,192},{80,208},{96,224},{112... | collective-permute-start | bytes 294920 | tf_op jit(solution)/shard_map/ppermute | solution.py:284
  104.6 3.9 %collective-permute-done.33.refs_5_ = bf16[4,48,256]{2,1,0:T(8,128)(2,1)S(1)} collective-permute-done((bf16[4,48,256]{2,1,0:T(8,128)(2,1)S(1)}, bf16[4,48,256]{2,1,0:T(8,128)(2,1)S(1)}, u32[]{:S(2)}, u32[]{:S(2)}) %collective-permute-start.33) | collective-permute-done | bytes 98336 | tf_op jit(solution)/shard_map/ppermute | solution.py:284
  109.4 2.4 %collective-permute-start.37 = (bf16[2,48,256]{2,1,0:T(8,128)(2,1)S(1)}, bf16[2,48,256]{2,1,0:T(8,128)(2,1)S(1)}, u32[]{:S(2)}, u32[]{:S(2)}) collective-permute-start(bf16[2,48,256]{2,1,0:T(8,128)(2,1)S(1)} %get-tuple-element.88), channel_id=1, source_target_pairs={{0,32},{16,48},{32,0},{48,16},{64,96},{80,112},{96,64},{112,80},{1... | collective-permute-start | bytes 147464 | tf_op jit(solution)/shard_map/ppermute | solution.py:284
  111.7 1.9 %collective-permute-start.38 = (bf16[2,48,256]{2,1,0:T(8,128)(2,1)S(1)}, bf16[2,48,256]{2,1,0:T(8,128)(2,1)S(1)}, u32[]{:S(2)}, u32[]{:S(2)}) collective-permute-start(bf16[2,48,256]{2,1,0:T(8,128)(2,1)S(1)} %get-tuple-element.89), channel_id=1, source_target_pairs={{0,48},{16,32},{32,16},{48,0},{64,112},{80,96},{96,80},{112,64},{1... | collective-permute-start | bytes 147464 | tf_op jit(solution)/shard_map/ppermute | solution.py:284
  114.4 3.2 %collective-permute-done.38.g3 = bf16[2,48,256]{2,1,0:T(8,128)(2,1)S(1)} collective-permute-done((bf16[2,48,256]{2,1,0:T(8,128)(2,1)S(1)}, bf16[2,48,256]{2,1,0:T(8,128)(2,1)S(1)}, u32[]{:S(2)}, u32[]{:S(2)}) %collective-permute-start.38) | collective-permute-done | bytes 49184 | tf_op jit(solution)/shard_map/ppermute | solution.py:284
  (75 shorter events, 26.4 us)
Async XLA Ops:
  2.1 8.8 %collective-permute-start = (bf16[96,256]{1,0:T(8,128)(2,1)S(1)}, bf16[96,256]{1,0:T(8,128)(2,1)S(1)}, u32[]{:S(2)}, u32[]{:S(2)}) collective-permute-start(bf16[96,256]{1,0:T(8,128)(2,1)S(1)} %spectra.1), channel_id=1, source_target_pairs={{0,16},{16,0},{32,48},{48,32},{64,80},{80,64},{96,112},{112,96},{1... | collective-permute-start | bytes 147464 | tf_op jit(solution)/shard_map/ppermute | solution.py:284
  4.1 6.8 %collective-permute-start.1 = (bf16[96,256]{1,0:T(8,128)(2,1)S(1)}, bf16[96,256]{1,0:T(8,128)(2,1)S(1)}, u32[]{:S(2)}, u32[]{:S(2)}) collective-permute-start(bf16[96,256]{1,0:T(8,128)(2,1)S(1)} %spectra.1), channel_id=1, source_target_pairs={{0,32},{16,48},{32,0},{48,16},{64,96},{80,112},{96,64},{112,80},{1... | collective-permute-start | bytes 147464 | tf_op jit(solution)/shard_map/ppermute | solution.py:284
  7.3 5.9 %collective-permute-start.2 = (bf16[96,256]{1,0:T(8,128)(2,1)S(1)}, bf16[96,256]{1,0:T(8,128)(2,1)S(1)}, u32[]{:S(2)}, u32[]{:S(2)}) collective-permute-start(bf16[96,256]{1,0:T(8,128)(2,1)S(1)} %spectra.1), channel_id=1, source_target_pairs={{0,48},{16,32},{32,16},{48,0},{64,112},{80,96},{96,80},{112,64},{1... | collective-permute-start | bytes 147464 | tf_op jit(solution)/shard_map/ppermute | solution.py:284
  13.3 9.1 %collective-permute-start.3 = (bf16[4,96,256]{2,1,0:T(8,128)(2,1)S(1)}, bf16[4,96,256]{2,1,0:T(8,128)(2,1)S(1)}, u32[]{:S(2)}, u32[]{:S(2)}) collective-permute-start(bf16[4,96,256]{2,1,0:T(8,128)(2,1)S(1)} %pad_maximum_fusion.f0), channel_id=1, source_target_pairs={{0,64},{16,80},{32,96},{48,112},{64,128},{80,144},{96,160},{112,17... | collective-permute-start | bytes 589832 | tf_op jit(solution)/shard_map/ppermute | solution.py:284
  14.8 9.8 %collective-permute-start.4 = (bf16[4,96,256]{2,1,0:T(8,128)(2,1)S(1)}, bf16[4,96,256]{2,1,0:T(8,128)(2,1)S(1)}, u32[]{:S(2)}, u32[]{:S(2)}) collective-permute-start(bf16[4,96,256]{2,1,0:T(8,128)(2,1)S(1)} %pad_maximum_fusion.f0), channel_id=1, source_target_pairs={{0,128},{16,144},{32,160},{48,176},{64,192},{80,208},{96,224},{112... | collective-permute-start | bytes 589832 | tf_op jit(solution)/shard_map/ppermute | solution.py:284
  17.6 7.1 %collective-permute-start.5 = (bf16[4,96,256]{2,1,0:T(8,128)(2,1)S(1)}, bf16[4,96,256]{2,1,0:T(8,128)(2,1)S(1)}, u32[]{:S(2)}, u32[]{:S(2)}) collective-permute-start(bf16[4,96,256]{2,1,0:T(8,128)(2,1)S(1)} %pad_maximum_fusion.f0), channel_id=1, source_target_pairs={{0,192},{16,208},{32,224},{48,240},{64,0},{80,16},{96,32},{112,48}... | collective-permute-start | bytes 589832 | tf_op jit(solution)/shard_map/ppermute | solution.py:284
  28.9 5.0 %collective-permute-start.6 = (bf16[4,2,48,1024]{3,2,1,0:T(8,128)(2,1)S(1)}, bf16[4,2,48,1024]{3,2,1,0:T(8,128)(2,1)S(1)}, u32[]{:S(2)}, u32[]{:S(2)}) collective-permute-start(bf16[4,2,48,1024]{3,2,1,0:T(8,128)(2,1)S(1)} %bitcast.76), channel_id=1, source_target_pairs={{0,1},{1,0},{2,3},{3,2},{4,5},{5,4},{6,7},{7,6},{8,9},{9,8},{10,11... | collective-permute-start | bytes 2359304 | tf_op jit(solution)/shard_map/ppermute | solution.py:284
  33.2 6.0 %collective-permute-start.10 = (bf16[4,2,48,1024]{3,2,1,0:T(8,128)(2,1)S(1)}, bf16[4,2,48,1024]{3,2,1,0:T(8,128)(2,1)S(1)}, u32[]{:S(2)}, u32[]{:S(2)}) collective-permute-start(bf16[4,2,48,1024]{3,2,1,0:T(8,128)(2,1)S(1)} %bitcast.75), channel_id=1, source_target_pairs={{0,1},{1,0},{2,3},{3,2},{4,5},{5,4},{6,7},{7,6},{8,9},{9,8},{10,11... | collective-permute-start | bytes 2359304 | tf_op jit(solution)/shard_map/ppermute | solution.py:284
  34.2 7.8 %collective-permute-start.7 = (bf16[2,48,1024]{2,1,0:T(8,128)(2,1)S(1)}, bf16[2,48,1024]{2,1,0:T(8,128)(2,1)S(1)}, u32[]{:S(2)}, u32[]{:S(2)}) collective-permute-start(bf16[2,48,1024]{2,1,0:T(8,128)(2,1)S(1)} %get-tuple-element.106), channel_id=1, source_target_pairs={{0,2},{1,3},{2,4},{3,5},{4,6},{5,7},{6,0},{7,1},{8,10},{9,11},{10,... | collective-permute-start | bytes 589832 | tf_op jit(solution)/shard_map/ppermute | solution.py:284
  35.8 9.3 %collective-permute-start.8 = (bf16[2,48,1024]{2,1,0:T(8,128)(2,1)S(1)}, bf16[2,48,1024]{2,1,0:T(8,128)(2,1)S(1)}, u32[]{:S(2)}, u32[]{:S(2)}) collective-permute-start(bf16[2,48,1024]{2,1,0:T(8,128)(2,1)S(1)} %get-tuple-element.105), channel_id=1, source_target_pairs={{0,4},{1,5},{2,6},{3,7},{4,0},{5,1},{6,2},{7,3},{8,12},{9,13},{10,... | collective-permute-start | bytes 589832 | tf_op jit(solution)/shard_map/ppermute | solution.py:284
  36.8 10.6 %collective-permute-start.9 = (bf16[2,48,1024]{2,1,0:T(8,128)(2,1)S(1)}, bf16[2,48,1024]{2,1,0:T(8,128)(2,1)S(1)}, u32[]{:S(2)}, u32[]{:S(2)}) collective-permute-start(bf16[2,48,1024]{2,1,0:T(8,128)(2,1)S(1)} %get-tuple-element.104), channel_id=1, source_target_pairs={{0,6},{1,7},{2,0},{3,1},{4,2},{5,3},{6,4},{7,5},{8,14},{9,15},{10,... | collective-permute-start | bytes 589832 | tf_op jit(solution)/shard_map/ppermute | solution.py:284
  47.4 9.6 %collective-permute-start.12 = (bf16[2,48,1024]{2,1,0:T(8,128)(2,1)S(1)}, bf16[2,48,1024]{2,1,0:T(8,128)(2,1)S(1)}, u32[]{:S(2)}, u32[]{:S(2)}) collective-permute-start(bf16[2,48,1024]{2,1,0:T(8,128)(2,1)S(1)} %get-tuple-element.59), channel_id=1, source_target_pairs={{0,2},{1,3},{2,4},{3,5},{4,6},{5,7},{6,0},{7,1},{8,10},{9,11},{10,... | collective-permute-start | bytes 589832 | tf_op jit(solution)/shard_map/ppermute | solution.py:284
  48.7 9.1 %collective-permute-start.13 = (bf16[2,48,1024]{2,1,0:T(8,128)(2,1)S(1)}, bf16[2,48,1024]{2,1,0:T(8,128)(2,1)S(1)}, u32[]{:S(2)}, u32[]{:S(2)}) collective-permute-start(bf16[2,48,1024]{2,1,0:T(8,128)(2,1)S(1)} %get-tuple-element.60), channel_id=1, source_target_pairs={{0,4},{1,5},{2,6},{3,7},{4,0},{5,1},{6,2},{7,3},{8,12},{9,13},{10,... | collective-permute-start | bytes 589832 | tf_op jit(solution)/shard_map/ppermute | solution.py:284
  50.3 9.6 %collective-permute-start.14 = (bf16[2,48,1024]{2,1,0:T(8,128)(2,1)S(1)}, bf16[2,48,1024]{2,1,0:T(8,128)(2,1)S(1)}, u32[]{:S(2)}, u32[]{:S(2)}) collective-permute-start(bf16[2,48,1024]{2,1,0:T(8,128)(2,1)S(1)} %get-tuple-element.61), channel_id=1, source_target_pairs={{0,6},{1,7},{2,0},{3,1},{4,2},{5,3},{6,4},{7,5},{8,14},{9,15},{10,... | collective-permute-start | bytes 589832 | tf_op jit(solution)/shard_map/ppermute | solution.py:284
  52.0 13.2 %collective-permute-start.11 = (bf16[2,48,1024]{2,1,0:T(8,128)(2,1)S(1)}, bf16[2,48,1024]{2,1,0:T(8,128)(2,1)S(1)}, u32[]{:S(2)}, u32[]{:S(2)}) collective-permute-start(bf16[2,48,1024]{2,1,0:T(8,128)(2,1)S(1)} %get-tuple-element.90), channel_id=1, source_target_pairs={{0,8},{1,9},{2,10},{3,11},{4,12},{5,13},{6,14},{7,15},{8,0},{9,1},... | collective-permute-start | bytes 589832 | tf_op jit(solution)/shard_map/ppermute | solution.py:284
  60.0 15.8 %collective-permute-start.15 = (bf16[2,48,1024]{2,1,0:T(8,128)(2,1)S(1)}, bf16[2,48,1024]{2,1,0:T(8,128)(2,1)S(1)}, u32[]{:S(2)}, u32[]{:S(2)}) collective-permute-start(bf16[2,48,1024]{2,1,0:T(8,128)(2,1)S(1)} %add_convert_fusion), channel_id=1, source_target_pairs={{0,8},{1,9},{2,10},{3,11},{4,12},{5,13},{6,14},{7,15},{8,0},{9,1},... | collective-permute-start | bytes 589832 | tf_op jit(solution)/shard_map/ppermute | solution.py:284
  66.8 12.2 %collective-permute-start.18 = (bf16[2,48,1024]{2,1,0:T(8,128)(2,1)S(1)}, bf16[2,48,1024]{2,1,0:T(8,128)(2,1)S(1)}, u32[]{:S(2)}, u32[]{:S(2)}) collective-permute-start(bf16[2,48,1024]{2,1,0:T(8,128)(2,1)S(1)} %get-tuple-element.72.w0), channel_id=1, source_target_pairs={{0,2},{1,3},{2,4},{3,5},{4,6},{5,7},{6,0},{7,1},{8,10},{9,11},{10,... | collective-permute-start | bytes 589832 | tf_op jit(solution)/shard_map/ppermute | solution.py:284
  67.5 12.1 %collective-permute-start.19 = (bf16[2,48,1024]{2,1,0:T(8,128)(2,1)S(1)}, bf16[2,48,1024]{2,1,0:T(8,128)(2,1)S(1)}, u32[]{:S(2)}, u32[]{:S(2)}) collective-permute-start(bf16[2,48,1024]{2,1,0:T(8,128)(2,1)S(1)} %get-tuple-element.72.w0), channel_id=1, source_target_pairs={{0,4},{1,5},{2,6},{3,7},{4,0},{5,1},{6,2},{7,3},{8,12},{9,13},{10,... | collective-permute-start | bytes 589832 | tf_op jit(solution)/shard_map/ppermute | solution.py:284
  69.9 9.7 %collective-permute-start.20 = (bf16[2,48,1024]{2,1,0:T(8,128)(2,1)S(1)}, bf16[2,48,1024]{2,1,0:T(8,128)(2,1)S(1)}, u32[]{:S(2)}, u32[]{:S(2)}) collective-permute-start(bf16[2,48,1024]{2,1,0:T(8,128)(2,1)S(1)} %get-tuple-element.72.w0), channel_id=1, source_target_pairs={{0,6},{1,7},{2,0},{3,1},{4,2},{5,3},{6,4},{7,5},{8,14},{9,15},{10,... | collective-permute-start | bytes 589832 | tf_op jit(solution)/shard_map/ppermute | solution.py:284
  80.1 11.4 %collective-permute-start.26 = (bf16[2,48,1024]{2,1,0:T(8,128)(2,1)S(1)}, bf16[2,48,1024]{2,1,0:T(8,128)(2,1)S(1)}, u32[]{:S(2)}, u32[]{:S(2)}) collective-permute-start(bf16[2,48,1024]{2,1,0:T(8,128)(2,1)S(1)} %get-tuple-element.71.w0), channel_id=1, source_target_pairs={{0,6},{1,7},{2,0},{3,1},{4,2},{5,3},{6,4},{7,5},{8,14},{9,15},{10,... | collective-permute-start | bytes 589832 | tf_op jit(solution)/shard_map/ppermute | solution.py:284
  80.5 9.9 %collective-permute-start.16 = (bf16[2,48,1024]{2,1,0:T(8,128)(2,1)S(1)}, bf16[2,48,1024]{2,1,0:T(8,128)(2,1)S(1)}, u32[]{:S(2)}, u32[]{:S(2)}) collective-permute-start(bf16[2,48,1024]{2,1,0:T(8,128)(2,1)S(1)} %get-tuple-element.71.w0), channel_id=1, source_target_pairs={{0,2},{1,3},{2,4},{3,5},{4,6},{5,7},{6,0},{7,1},{8,10},{9,11},{10,... | collective-permute-start | bytes 589832 | tf_op jit(solution)/shard_map/ppermute | solution.py:284
  82.1 8.8 %collective-permute-start.17 = (bf16[2,48,1024]{2,1,0:T(8,128)(2,1)S(1)}, bf16[2,48,1024]{2,1,0:T(8,128)(2,1)S(1)}, u32[]{:S(2)}, u32[]{:S(2)}) collective-permute-start(bf16[2,48,1024]{2,1,0:T(8,128)(2,1)S(1)} %get-tuple-element.71.w0), channel_id=1, source_target_pairs={{0,4},{1,5},{2,6},{3,7},{4,0},{5,1},{6,2},{7,3},{8,12},{9,13},{10,... | collective-permute-start | bytes 589832 | tf_op jit(solution)/shard_map/ppermute | solution.py:284
  87.6 6.2 %collective-permute-start.27 = (bf16[4,48,256]{2,1,0:T(8,128)(2,1)S(1)}, bf16[4,48,256]{2,1,0:T(8,128)(2,1)S(1)}, u32[]{:S(2)}, u32[]{:S(2)}) collective-permute-start(bf16[4,48,256]{2,1,0:T(8,128)(2,1)S(1)} %get-tuple-element.76), channel_id=1, source_target_pairs={{0,128},{16,144},{32,160},{48,176},{64,192},{80,208},{96,224},{112... | collective-permute-start | bytes 294920 | tf_op jit(solution)/shard_map/ppermute | solution.py:284
  90.9 6.2 %collective-permute-start.30 = (bf16[2,48,1024]{2,1,0:T(8,128)(2,1)S(1)}, bf16[2,48,1024]{2,1,0:T(8,128)(2,1)S(1)}, u32[]{:S(2)}, u32[]{:S(2)}) collective-permute-start(bf16[2,48,1024]{2,1,0:T(8,128)(2,1)S(1)} %collective-permute-done.16.w1), channel_id=1, source_target_pairs={{0,1},{1,0},{2,3},{3,2},{4,5},{5,4},{6,7},{7,6},{8,9},{9,8},{10,11... | collective-permute-start | bytes 589832 | tf_op jit(solution)/shard_map/ppermute | solution.py:284
  90.9 6.2 %collective-permute-start.31 = (bf16[2,48,1024]{2,1,0:T(8,128)(2,1)S(1)}, bf16[2,48,1024]{2,1,0:T(8,128)(2,1)S(1)}, u32[]{:S(2)}, u32[]{:S(2)}) collective-permute-start(bf16[2,48,1024]{2,1,0:T(8,128)(2,1)S(1)} %collective-permute-done.17.w2), channel_id=1, source_target_pairs={{0,1},{1,0},{2,3},{3,2},{4,5},{5,4},{6,7},{7,6},{8,9},{9,8},{10,11... | collective-permute-start | bytes 589832 | tf_op jit(solution)/shard_map/ppermute | solution.py:284
  93.9 10.8 %collective-permute-start.25 = (bf16[4,48,256]{2,1,0:T(8,128)(2,1)S(1)}, bf16[4,48,256]{2,1,0:T(8,128)(2,1)S(1)}, u32[]{:S(2)}, u32[]{:S(2)}) collective-permute-start(bf16[4,48,256]{2,1,0:T(8,128)(2,1)S(1)} %get-tuple-element.75), channel_id=1, source_target_pairs={{0,64},{16,80},{32,96},{48,112},{64,128},{80,144},{96,160},{112,17... | collective-permute-start | bytes 294920 | tf_op jit(solution)/shard_map/ppermute | solution.py:284
  95.2 9.4 %collective-permute-start.28 = (bf16[4,48,256]{2,1,0:T(8,128)(2,1)S(1)}, bf16[4,48,256]{2,1,0:T(8,128)(2,1)S(1)}, u32[]{:S(2)}, u32[]{:S(2)}) collective-permute-start(bf16[4,48,256]{2,1,0:T(8,128)(2,1)S(1)} %get-tuple-element.78), channel_id=1, source_target_pairs={{0,192},{16,208},{32,224},{48,240},{64,0},{80,16},{96,32},{112,48}... | collective-permute-start | bytes 294920 | tf_op jit(solution)/shard_map/ppermute | solution.py:284
  100.4 8.0 %collective-permute-start.33 = (bf16[4,48,256]{2,1,0:T(8,128)(2,1)S(1)}, bf16[4,48,256]{2,1,0:T(8,128)(2,1)S(1)}, u32[]{:S(2)}, u32[]{:S(2)}) collective-permute-start(bf16[4,48,256]{2,1,0:T(8,128)(2,1)S(1)} %get-tuple-element.83), channel_id=1, source_target_pairs={{0,64},{16,80},{32,96},{48,112},{64,128},{80,144},{96,160},{112,17... | collective-permute-start | bytes 294920 | tf_op jit(solution)/shard_map/ppermute | solution.py:284
  100.7 7.8 %collective-permute-start.34 = (bf16[4,48,256]{2,1,0:T(8,128)(2,1)S(1)}, bf16[4,48,256]{2,1,0:T(8,128)(2,1)S(1)}, u32[]{:S(2)}, u32[]{:S(2)}) collective-permute-start(bf16[4,48,256]{2,1,0:T(8,128)(2,1)S(1)} %get-tuple-element.84), channel_id=1, source_target_pairs={{0,128},{16,144},{32,160},{48,176},{64,192},{80,208},{96,224},{112... | collective-permute-start | bytes 294920 | tf_op jit(solution)/shard_map/ppermute | solution.py:284
  103.0 6.0 %collective-permute-start.35 = (bf16[4,48,256]{2,1,0:T(8,128)(2,1)S(1)}, bf16[4,48,256]{2,1,0:T(8,128)(2,1)S(1)}, u32[]{:S(2)}, u32[]{:S(2)}) collective-permute-start(bf16[4,48,256]{2,1,0:T(8,128)(2,1)S(1)} %get-tuple-element.85), channel_id=1, source_target_pairs={{0,192},{16,208},{32,224},{48,240},{64,0},{80,16},{96,32},{112,48}... | collective-permute-start | bytes 294920 | tf_op jit(solution)/shard_map/ppermute | solution.py:284
  109.4 5.0 %collective-permute-start.37 = (bf16[2,48,256]{2,1,0:T(8,128)(2,1)S(1)}, bf16[2,48,256]{2,1,0:T(8,128)(2,1)S(1)}, u32[]{:S(2)}, u32[]{:S(2)}) collective-permute-start(bf16[2,48,256]{2,1,0:T(8,128)(2,1)S(1)} %get-tuple-element.88), channel_id=1, source_target_pairs={{0,32},{16,48},{32,0},{48,16},{64,96},{80,112},{96,64},{112,80},{1... | collective-permute-start | bytes 147464 | tf_op jit(solution)/shard_map/ppermute | solution.py:284
  111.7 5.9 %collective-permute-start.38 = (bf16[2,48,256]{2,1,0:T(8,128)(2,1)S(1)}, bf16[2,48,256]{2,1,0:T(8,128)(2,1)S(1)}, u32[]{:S(2)}, u32[]{:S(2)}) collective-permute-start(bf16[2,48,256]{2,1,0:T(8,128)(2,1)S(1)} %get-tuple-element.89), channel_id=1, source_target_pairs={{0,48},{16,32},{32,16},{48,0},{64,112},{80,96},{96,80},{112,64},{1... | collective-permute-start | bytes 147464 | tf_op jit(solution)/shard_map/ppermute | solution.py:284
  (12 other events, 178.5 us)

commit v3 on v2

--- a/solution.py
+++ b/solution.py
@@ -145,10 +145,10 @@
             l1[to] = rows
             l2[to] = swap_rows(rows)
 
-    sb = 256
+    sb = 1024
 
     def step(i, carry):
-        g, at = i // 4, pl.ds(pl.multiple_of(lax.rem(i, 4) * sb, sb), sb)
+        g, at = i, slice(None)
         parts = {}
         for k in range(4):
             low, high = window_of(k, 8)
@@ -268,8 +268,9 @@
             give[h] = total[d + 1].astype(BF)
 
 
-def refocus_kernel(g0, g1, g2, g3, d_ref, on_ref, a_ref, o_ref):
+def refocus_kernel(g0, g1, g2, g3, d_ref, on_ref, a_ref, o_hbm, o_ref, sem):
     steps = lax.broadcasted_iota(jnp.int32, (NR, NT), 1)
+    copies = []
     for h in range(CH):
         g = (g0[h] + g1[h].astype(F32)) + (g2[h].astype(F32) + g3[h].astype(F32))
         gt = hi_lo_hi(g.T, 1)
@@ -278,6 +279,10 @@
             field = dot(gt, a_ref[i], 1, 1)
             field = jnp.where(steps < on_ref[:, j : j + 1], field, 0.0)
             o_ref[j] = d_ref[j].astype(F32) + field
+            copies.append(pltpu.make_async_copy(o_ref.at[j], o_hbm.at[j], sem.at[j]))
+            copies[-1].start()
+    for copy in copies:
+        copy.wait()
 
 
 def send(value, axis, to):
@@ -387,7 +392,7 @@
 
     parts_a = over_x(correlate(over_core(own_a), held))
     own_b[1:3], parts_a[:1] = together(own_b[1:3], parts_a[:1])
-    own_b[3:], parts_a[2:3] = together(own_b[3:], parts_a[2:3])
+    own_b[3:], parts_a[1:3] = together(own_b[3:], parts_a[1:3])
     parts = parts_a + over_x(correlate(over_core(own_b), held))
 
     keep, *gives = call(
@@ -396,7 +401,14 @@
         "sum_x",
     )(*parts)
     last = [keep] + [send(gives[d - 1], "src", to_zl(d)) for d in (1, 2, 3)]
-    refocused = call(refocus_kernel, jax.ShapeDtypeStruct((NP, NR, NT), F32), "refocus")(
+    refocused = call(
+        refocus_kernel,
+        jax.ShapeDtypeStruct((NP, NR, NT), F32),
+        "refocus",
+        in_specs=[pl.BlockSpec(memory_space=pltpu.VMEM)] * 7,
+        out_specs=pl.BlockSpec(memory_space=pltpu.HBM),
+        scratch_shapes=[pltpu.VMEM((NP, NR, NT), F32), pltpu.SemaphoreType.DMA((NP,))],
+    )(
         *last, direct, onset_receiver.T, t_samp
     )
     return (upgoing, refocused)

time: 120 us -> 117 us (0.975)
  Pallas kernels: 26.4 us -> 24 us
  waiting for transfers between devices: 34.8 us -> 36 us
    pallas_call x2, Pallas kernels: 8.36 us -> 6.05 us  [convolve(): call(functools.partial(conv_kernel, chunk), [jax.ShapeDtypeStruct((8, 2,...]
    ppermute x39, waiting for transfers between devices: 34.8 us -> 36 us  [send(): return lax.ppermute(value, axis, [(i, to(i)) for i in range(16)])]
  transfers between devices with their start and end apart: 39 -> 39, of which waited for: 16 -> 17; matrix products, arithmetic and copies ran while one was open for 1% -> 1% of each run, Pallas kernels for 16% -> 15%
where the time goes in v3:
time: 117 us
  starting transfers between devices  54.8 us (47%)
  waiting for transfers between devices  36 us (31%)
  Pallas kernels  24 us (21%)
    ppermute x39, starting transfers between devices, send(): return lax.ppermute(value, axis, [(i, to(i)) for i in range(16)])  54.8 us
    ppermute x39, waiting for transfers between devices, send(): return lax.ppermute(value, axis, [(i, to(i)) for i in range(16)])  36 us
    pallas_call x2, Pallas kernels, correlate(): call(corr_kernel, [jax.ShapeDtypeStruct((4, ROWS, NR), BF)] * 4, 'corr',...  6.64 us
    pallas_call x2, Pallas kernels, convolve(): call(functools.partial(conv_kernel, chunk), [jax.ShapeDtypeStruct((8, 2,...  6.05 us
    pallas_call x1, Pallas kernels, on_device(): call(load_kernel, pltpu.VMEM((2, NF, NS, NR), BF), 'load', in_specs=[pl.B...  3.51 us
    pallas_call x2, Pallas kernels, window(): call(functools.partial(window_kernel, h), (jax.ShapeDtypeStruct((2, ROWS,...  3.27 us
  transfers between devices with their start and end apart: 39, of which 17 were waited for; matrix products, arithmetic and copies ran while one was open for 1% of the time, Pallas kernels for 15%

profile of v3, /device:TPU:8, one launch (start us, length us, event | category | flops | bytes accessed | tf_op | source)
XLA Modules:
  0.0 117.0 jit_solution(17968391245984033814)
XLA Ops:
  2.1 2.0 %collective-permute-start = (bf16[96,256]{1,0:T(8,128)(2,1)S(1)}, bf16[96,256]{1,0:T(8,128)(2,1)S(1)}, u32[]{:S(2)}, u32[]{:S(2)}) collective-permute-start(bf16[96,256]{1,0:T(8,128)(2,1)S(1)} %spectra.1), channel_id=1, source_target_pairs={{0,16},{16,0},{32,48},{48,32},{64,80},{80,64},{96,112},{112,96},{1... | collective-permute-start | bytes 147464 | tf_op jit(solution)/shard_map/ppermute | solution.py:289
  4.1 3.3 %collective-permute-start.1 = (bf16[96,256]{1,0:T(8,128)(2,1)S(1)}, bf16[96,256]{1,0:T(8,128)(2,1)S(1)}, u32[]{:S(2)}, u32[]{:S(2)}) collective-permute-start(bf16[96,256]{1,0:T(8,128)(2,1)S(1)} %spectra.1), channel_id=1, source_target_pairs={{0,32},{16,48},{32,0},{48,16},{64,96},{80,112},{96,64},{112,80},{1... | collective-permute-start | bytes 147464 | tf_op jit(solution)/shard_map/ppermute | solution.py:289
  7.3 3.5 %load.1.r_ref = bf16[2,8,1024,256]{3,2,1,0:T(8,128)(2,1)S(1)} custom-call(bf16[2,8,1024,256]{3,2,1,0:T(8,128)(2,1)} %r_hbm.1), custom_call_target="tpu_custom_call" | custom-call | flops 3000000000 | bytes 65536 | tf_op jit(solution)/shard_map/load/pallas_call | solution.py:337
  10.9 2.3 %collective-permute-done.2 = bf16[96,256]{1,0:T(8,128)(2,1)S(1)} collective-permute-done((bf16[96,256]{1,0:T(8,128)(2,1)S(1)}, bf16[96,256]{1,0:T(8,128)(2,1)S(1)}, u32[]{:S(2)}, u32[]{:S(2)}) %collective-permute-start.2) | collective-permute-done | bytes 49184 | tf_op jit(solution)/shard_map/ppermute | solution.py:289
  14.8 2.7 %collective-permute-start.4 = (bf16[4,96,256]{2,1,0:T(8,128)(2,1)S(1)}, bf16[4,96,256]{2,1,0:T(8,128)(2,1)S(1)}, u32[]{:S(2)}, u32[]{:S(2)}) collective-permute-start(bf16[4,96,256]{2,1,0:T(8,128)(2,1)S(1)} %pad_maximum_fusion.f0), channel_id=1, source_target_pairs={{0,128},{16,144},{32,160},{48,176},{64,192},{80,208},{96,224},{112... | collective-permute-start | bytes 589832 | tf_op jit(solution)/shard_map/ppermute | solution.py:289
  19.0 3.3 %collective-permute-done.3.f1 = bf16[4,96,256]{2,1,0:T(8,128)(2,1)S(1)} collective-permute-done((bf16[4,96,256]{2,1,0:T(8,128)(2,1)S(1)}, bf16[4,96,256]{2,1,0:T(8,128)(2,1)S(1)}, u32[]{:S(2)}, u32[]{:S(2)}) %collective-permute-start.3) | collective-permute-done | bytes 196640 | tf_op jit(solution)/shard_map/ppermute | solution.py:289
  22.3 2.4 %collective-permute-done.4.f2 = bf16[4,96,256]{2,1,0:T(8,128)(2,1)S(1)} collective-permute-done((bf16[4,96,256]{2,1,0:T(8,128)(2,1)S(1)}, bf16[4,96,256]{2,1,0:T(8,128)(2,1)S(1)}, u32[]{:S(2)}, u32[]{:S(2)}) %collective-permute-start.4) | collective-permute-done | bytes 196640 | tf_op jit(solution)/shard_map/ppermute | solution.py:289
  24.7 3.0 %conv0.1 = (bf16[8,2,24,1024]{3,2,1,0:T(8,128)(2,1)S(1)}, bf16[8,2,24,1024]{3,2,1,0:T(8,128)(2,1)S(1)}) custom-call(bf16[4,96,256]{2,1,0:T(8,128)(2,1)S(1)} %pad_maximum_fusion.f0, bf16[4,96,256]{2,1,0:T(8,128)(2,1)S(1)} %collective-permute-done.3.f1, bf16[4,96,256]{2,1,0:T(8,128)(2,1)S(1)} %collective-permute-done.4.f2, ...), custom_call_target="tpu_custom_call" | custom-call | flops 4000000000 | bytes 65536 | tf_op jit(solution)/shard_map/conv0/pallas_call | solution.py:170
  27.8 3.0 %conv1.1 = (bf16[8,2,24,1024]{3,2,1,0:T(8,128)(2,1)S(1)}, bf16[8,2,24,1024]{3,2,1,0:T(8,128)(2,1)S(1)}) custom-call(bf16[4,96,256]{2,1,0:T(8,128)(2,1)S(1)} %pad_maximum_fusion.f0, bf16[4,96,256]{2,1,0:T(8,128)(2,1)S(1)} %collective-permute-done.3.f1, bf16[4,96,256]{2,1,0:T(8,128)(2,1)S(1)} %collective-permute-done.4.f2, ...), custom_call_target="tpu_custom_call" | custom-call | flops 4000000000 | bytes 65536 | tf_op jit(solution)/shard_map/conv1/pallas_call | solution.py:170
  31.9 1.7 %collective-permute-start.7 = (bf16[2,48,1024]{2,1,0:T(8,128)(2,1)S(1)}, bf16[2,48,1024]{2,1,0:T(8,128)(2,1)S(1)}, u32[]{:S(2)}, u32[]{:S(2)}) collective-permute-start(bf16[2,48,1024]{2,1,0:T(8,128)(2,1)S(1)} %get-tuple-element.108), channel_id=1, source_target_pairs={{0,2},{1,3},{2,4},{3,5},{4,6},{5,7},{6,0},{7,1},{8,10},{9,11},{10,... | collective-permute-start | bytes 589832 | tf_op jit(solution)/shard_map/ppermute | solution.py:289
  34.5 2.4 %collective-permute-start.9 = (bf16[2,48,1024]{2,1,0:T(8,128)(2,1)S(1)}, bf16[2,48,1024]{2,1,0:T(8,128)(2,1)S(1)}, u32[]{:S(2)}, u32[]{:S(2)}) collective-permute-start(bf16[2,48,1024]{2,1,0:T(8,128)(2,1)S(1)} %get-tuple-element.106), channel_id=1, source_target_pairs={{0,6},{1,7},{2,0},{3,1},{4,2},{5,3},{6,4},{7,5},{8,14},{9,15},{10,... | collective-permute-start | bytes 589832 | tf_op jit(solution)/shard_map/ppermute | solution.py:289
  37.2 2.5 %collective-permute-done.7.p1 = bf16[2,48,1024]{2,1,0:T(8,128)(2,1)S(1)} collective-permute-done((bf16[2,48,1024]{2,1,0:T(8,128)(2,1)S(1)}, bf16[2,48,1024]{2,1,0:T(8,128)(2,1)S(1)}, u32[]{:S(2)}, u32[]{:S(2)}) %collective-permute-start.7) | collective-permute-done | bytes 196640 | tf_op jit(solution)/shard_map/ppermute | solution.py:289
  39.7 3.1 %collective-permute-done.8.p2 = bf16[2,48,1024]{2,1,0:T(8,128)(2,1)S(1)} collective-permute-done((bf16[2,48,1024]{2,1,0:T(8,128)(2,1)S(1)}, bf16[2,48,1024]{2,1,0:T(8,128)(2,1)S(1)}, u32[]{:S(2)}, u32[]{:S(2)}) %collective-permute-start.8) | collective-permute-done | bytes 196640 | tf_op jit(solution)/shard_map/ppermute | solution.py:289
  42.8 2.3 %collective-permute-done.9.p3 = bf16[2,48,1024]{2,1,0:T(8,128)(2,1)S(1)} collective-permute-done((bf16[2,48,1024]{2,1,0:T(8,128)(2,1)S(1)}, bf16[2,48,1024]{2,1,0:T(8,128)(2,1)S(1)}, u32[]{:S(2)}, u32[]{:S(2)}) %collective-permute-start.9) | collective-permute-done | bytes 196640 | tf_op jit(solution)/shard_map/ppermute | solution.py:289
  49.7 5.0 %collective-permute-start.11 = (bf16[2,48,1024]{2,1,0:T(8,128)(2,1)S(1)}, bf16[2,48,1024]{2,1,0:T(8,128)(2,1)S(1)}, u32[]{:S(2)}, u32[]{:S(2)}) collective-permute-start(bf16[2,48,1024]{2,1,0:T(8,128)(2,1)S(1)} %get-tuple-element.92), channel_id=1, source_target_pairs={{0,8},{1,9},{2,10},{3,11},{4,12},{5,13},{6,14},{7,15},{8,0},{9,1},... | collective-permute-start | bytes 589832 | tf_op jit(solution)/shard_map/ppermute | solution.py:289
  55.5 2.0 %collective-permute-done.14.p3 = bf16[2,48,1024]{2,1,0:T(8,128)(2,1)S(1)} collective-permute-done((bf16[2,48,1024]{2,1,0:T(8,128)(2,1)S(1)}, bf16[2,48,1024]{2,1,0:T(8,128)(2,1)S(1)}, u32[]{:S(2)}, u32[]{:S(2)}) %collective-permute-start.14) | collective-permute-done | bytes 196640 | tf_op jit(solution)/shard_map/ppermute | solution.py:289
  57.6 5.0 %collective-permute-start.15 = (bf16[2,48,1024]{2,1,0:T(8,128)(2,1)S(1)}, bf16[2,48,1024]{2,1,0:T(8,128)(2,1)S(1)}, u32[]{:S(2)}, u32[]{:S(2)}) collective-permute-start(bf16[2,48,1024]{2,1,0:T(8,128)(2,1)S(1)} %add_convert_fusion), channel_id=1, source_target_pairs={{0,8},{1,9},{2,10},{3,11},{4,12},{5,13},{6,14},{7,15},{8,0},{9,1},... | collective-permute-start | bytes 589832 | tf_op jit(solution)/shard_map/ppermute | solution.py:289
  62.7 1.6 %window0.1 = (bf16[2,48,1024]{2,1,0:T(8,128)(2,1)S(1)}, bf16[3,128,1024]{2,1,0:T(8,128)(2,1)S(1)}) custom-call(bf16[2,48,1024]{2,1,0:T(8,128)(2,1)S(1)} %get-tuple-element.93.p0, bf16[2,48,1024]{2,1,0:T(8,128)(2,1)S(1)} %collective-permute-done.7.p1, bf16[2,48,1024]{2,1,0:T(8,128)(2,1)S(1)} %collective-permute-done.8.p2, ...), custom_call_target="tpu_custom_call" | custom-call | flops 2000000000 | bytes 65536 | tf_op jit(solution)/shard_map/window0/pallas_call | solution.py:362
  65.0 2.4 %collective-permute-start.19 = (bf16[2,48,1024]{2,1,0:T(8,128)(2,1)S(1)}, bf16[2,48,1024]{2,1,0:T(8,128)(2,1)S(1)}, u32[]{:S(2)}, u32[]{:S(2)}) collective-permute-start(bf16[2,48,1024]{2,1,0:T(8,128)(2,1)S(1)} %get-tuple-element.73.w0), channel_id=1, source_target_pairs={{0,4},{1,5},{2,6},{3,7},{4,0},{5,1},{6,2},{7,3},{8,12},{9,13},{10,... | collective-permute-start | bytes 589832 | tf_op jit(solution)/shard_map/ppermute | solution.py:289
  68.9 4.6 %collective-permute-done.15.r_ref = bf16[2,48,1024]{2,1,0:T(8,128)(2,1)S(1)} collective-permute-done((bf16[2,48,1024]{2,1,0:T(8,128)(2,1)S(1)}, bf16[2,48,1024]{2,1,0:T(8,128)(2,1)S(1)}, u32[]{:S(2)}, u32[]{:S(2)}) %collective-permute-start.15) | collective-permute-done | bytes 196640 | tf_op jit(solution)/shard_map/ppermute | solution.py:289
  73.4 1.6 %window1.1 = (bf16[2,48,1024]{2,1,0:T(8,128)(2,1)S(1)}, bf16[3,128,1024]{2,1,0:T(8,128)(2,1)S(1)}) custom-call(bf16[2,48,1024]{2,1,0:T(8,128)(2,1)S(1)} %get-tuple-element.66.p0, bf16[2,48,1024]{2,1,0:T(8,128)(2,1)S(1)} %collective-permute-done.12.p1, bf16[2,48,1024]{2,1,0:T(8,128)(2,1)S(1)} %collective-permute-done.13.p2, ...), custom_call_target="tpu_custom_call" | custom-call | flops 2000000000 | bytes 65536 | tf_op jit(solution)/shard_map/window1/pallas_call | solution.py:362
  79.8 2.0 %collective-permute-start.17 = (bf16[2,48,1024]{2,1,0:T(8,128)(2,1)S(1)}, bf16[2,48,1024]{2,1,0:T(8,128)(2,1)S(1)}, u32[]{:S(2)}, u32[]{:S(2)}) collective-permute-start(bf16[2,48,1024]{2,1,0:T(8,128)(2,1)S(1)} %get-tuple-element.72.w0), channel_id=1, source_target_pairs={{0,4},{1,5},{2,6},{3,7},{4,0},{5,1},{6,2},{7,3},{8,12},{9,13},{10,... | collective-permute-start | bytes 589832 | tf_op jit(solution)/shard_map/ppermute | solution.py:289
  81.8 3.3 %corr.2 = (bf16[4,48,256]{2,1,0:T(8,128)(2,1)S(1)}, bf16[4,48,256]{2,1,0:T(8,128)(2,1)S(1)}, bf16[4,48,256]{2,1,0:T(8,128)(2,1)S(1)}, bf16[4,48,256]{2,1,0:T(8,128)(2,1)S(1)}) custom-call(bf16[2,48,1024]{2,1,0:T(8,128)(2,1)S(1)} %get-tuple-element.73.w0, bf16[2,48,1024]{2,1,0:T(8,128)(2,1)S(1)} %collective-permute-done.18.w1, ...), custom_call_target="tpu_custom_call" | custom-call | flops 4000000000 | bytes 65536 | tf_op jit(solution)/shard_map/corr/pallas_call | solution.py:250
  86.6 2.4 %collective-permute-start.27 = (bf16[4,48,256]{2,1,0:T(8,128)(2,1)S(1)}, bf16[4,48,256]{2,1,0:T(8,128)(2,1)S(1)}, u32[]{:S(2)}, u32[]{:S(2)}) collective-permute-start(bf16[4,48,256]{2,1,0:T(8,128)(2,1)S(1)} %get-tuple-element.77), channel_id=1, source_target_pairs={{0,128},{16,144},{32,160},{48,176},{64,192},{80,208},{96,224},{112... | collective-permute-start | bytes 294920 | tf_op jit(solution)/shard_map/ppermute | solution.py:289
  89.6 2.5 %collective-permute-done.26.refs_1_ = bf16[4,48,256]{2,1,0:T(8,128)(2,1)S(1)} collective-permute-done((bf16[4,48,256]{2,1,0:T(8,128)(2,1)S(1)}, bf16[4,48,256]{2,1,0:T(8,128)(2,1)S(1)}, u32[]{:S(2)}, u32[]{:S(2)}) %collective-permute-start.26) | collective-permute-done | bytes 98336 | tf_op jit(solution)/shard_map/ppermute | solution.py:289
  94.8 3.3 %corr.3 = (bf16[4,48,256]{2,1,0:T(8,128)(2,1)S(1)}, bf16[4,48,256]{2,1,0:T(8,128)(2,1)S(1)}, bf16[4,48,256]{2,1,0:T(8,128)(2,1)S(1)}, bf16[4,48,256]{2,1,0:T(8,128)(2,1)S(1)}) custom-call(bf16[2,48,1024]{2,1,0:T(8,128)(2,1)S(1)} %get-tuple-element.72.w0, bf16[2,48,1024]{2,1,0:T(8,128)(2,1)S(1)} %collective-permute-done.16.w1, ...), custom_call_target="tpu_custom_call" | custom-call | flops 4000000000 | bytes 65536 | tf_op jit(solution)/shard_map/corr/pallas_call | solution.py:250
  98.9 2.0 %collective-permute-start.34 = (bf16[4,48,256]{2,1,0:T(8,128)(2,1)S(1)}, bf16[4,48,256]{2,1,0:T(8,128)(2,1)S(1)}, u32[]{:S(2)}, u32[]{:S(2)}) collective-permute-start(bf16[4,48,256]{2,1,0:T(8,128)(2,1)S(1)} %get-tuple-element.86), channel_id=1, source_target_pairs={{0,128},{16,144},{32,160},{48,176},{64,192},{80,208},{96,224},{112... | collective-permute-start | bytes 294920 | tf_op jit(solution)/shard_map/ppermute | solution.py:289
  100.9 1.7 %collective-permute-start.35 = (bf16[4,48,256]{2,1,0:T(8,128)(2,1)S(1)}, bf16[4,48,256]{2,1,0:T(8,128)(2,1)S(1)}, u32[]{:S(2)}, u32[]{:S(2)}) collective-permute-start(bf16[4,48,256]{2,1,0:T(8,128)(2,1)S(1)} %get-tuple-element.87), channel_id=1, source_target_pairs={{0,192},{16,208},{32,224},{48,240},{64,0},{80,16},{96,32},{112,48}... | collective-permute-start | bytes 294920 | tf_op jit(solution)/shard_map/ppermute | solution.py:289
  102.6 3.8 %collective-permute-done.33.refs_5_ = bf16[4,48,256]{2,1,0:T(8,128)(2,1)S(1)} collective-permute-done((bf16[4,48,256]{2,1,0:T(8,128)(2,1)S(1)}, bf16[4,48,256]{2,1,0:T(8,128)(2,1)S(1)}, u32[]{:S(2)}, u32[]{:S(2)}) %collective-permute-start.33) | collective-permute-done | bytes 98336 | tf_op jit(solution)/shard_map/ppermute | solution.py:289
  107.3 2.3 %collective-permute-start.37 = (bf16[2,48,256]{2,1,0:T(8,128)(2,1)S(1)}, bf16[2,48,256]{2,1,0:T(8,128)(2,1)S(1)}, u32[]{:S(2)}, u32[]{:S(2)}) collective-permute-start(bf16[2,48,256]{2,1,0:T(8,128)(2,1)S(1)} %get-tuple-element.90), channel_id=1, source_target_pairs={{0,32},{16,48},{32,0},{48,16},{64,96},{80,112},{96,64},{112,80},{1... | collective-permute-start | bytes 147464 | tf_op jit(solution)/shard_map/ppermute | solution.py:289
  109.6 1.9 %collective-permute-start.38 = (bf16[2,48,256]{2,1,0:T(8,128)(2,1)S(1)}, bf16[2,48,256]{2,1,0:T(8,128)(2,1)S(1)}, u32[]{:S(2)}, u32[]{:S(2)}) collective-permute-start(bf16[2,48,256]{2,1,0:T(8,128)(2,1)S(1)} %get-tuple-element.91), channel_id=1, source_target_pairs={{0,48},{16,32},{32,16},{48,0},{64,112},{80,96},{96,80},{112,64},{1... | collective-permute-start | bytes 147464 | tf_op jit(solution)/shard_map/ppermute | solution.py:289
  112.3 3.2 %collective-permute-done.38.g3 = bf16[2,48,256]{2,1,0:T(8,128)(2,1)S(1)} collective-permute-done((bf16[2,48,256]{2,1,0:T(8,128)(2,1)S(1)}, bf16[2,48,256]{2,1,0:T(8,128)(2,1)S(1)}, u32[]{:S(2)}, u32[]{:S(2)}) %collective-permute-start.38) | collective-permute-done | bytes 49184 | tf_op jit(solution)/shard_map/ppermute | solution.py:289
  (75 shorter events, 27.6 us)
Async XLA Ops:
  2.1 8.8 %collective-permute-start = (bf16[96,256]{1,0:T(8,128)(2,1)S(1)}, bf16[96,256]{1,0:T(8,128)(2,1)S(1)}, u32[]{:S(2)}, u32[]{:S(2)}) collective-permute-start(bf16[96,256]{1,0:T(8,128)(2,1)S(1)} %spectra.1), channel_id=1, source_target_pairs={{0,16},{16,0},{32,48},{48,32},{64,80},{80,64},{96,112},{112,96},{1... | collective-permute-start | bytes 147464 | tf_op jit(solution)/shard_map/ppermute | solution.py:289
  4.1 6.8 %collective-permute-start.1 = (bf16[96,256]{1,0:T(8,128)(2,1)S(1)}, bf16[96,256]{1,0:T(8,128)(2,1)S(1)}, u32[]{:S(2)}, u32[]{:S(2)}) collective-permute-start(bf16[96,256]{1,0:T(8,128)(2,1)S(1)} %spectra.1), channel_id=1, source_target_pairs={{0,32},{16,48},{32,0},{48,16},{64,96},{80,112},{96,64},{112,80},{1... | collective-permute-start | bytes 147464 | tf_op jit(solution)/shard_map/ppermute | solution.py:289
  7.3 5.9 %collective-permute-start.2 = (bf16[96,256]{1,0:T(8,128)(2,1)S(1)}, bf16[96,256]{1,0:T(8,128)(2,1)S(1)}, u32[]{:S(2)}, u32[]{:S(2)}) collective-permute-start(bf16[96,256]{1,0:T(8,128)(2,1)S(1)} %spectra.1), channel_id=1, source_target_pairs={{0,48},{16,32},{32,16},{48,0},{64,112},{80,96},{96,80},{112,64},{1... | collective-permute-start | bytes 147464 | tf_op jit(solution)/shard_map/ppermute | solution.py:289
  13.3 9.1 %collective-permute-start.3 = (bf16[4,96,256]{2,1,0:T(8,128)(2,1)S(1)}, bf16[4,96,256]{2,1,0:T(8,128)(2,1)S(1)}, u32[]{:S(2)}, u32[]{:S(2)}) collective-permute-start(bf16[4,96,256]{2,1,0:T(8,128)(2,1)S(1)} %pad_maximum_fusion.f0), channel_id=1, source_target_pairs={{0,64},{16,80},{32,96},{48,112},{64,128},{80,144},{96,160},{112,17... | collective-permute-start | bytes 589832 | tf_op jit(solution)/shard_map/ppermute | solution.py:289
  14.8 9.8 %collective-permute-start.4 = (bf16[4,96,256]{2,1,0:T(8,128)(2,1)S(1)}, bf16[4,96,256]{2,1,0:T(8,128)(2,1)S(1)}, u32[]{:S(2)}, u32[]{:S(2)}) collective-permute-start(bf16[4,96,256]{2,1,0:T(8,128)(2,1)S(1)} %pad_maximum_fusion.f0), channel_id=1, source_target_pairs={{0,128},{16,144},{32,160},{48,176},{64,192},{80,208},{96,224},{112... | collective-permute-start | bytes 589832 | tf_op jit(solution)/shard_map/ppermute | solution.py:289
  17.6 7.1 %collective-permute-start.5 = (bf16[4,96,256]{2,1,0:T(8,128)(2,1)S(1)}, bf16[4,96,256]{2,1,0:T(8,128)(2,1)S(1)}, u32[]{:S(2)}, u32[]{:S(2)}) collective-permute-start(bf16[4,96,256]{2,1,0:T(8,128)(2,1)S(1)} %pad_maximum_fusion.f0), channel_id=1, source_target_pairs={{0,192},{16,208},{32,224},{48,240},{64,0},{80,16},{96,32},{112,48}... | collective-permute-start | bytes 589832 | tf_op jit(solution)/shard_map/ppermute | solution.py:289
  30.9 6.0 %collective-permute-start.10 = (bf16[4,2,48,1024]{3,2,1,0:T(8,128)(2,1)S(1)}, bf16[4,2,48,1024]{3,2,1,0:T(8,128)(2,1)S(1)}, u32[]{:S(2)}, u32[]{:S(2)}) collective-permute-start(bf16[4,2,48,1024]{3,2,1,0:T(8,128)(2,1)S(1)} %bitcast.75), channel_id=1, source_target_pairs={{0,1},{1,0},{2,3},{3,2},{4,5},{5,4},{6,7},{7,6},{8,9},{9,8},{10,11... | collective-permute-start | bytes 2359304 | tf_op jit(solution)/shard_map/ppermute | solution.py:289
  31.9 7.8 %collective-permute-start.7 = (bf16[2,48,1024]{2,1,0:T(8,128)(2,1)S(1)}, bf16[2,48,1024]{2,1,0:T(8,128)(2,1)S(1)}, u32[]{:S(2)}, u32[]{:S(2)}) collective-permute-start(bf16[2,48,1024]{2,1,0:T(8,128)(2,1)S(1)} %get-tuple-element.108), channel_id=1, source_target_pairs={{0,2},{1,3},{2,4},{3,5},{4,6},{5,7},{6,0},{7,1},{8,10},{9,11},{10,... | collective-permute-start | bytes 589832 | tf_op jit(solution)/shard_map/ppermute | solution.py:289
  33.5 9.3 %collective-permute-start.8 = (bf16[2,48,1024]{2,1,0:T(8,128)(2,1)S(1)}, bf16[2,48,1024]{2,1,0:T(8,128)(2,1)S(1)}, u32[]{:S(2)}, u32[]{:S(2)}) collective-permute-start(bf16[2,48,1024]{2,1,0:T(8,128)(2,1)S(1)} %get-tuple-element.107), channel_id=1, source_target_pairs={{0,4},{1,5},{2,6},{3,7},{4,0},{5,1},{6,2},{7,3},{8,12},{9,13},{10,... | collective-permute-start | bytes 589832 | tf_op jit(solution)/shard_map/ppermute | solution.py:289
  34.5 10.6 %collective-permute-start.9 = (bf16[2,48,1024]{2,1,0:T(8,128)(2,1)S(1)}, bf16[2,48,1024]{2,1,0:T(8,128)(2,1)S(1)}, u32[]{:S(2)}, u32[]{:S(2)}) collective-permute-start(bf16[2,48,1024]{2,1,0:T(8,128)(2,1)S(1)} %get-tuple-element.106), channel_id=1, source_target_pairs={{0,6},{1,7},{2,0},{3,1},{4,2},{5,3},{6,4},{7,5},{8,14},{9,15},{10,... | collective-permute-start | bytes 589832 | tf_op jit(solution)/shard_map/ppermute | solution.py:289
  45.1 9.6 %collective-permute-start.12 = (bf16[2,48,1024]{2,1,0:T(8,128)(2,1)S(1)}, bf16[2,48,1024]{2,1,0:T(8,128)(2,1)S(1)}, u32[]{:S(2)}, u32[]{:S(2)}) collective-permute-start(bf16[2,48,1024]{2,1,0:T(8,128)(2,1)S(1)} %get-tuple-element.60), channel_id=1, source_target_pairs={{0,2},{1,3},{2,4},{3,5},{4,6},{5,7},{6,0},{7,1},{8,10},{9,11},{10,... | collective-permute-start | bytes 589832 | tf_op jit(solution)/shard_map/ppermute | solution.py:289
  46.4 9.1 %collective-permute-start.13 = (bf16[2,48,1024]{2,1,0:T(8,128)(2,1)S(1)}, bf16[2,48,1024]{2,1,0:T(8,128)(2,1)S(1)}, u32[]{:S(2)}, u32[]{:S(2)}) collective-permute-start(bf16[2,48,1024]{2,1,0:T(8,128)(2,1)S(1)} %get-tuple-element.61), channel_id=1, source_target_pairs={{0,4},{1,5},{2,6},{3,7},{4,0},{5,1},{6,2},{7,3},{8,12},{9,13},{10,... | collective-permute-start | bytes 589832 | tf_op jit(solution)/shard_map/ppermute | solution.py:289
  47.9 9.6 %collective-permute-start.14 = (bf16[2,48,1024]{2,1,0:T(8,128)(2,1)S(1)}, bf16[2,48,1024]{2,1,0:T(8,128)(2,1)S(1)}, u32[]{:S(2)}, u32[]{:S(2)}) collective-permute-start(bf16[2,48,1024]{2,1,0:T(8,128)(2,1)S(1)} %get-tuple-element.62), channel_id=1, source_target_pairs={{0,6},{1,7},{2,0},{3,1},{4,2},{5,3},{6,4},{7,5},{8,14},{9,15},{10,... | collective-permute-start | bytes 589832 | tf_op jit(solution)/shard_map/ppermute | solution.py:289
  49.7 13.0 %collective-permute-start.11 = (bf16[2,48,1024]{2,1,0:T(8,128)(2,1)S(1)}, bf16[2,48,1024]{2,1,0:T(8,128)(2,1)S(1)}, u32[]{:S(2)}, u32[]{:S(2)}) collective-permute-start(bf16[2,48,1024]{2,1,0:T(8,128)(2,1)S(1)} %get-tuple-element.92), channel_id=1, source_target_pairs={{0,8},{1,9},{2,10},{3,11},{4,12},{5,13},{6,14},{7,15},{8,0},{9,1},... | collective-permute-start | bytes 589832 | tf_op jit(solution)/shard_map/ppermute | solution.py:289
  57.6 15.8 %collective-permute-start.15 = (bf16[2,48,1024]{2,1,0:T(8,128)(2,1)S(1)}, bf16[2,48,1024]{2,1,0:T(8,128)(2,1)S(1)}, u32[]{:S(2)}, u32[]{:S(2)}) collective-permute-start(bf16[2,48,1024]{2,1,0:T(8,128)(2,1)S(1)} %add_convert_fusion), channel_id=1, source_target_pairs={{0,8},{1,9},{2,10},{3,11},{4,12},{5,13},{6,14},{7,15},{8,0},{9,1},... | collective-permute-start | bytes 589832 | tf_op jit(solution)/shard_map/ppermute | solution.py:289
  64.3 12.4 %collective-permute-start.18 = (bf16[2,48,1024]{2,1,0:T(8,128)(2,1)S(1)}, bf16[2,48,1024]{2,1,0:T(8,128)(2,1)S(1)}, u32[]{:S(2)}, u32[]{:S(2)}) collective-permute-start(bf16[2,48,1024]{2,1,0:T(8,128)(2,1)S(1)} %get-tuple-element.73.w0), channel_id=1, source_target_pairs={{0,2},{1,3},{2,4},{3,5},{4,6},{5,7},{6,0},{7,1},{8,10},{9,11},{10,... | collective-permute-start | bytes 589832 | tf_op jit(solution)/shard_map/ppermute | solution.py:289
  65.0 12.2 %collective-permute-start.19 = (bf16[2,48,1024]{2,1,0:T(8,128)(2,1)S(1)}, bf16[2,48,1024]{2,1,0:T(8,128)(2,1)S(1)}, u32[]{:S(2)}, u32[]{:S(2)}) collective-permute-start(bf16[2,48,1024]{2,1,0:T(8,128)(2,1)S(1)} %get-tuple-element.73.w0), channel_id=1, source_target_pairs={{0,4},{1,5},{2,6},{3,7},{4,0},{5,1},{6,2},{7,3},{8,12},{9,13},{10,... | collective-permute-start | bytes 589832 | tf_op jit(solution)/shard_map/ppermute | solution.py:289
  67.4 9.9 %collective-permute-start.20 = (bf16[2,48,1024]{2,1,0:T(8,128)(2,1)S(1)}, bf16[2,48,1024]{2,1,0:T(8,128)(2,1)S(1)}, u32[]{:S(2)}, u32[]{:S(2)}) collective-permute-start(bf16[2,48,1024]{2,1,0:T(8,128)(2,1)S(1)} %get-tuple-element.73.w0), channel_id=1, source_target_pairs={{0,6},{1,7},{2,0},{3,1},{4,2},{5,3},{6,4},{7,5},{8,14},{9,15},{10,... | collective-permute-start | bytes 589832 | tf_op jit(solution)/shard_map/ppermute | solution.py:289
  77.7 11.8 %collective-permute-start.25 = (bf16[2,48,1024]{2,1,0:T(8,128)(2,1)S(1)}, bf16[2,48,1024]{2,1,0:T(8,128)(2,1)S(1)}, u32[]{:S(2)}, u32[]{:S(2)}) collective-permute-start(bf16[2,48,1024]{2,1,0:T(8,128)(2,1)S(1)} %get-tuple-element.72.w0), channel_id=1, source_target_pairs={{0,6},{1,7},{2,0},{3,1},{4,2},{5,3},{6,4},{7,5},{8,14},{9,15},{10,... | collective-permute-start | bytes 589832 | tf_op jit(solution)/shard_map/ppermute | solution.py:289
  78.1 10.8 %collective-permute-start.16 = (bf16[2,48,1024]{2,1,0:T(8,128)(2,1)S(1)}, bf16[2,48,1024]{2,1,0:T(8,128)(2,1)S(1)}, u32[]{:S(2)}, u32[]{:S(2)}) collective-permute-start(bf16[2,48,1024]{2,1,0:T(8,128)(2,1)S(1)} %get-tuple-element.72.w0), channel_id=1, source_target_pairs={{0,2},{1,3},{2,4},{3,5},{4,6},{5,7},{6,0},{7,1},{8,10},{9,11},{10,... | collective-permute-start | bytes 589832 | tf_op jit(solution)/shard_map/ppermute | solution.py:289
  79.8 9.2 %collective-permute-start.17 = (bf16[2,48,1024]{2,1,0:T(8,128)(2,1)S(1)}, bf16[2,48,1024]{2,1,0:T(8,128)(2,1)S(1)}, u32[]{:S(2)}, u32[]{:S(2)}) collective-permute-start(bf16[2,48,1024]{2,1,0:T(8,128)(2,1)S(1)} %get-tuple-element.72.w0), channel_id=1, source_target_pairs={{0,4},{1,5},{2,6},{3,7},{4,0},{5,1},{6,2},{7,3},{8,12},{9,13},{10,... | collective-permute-start | bytes 589832 | tf_op jit(solution)/shard_map/ppermute | solution.py:289
  85.1 7.0 %collective-permute-start.26 = (bf16[4,48,256]{2,1,0:T(8,128)(2,1)S(1)}, bf16[4,48,256]{2,1,0:T(8,128)(2,1)S(1)}, u32[]{:S(2)}, u32[]{:S(2)}) collective-permute-start(bf16[4,48,256]{2,1,0:T(8,128)(2,1)S(1)} %get-tuple-element.76), channel_id=1, source_target_pairs={{0,64},{16,80},{32,96},{48,112},{64,128},{80,144},{96,160},{112,17... | collective-permute-start | bytes 294920 | tf_op jit(solution)/shard_map/ppermute | solution.py:289
  86.6 6.8 %collective-permute-start.27 = (bf16[4,48,256]{2,1,0:T(8,128)(2,1)S(1)}, bf16[4,48,256]{2,1,0:T(8,128)(2,1)S(1)}, u32[]{:S(2)}, u32[]{:S(2)}) collective-permute-start(bf16[4,48,256]{2,1,0:T(8,128)(2,1)S(1)} %get-tuple-element.77), channel_id=1, source_target_pairs={{0,128},{16,144},{32,160},{48,176},{64,192},{80,208},{96,224},{112... | collective-permute-start | bytes 294920 | tf_op jit(solution)/shard_map/ppermute | solution.py:289
  89.0 5.6 %collective-permute-start.29 = (bf16[2,48,1024]{2,1,0:T(8,128)(2,1)S(1)}, bf16[2,48,1024]{2,1,0:T(8,128)(2,1)S(1)}, u32[]{:S(2)}, u32[]{:S(2)}) collective-permute-start(bf16[2,48,1024]{2,1,0:T(8,128)(2,1)S(1)} %get-tuple-element.72.w0), channel_id=1, source_target_pairs={{0,1},{1,0},{2,3},{3,2},{4,5},{5,4},{6,7},{7,6},{8,9},{9,8},{10,11... | collective-permute-start | bytes 589832 | tf_op jit(solution)/shard_map/ppermute | solution.py:289
  89.0 5.6 %collective-permute-start.30 = (bf16[2,48,1024]{2,1,0:T(8,128)(2,1)S(1)}, bf16[2,48,1024]{2,1,0:T(8,128)(2,1)S(1)}, u32[]{:S(2)}, u32[]{:S(2)}) collective-permute-start(bf16[2,48,1024]{2,1,0:T(8,128)(2,1)S(1)} %collective-permute-done.16.w1), channel_id=1, source_target_pairs={{0,1},{1,0},{2,3},{3,2},{4,5},{5,4},{6,7},{7,6},{8,9},{9,8},{10,11... | collective-permute-start | bytes 589832 | tf_op jit(solution)/shard_map/ppermute | solution.py:289
  89.5 5.1 %collective-permute-start.31 = (bf16[2,48,1024]{2,1,0:T(8,128)(2,1)S(1)}, bf16[2,48,1024]{2,1,0:T(8,128)(2,1)S(1)}, u32[]{:S(2)}, u32[]{:S(2)}) collective-permute-start(bf16[2,48,1024]{2,1,0:T(8,128)(2,1)S(1)} %collective-permute-done.17.w2), channel_id=1, source_target_pairs={{0,1},{1,0},{2,3},{3,2},{4,5},{5,4},{6,7},{7,6},{8,9},{9,8},{10,11... | collective-permute-start | bytes 589832 | tf_op jit(solution)/shard_map/ppermute | solution.py:289
  93.4 9.2 %collective-permute-start.28 = (bf16[4,48,256]{2,1,0:T(8,128)(2,1)S(1)}, bf16[4,48,256]{2,1,0:T(8,128)(2,1)S(1)}, u32[]{:S(2)}, u32[]{:S(2)}) collective-permute-start(bf16[4,48,256]{2,1,0:T(8,128)(2,1)S(1)} %get-tuple-element.80), channel_id=1, source_target_pairs={{0,192},{16,208},{32,224},{48,240},{64,0},{80,16},{96,32},{112,48}... | collective-permute-start | bytes 294920 | tf_op jit(solution)/shard_map/ppermute | solution.py:289
  98.2 8.2 %collective-permute-start.33 = (bf16[4,48,256]{2,1,0:T(8,128)(2,1)S(1)}, bf16[4,48,256]{2,1,0:T(8,128)(2,1)S(1)}, u32[]{:S(2)}, u32[]{:S(2)}) collective-permute-start(bf16[4,48,256]{2,1,0:T(8,128)(2,1)S(1)} %get-tuple-element.85), channel_id=1, source_target_pairs={{0,64},{16,80},{32,96},{48,112},{64,128},{80,144},{96,160},{112,17... | collective-permute-start | bytes 294920 | tf_op jit(solution)/shard_map/ppermute | solution.py:289
  98.9 7.5 %collective-permute-start.34 = (bf16[4,48,256]{2,1,0:T(8,128)(2,1)S(1)}, bf16[4,48,256]{2,1,0:T(8,128)(2,1)S(1)}, u32[]{:S(2)}, u32[]{:S(2)}) collective-permute-start(bf16[4,48,256]{2,1,0:T(8,128)(2,1)S(1)} %get-tuple-element.86), channel_id=1, source_target_pairs={{0,128},{16,144},{32,160},{48,176},{64,192},{80,208},{96,224},{112... | collective-permute-start | bytes 294920 | tf_op jit(solution)/shard_map/ppermute | solution.py:289
  100.9 6.1 %collective-permute-start.35 = (bf16[4,48,256]{2,1,0:T(8,128)(2,1)S(1)}, bf16[4,48,256]{2,1,0:T(8,128)(2,1)S(1)}, u32[]{:S(2)}, u32[]{:S(2)}) collective-permute-start(bf16[4,48,256]{2,1,0:T(8,128)(2,1)S(1)} %get-tuple-element.87), channel_id=1, source_target_pairs={{0,192},{16,208},{32,224},{48,240},{64,0},{80,16},{96,32},{112,48}... | collective-permute-start | bytes 294920 | tf_op jit(solution)/shard_map/ppermute | solution.py:289
  107.3 5.0 %collective-permute-start.37 = (bf16[2,48,256]{2,1,0:T(8,128)(2,1)S(1)}, bf16[2,48,256]{2,1,0:T(8,128)(2,1)S(1)}, u32[]{:S(2)}, u32[]{:S(2)}) collective-permute-start(bf16[2,48,256]{2,1,0:T(8,128)(2,1)S(1)} %get-tuple-element.90), channel_id=1, source_target_pairs={{0,32},{16,48},{32,0},{48,16},{64,96},{80,112},{96,64},{112,80},{1... | collective-permute-start | bytes 147464 | tf_op jit(solution)/shard_map/ppermute | solution.py:289
  109.6 5.9 %collective-permute-start.38 = (bf16[2,48,256]{2,1,0:T(8,128)(2,1)S(1)}, bf16[2,48,256]{2,1,0:T(8,128)(2,1)S(1)}, u32[]{:S(2)}, u32[]{:S(2)}) collective-permute-start(bf16[2,48,256]{2,1,0:T(8,128)(2,1)S(1)} %get-tuple-element.91), channel_id=1, source_target_pairs={{0,48},{16,32},{32,16},{48,0},{64,112},{80,96},{96,80},{112,64},{1... | collective-permute-start | bytes 147464 | tf_op jit(solution)/shard_map/ppermute | solution.py:289
  (12 other events, 175.7 us)

commit v4 on v3

--- a/solution.py
+++ b/solution.py
@@ -135,10 +135,10 @@
 
 def conv_kernel(chunk, f0, f1, f2, f3, r_ref, give, keep, l1, l2):
     x, zl, zh, y, c = place()
-    for dx, ref in enumerate((f0, f1, f2, f3)):
+    for dx, ref in ((0, f0), (2, f1), (1, f2), (3, f3)):
         for dz in range(4):
             xb = lax.rem(x + 4 - dx, 4)
-            zb = zl ^ dz
+            zb = zl ^ (3 - dz)
             yb = lax.rem(xb, 2) * 2 + zb // 2
             to = lax.rem(zb + c, 2) * 8 + lax.rem(yb + 4 - y, 4) * 2 + lax.rem(xb // 2 + zh, 2)
             rows = ref[dz, chunk * ROWS : (chunk + 1) * ROWS].astype(F32)
@@ -268,7 +268,7 @@
             give[h] = total[d + 1].astype(BF)
 
 
-def refocus_kernel(g0, g1, g2, g3, d_ref, on_ref, a_ref, o_hbm, o_ref, sem):
+def refocus_kernel(g3, g2, g1, g0, d_ref, on_ref, a_ref, o_hbm, o_ref, sem):
     steps = lax.broadcasted_iota(jnp.int32, (NR, NT), 1)
     copies = []
     for h in range(CH):
@@ -333,7 +333,7 @@
     )(
         focusing, jnp.asarray(trace_table())
     )
-    near = [send(spectra, "src", to_zl(d)) for d in (1, 2, 3)]
+    near = [send(spectra, "src", to_zl(d)) for d in (3, 2, 1)]
     held = call(
         load_kernel,
         pltpu.VMEM((2, NF, NS, NR), BF),
@@ -345,8 +345,8 @@
         mib=50,
     )(reflection)
     near, [spectra, held] = together(near, [spectra, held])
-    stack = jnp.stack([spectra, *near])
-    pieces = [stack] + [send(stack, "src", to_x(d)) for d in (1, 2, 3)]
+    stack = jnp.stack([*near, spectra])
+    pieces = [stack] + [send(stack, "src", to_x(d)) for d in (2, 1, 3)]
 
     def summed(give, keep):
         got = send(give, "rcv", to_core)
@@ -388,11 +388,11 @@
         return [*own, *[send(w, "rcv", to_core) for w in own]]
 
     def over_x(back):
-        return [back[0]] + [send(back[d], "src", to_x(d)) for d in (1, 2, 3)]
+        return [back[0]] + [send(back[d], "src", to_x(d)) for d in (2, 1, 3)]
 
     parts_a = over_x(correlate(over_core(own_a), held))
-    own_b[1:3], parts_a[:1] = together(own_b[1:3], parts_a[:1])
-    own_b[3:], parts_a[1:3] = together(own_b[3:], parts_a[1:3])
+    own_b[1::2], parts_a[:1] = together(own_b[1::2], parts_a[:1])
+    own_b[2:3], parts_a[1:3] = together(own_b[2:3], parts_a[1:3])
     parts = parts_a + over_x(correlate(over_core(own_b), held))
 
     keep, *gives = call(
@@ -400,7 +400,7 @@
         [jax.ShapeDtypeStruct((CH, ROWS, NR), F32)] + [jax.ShapeDtypeStruct((CH, ROWS, NR), BF)] * 3,
         "sum_x",
     )(*parts)
-    last = [keep] + [send(gives[d - 1], "src", to_zl(d)) for d in (1, 2, 3)]
+    last = [send(gives[d - 1], "src", to_zl(d)) for d in (3, 2, 1)]
     refocused = call(
         refocus_kernel,
         jax.ShapeDtypeStruct((NP, NR, NT), F32),
@@ -409,7 +409,7 @@
         out_specs=pl.BlockSpec(memory_space=pltpu.HBM),
         scratch_shapes=[pltpu.VMEM((NP, NR, NT), F32), pltpu.SemaphoreType.DMA((NP,))],
     )(
-        *last, direct, onset_receiver.T, t_samp
+        *last, keep, direct, onset_receiver.T, t_samp
     )
     return (upgoing, refocused)
 

time: 117 us -> 116 us (level); the launches traced: 117 us -> 115 us
  waiting for transfers between devices: 36 us -> 30.8 us
  starting transfers between devices: 54.8 us -> 57.9 us
    ppermute x39, waiting for transfers between devices: 36 us -> 30.8 us  [send(): return lax.ppermute(value, axis, [(i, to(i)) for i in range(16)])]
    ppermute x39, starting transfers between devices: 54.8 us -> 57.9 us  [send(): return lax.ppermute(value, axis, [(i, to(i)) for i in range(16)])]
  transfers between devices with their start and end apart: 39 -> 39, of which waited for: 17 -> 15; matrix products, arithmetic and copies ran while one was open for 1% -> 1% of each run, Pallas kernels for 15% -> 16%
where the time goes in v4:
time: 116 us; the launch traced here: 115 us
  starting transfers between devices  57.9 us (50%)
  waiting for transfers between devices  30.8 us (27%)
  Pallas kernels  24 us (21%)
    ppermute x39, starting transfers between devices, send(): return lax.ppermute(value, axis, [(i, to(i)) for i in range(16)])  57.9 us
    ppermute x39, waiting for transfers between devices, send(): return lax.ppermute(value, axis, [(i, to(i)) for i in range(16)])  30.8 us
    pallas_call x2, Pallas kernels, correlate(): call(corr_kernel, [jax.ShapeDtypeStruct((4, ROWS, NR), BF)] * 4, 'corr',...  6.65 us
    pallas_call x2, Pallas kernels, convolve(): call(functools.partial(conv_kernel, chunk), [jax.ShapeDtypeStruct((8, 2,...  6.05 us
    pallas_call x1, Pallas kernels, on_device(): call(load_kernel, pltpu.VMEM((2, NF, NS, NR), BF), 'load', in_specs=[pl.B...  3.51 us
    pallas_call x2, Pallas kernels, window(): call(functools.partial(window_kernel, h), (jax.ShapeDtypeStruct((2, ROWS,...  3.28 us
  transfers between devices with their start and end apart: 39, of which 15 were waited for; matrix products, arithmetic and copies ran while one was open for 1% of the time, Pallas kernels for 16%

profile of v4, /device:TPU:8, one launch (start us, length us, event | category | flops | bytes accessed | tf_op | source)
XLA Modules:
  0.0 114.8 jit_solution(13184368085919995386)
XLA Ops:
  2.1 4.7 %collective-permute-start = (bf16[96,256]{1,0:T(8,128)(2,1)S(1)}, bf16[96,256]{1,0:T(8,128)(2,1)S(1)}, u32[]{:S(2)}, u32[]{:S(2)}) collective-permute-start(bf16[96,256]{1,0:T(8,128)(2,1)S(1)} %spectra.1), channel_id=1, source_target_pairs={{0,48},{16,32},{32,16},{48,0},{64,112},{80,96},{96,80},{112,64},{1... | collective-permute-start | bytes 147464 | tf_op jit(solution)/shard_map/ppermute | solution.py:289
  7.4 3.5 %load.1.r_ref = bf16[2,8,1024,256]{3,2,1,0:T(8,128)(2,1)S(1)} custom-call(bf16[2,8,1024,256]{3,2,1,0:T(8,128)(2,1)} %r_hbm.1), custom_call_target="tpu_custom_call" | custom-call | flops 3000000000 | bytes 65536 | tf_op jit(solution)/shard_map/load/pallas_call | solution.py:337
  11.8 3.1 %collective-permute-start.3 = (bf16[4,96,256]{2,1,0:T(8,128)(2,1)S(1)}, bf16[4,96,256]{2,1,0:T(8,128)(2,1)S(1)}, u32[]{:S(2)}, u32[]{:S(2)}) collective-permute-start(bf16[4,96,256]{2,1,0:T(8,128)(2,1)S(1)} %pad_maximum_fusion.f0), channel_id=1, source_target_pairs={{0,128},{16,144},{32,160},{48,176},{64,192},{80,208},{96,224},{112... | collective-permute-start | bytes 589832 | tf_op jit(solution)/shard_map/ppermute | solution.py:289
  15.5 2.6 %collective-permute-start.5 = (bf16[4,96,256]{2,1,0:T(8,128)(2,1)S(1)}, bf16[4,96,256]{2,1,0:T(8,128)(2,1)S(1)}, u32[]{:S(2)}, u32[]{:S(2)}) collective-permute-start(bf16[4,96,256]{2,1,0:T(8,128)(2,1)S(1)} %pad_maximum_fusion.f0), channel_id=1, source_target_pairs={{0,192},{16,208},{32,224},{48,240},{64,0},{80,16},{96,32},{112,48}... | collective-permute-start | bytes 589832 | tf_op jit(solution)/shard_map/ppermute | solution.py:289
  18.2 3.1 %collective-permute-done.3.f1 = bf16[4,96,256]{2,1,0:T(8,128)(2,1)S(1)} collective-permute-done((bf16[4,96,256]{2,1,0:T(8,128)(2,1)S(1)}, bf16[4,96,256]{2,1,0:T(8,128)(2,1)S(1)}, u32[]{:S(2)}, u32[]{:S(2)}) %collective-permute-start.3) | collective-permute-done | bytes 196640 | tf_op jit(solution)/shard_map/ppermute | solution.py:289
  21.2 2.3 %collective-permute-done.4.f2 = bf16[4,96,256]{2,1,0:T(8,128)(2,1)S(1)} collective-permute-done((bf16[4,96,256]{2,1,0:T(8,128)(2,1)S(1)}, bf16[4,96,256]{2,1,0:T(8,128)(2,1)S(1)}, u32[]{:S(2)}, u32[]{:S(2)}) %collective-permute-start.4) | collective-permute-done | bytes 196640 | tf_op jit(solution)/shard_map/ppermute | solution.py:289
  23.6 3.0 %conv0.1 = (bf16[8,2,24,1024]{3,2,1,0:T(8,128)(2,1)S(1)}, bf16[8,2,24,1024]{3,2,1,0:T(8,128)(2,1)S(1)}) custom-call(bf16[4,96,256]{2,1,0:T(8,128)(2,1)S(1)} %pad_maximum_fusion.f0, bf16[4,96,256]{2,1,0:T(8,128)(2,1)S(1)} %collective-permute-done.3.f1, bf16[4,96,256]{2,1,0:T(8,128)(2,1)S(1)} %collective-permute-done.4.f2, ...), custom_call_target="tpu_custom_call" | custom-call | flops 4000000000 | bytes 65536 | tf_op jit(solution)/shard_map/conv0/pallas_call | solution.py:170
  26.7 3.0 %conv1.1 = (bf16[8,2,24,1024]{3,2,1,0:T(8,128)(2,1)S(1)}, bf16[8,2,24,1024]{3,2,1,0:T(8,128)(2,1)S(1)}) custom-call(bf16[4,96,256]{2,1,0:T(8,128)(2,1)S(1)} %pad_maximum_fusion.f0, bf16[4,96,256]{2,1,0:T(8,128)(2,1)S(1)} %collective-permute-done.3.f1, bf16[4,96,256]{2,1,0:T(8,128)(2,1)S(1)} %collective-permute-done.4.f2, ...), custom_call_target="tpu_custom_call" | custom-call | flops 4000000000 | bytes 65536 | tf_op jit(solution)/shard_map/conv1/pallas_call | solution.py:170
  30.7 1.6 %collective-permute-start.7 = (bf16[2,48,1024]{2,1,0:T(8,128)(2,1)S(1)}, bf16[2,48,1024]{2,1,0:T(8,128)(2,1)S(1)}, u32[]{:S(2)}, u32[]{:S(2)}) collective-permute-start(bf16[2,48,1024]{2,1,0:T(8,128)(2,1)S(1)} %get-tuple-element.108), channel_id=1, source_target_pairs={{0,2},{1,3},{2,4},{3,5},{4,6},{5,7},{6,0},{7,1},{8,10},{9,11},{10,... | collective-permute-start | bytes 589832 | tf_op jit(solution)/shard_map/ppermute | solution.py:289
  33.4 2.4 %collective-permute-start.9 = (bf16[2,48,1024]{2,1,0:T(8,128)(2,1)S(1)}, bf16[2,48,1024]{2,1,0:T(8,128)(2,1)S(1)}, u32[]{:S(2)}, u32[]{:S(2)}) collective-permute-start(bf16[2,48,1024]{2,1,0:T(8,128)(2,1)S(1)} %get-tuple-element.106), channel_id=1, source_target_pairs={{0,6},{1,7},{2,0},{3,1},{4,2},{5,3},{6,4},{7,5},{8,14},{9,15},{10,... | collective-permute-start | bytes 589832 | tf_op jit(solution)/shard_map/ppermute | solution.py:289
  36.1 2.5 %collective-permute-done.7.p1 = bf16[2,48,1024]{2,1,0:T(8,128)(2,1)S(1)} collective-permute-done((bf16[2,48,1024]{2,1,0:T(8,128)(2,1)S(1)}, bf16[2,48,1024]{2,1,0:T(8,128)(2,1)S(1)}, u32[]{:S(2)}, u32[]{:S(2)}) %collective-permute-start.7) | collective-permute-done | bytes 196640 | tf_op jit(solution)/shard_map/ppermute | solution.py:289
  38.6 3.1 %collective-permute-done.8.p2 = bf16[2,48,1024]{2,1,0:T(8,128)(2,1)S(1)} collective-permute-done((bf16[2,48,1024]{2,1,0:T(8,128)(2,1)S(1)}, bf16[2,48,1024]{2,1,0:T(8,128)(2,1)S(1)}, u32[]{:S(2)}, u32[]{:S(2)}) %collective-permute-start.8) | collective-permute-done | bytes 196640 | tf_op jit(solution)/shard_map/ppermute | solution.py:289
  41.7 2.3 %collective-permute-done.9.p3 = bf16[2,48,1024]{2,1,0:T(8,128)(2,1)S(1)} collective-permute-done((bf16[2,48,1024]{2,1,0:T(8,128)(2,1)S(1)}, bf16[2,48,1024]{2,1,0:T(8,128)(2,1)S(1)}, u32[]{:S(2)}, u32[]{:S(2)}) %collective-permute-start.9) | collective-permute-done | bytes 196640 | tf_op jit(solution)/shard_map/ppermute | solution.py:289
  48.6 6.2 %collective-permute-start.11 = (bf16[2,48,1024]{2,1,0:T(8,128)(2,1)S(1)}, bf16[2,48,1024]{2,1,0:T(8,128)(2,1)S(1)}, u32[]{:S(2)}, u32[]{:S(2)}) collective-permute-start(bf16[2,48,1024]{2,1,0:T(8,128)(2,1)S(1)} %get-tuple-element.92), channel_id=1, source_target_pairs={{0,8},{1,9},{2,10},{3,11},{4,12},{5,13},{6,14},{7,15},{8,0},{9,1},... | collective-permute-start | bytes 589832 | tf_op jit(solution)/shard_map/ppermute | solution.py:289
  54.8 1.6 %collective-permute-done.14.p3 = bf16[2,48,1024]{2,1,0:T(8,128)(2,1)S(1)} collective-permute-done((bf16[2,48,1024]{2,1,0:T(8,128)(2,1)S(1)}, bf16[2,48,1024]{2,1,0:T(8,128)(2,1)S(1)}, u32[]{:S(2)}, u32[]{:S(2)}) %collective-permute-start.14) | collective-permute-done | bytes 196640 | tf_op jit(solution)/shard_map/ppermute | solution.py:289
  56.5 6.2 %collective-permute-start.15 = (bf16[2,48,1024]{2,1,0:T(8,128)(2,1)S(1)}, bf16[2,48,1024]{2,1,0:T(8,128)(2,1)S(1)}, u32[]{:S(2)}, u32[]{:S(2)}) collective-permute-start(bf16[2,48,1024]{2,1,0:T(8,128)(2,1)S(1)} %add_convert_fusion), channel_id=1, source_target_pairs={{0,8},{1,9},{2,10},{3,11},{4,12},{5,13},{6,14},{7,15},{8,0},{9,1},... | collective-permute-start | bytes 589832 | tf_op jit(solution)/shard_map/ppermute | solution.py:289
  62.7 1.6 %window0.1 = (bf16[2,48,1024]{2,1,0:T(8,128)(2,1)S(1)}, bf16[3,128,1024]{2,1,0:T(8,128)(2,1)S(1)}) custom-call(bf16[2,48,1024]{2,1,0:T(8,128)(2,1)S(1)} %get-tuple-element.93.p0, bf16[2,48,1024]{2,1,0:T(8,128)(2,1)S(1)} %collective-permute-done.7.p1, bf16[2,48,1024]{2,1,0:T(8,128)(2,1)S(1)} %collective-permute-done.8.p2, ...), custom_call_target="tpu_custom_call" | custom-call | flops 2000000000 | bytes 65536 | tf_op jit(solution)/shard_map/window0/pallas_call | solution.py:362
  65.7 2.3 %collective-permute-start.19 = (bf16[2,48,1024]{2,1,0:T(8,128)(2,1)S(1)}, bf16[2,48,1024]{2,1,0:T(8,128)(2,1)S(1)}, u32[]{:S(2)}, u32[]{:S(2)}) collective-permute-start(bf16[2,48,1024]{2,1,0:T(8,128)(2,1)S(1)} %get-tuple-element.73.w0), channel_id=1, source_target_pairs={{0,4},{1,5},{2,6},{3,7},{4,0},{5,1},{6,2},{7,3},{8,12},{9,13},{10,... | collective-permute-start | bytes 589832 | tf_op jit(solution)/shard_map/ppermute | solution.py:289
  69.0 4.5 %collective-permute-done.15.r_ref = bf16[2,48,1024]{2,1,0:T(8,128)(2,1)S(1)} collective-permute-done((bf16[2,48,1024]{2,1,0:T(8,128)(2,1)S(1)}, bf16[2,48,1024]{2,1,0:T(8,128)(2,1)S(1)}, u32[]{:S(2)}, u32[]{:S(2)}) %collective-permute-start.15) | collective-permute-done | bytes 196640 | tf_op jit(solution)/shard_map/ppermute | solution.py:289
  73.5 1.6 %window1.1 = (bf16[2,48,1024]{2,1,0:T(8,128)(2,1)S(1)}, bf16[3,128,1024]{2,1,0:T(8,128)(2,1)S(1)}) custom-call(bf16[2,48,1024]{2,1,0:T(8,128)(2,1)S(1)} %get-tuple-element.66.p0, bf16[2,48,1024]{2,1,0:T(8,128)(2,1)S(1)} %collective-permute-done.12.p1, bf16[2,48,1024]{2,1,0:T(8,128)(2,1)S(1)} %collective-permute-done.13.p2, ...), custom_call_target="tpu_custom_call" | custom-call | flops 2000000000 | bytes 65536 | tf_op jit(solution)/shard_map/window1/pallas_call | solution.py:362
  75.1 1.6 %flip.1 = bf16[6,1024,128]{2,1,0:T(8,128)(2,1)} custom-call(bf16[3,128,1024]{2,1,0:T(8,128)(2,1)S(1)} %get-tuple-element.65.a_ref, bf16[3,128,1024]{2,1,0:T(8,128)(2,1)S(1)} %get-tuple-element.70.b_ref), custom_call_target="tpu_custom_call" | custom-call | flops 2000000000 | bytes 65536 | tf_op jit(solution)/shard_map/flip/pallas_call | solution.py:381
  79.0 1.7 %collective-permute-start.17 = (bf16[2,48,1024]{2,1,0:T(8,128)(2,1)S(1)}, bf16[2,48,1024]{2,1,0:T(8,128)(2,1)S(1)}, u32[]{:S(2)}, u32[]{:S(2)}) collective-permute-start(bf16[2,48,1024]{2,1,0:T(8,128)(2,1)S(1)} %get-tuple-element.72.w0), channel_id=1, source_target_pairs={{0,6},{1,7},{2,0},{3,1},{4,2},{5,3},{6,4},{7,5},{8,14},{9,15},{10,... | collective-permute-start | bytes 589832 | tf_op jit(solution)/shard_map/ppermute | solution.py:289
  80.7 3.3 %corr.2 = (bf16[4,48,256]{2,1,0:T(8,128)(2,1)S(1)}, bf16[4,48,256]{2,1,0:T(8,128)(2,1)S(1)}, bf16[4,48,256]{2,1,0:T(8,128)(2,1)S(1)}, bf16[4,48,256]{2,1,0:T(8,128)(2,1)S(1)}) custom-call(bf16[2,48,1024]{2,1,0:T(8,128)(2,1)S(1)} %get-tuple-element.73.w0, bf16[2,48,1024]{2,1,0:T(8,128)(2,1)S(1)} %collective-permute-done.18.w1, ...), custom_call_target="tpu_custom_call" | custom-call | flops 4000000000 | bytes 65536 | tf_op jit(solution)/shard_map/corr/pallas_call | solution.py:250
  84.0 2.2 %collective-permute-start.26 = (bf16[4,48,256]{2,1,0:T(8,128)(2,1)S(1)}, bf16[4,48,256]{2,1,0:T(8,128)(2,1)S(1)}, u32[]{:S(2)}, u32[]{:S(2)}) collective-permute-start(bf16[4,48,256]{2,1,0:T(8,128)(2,1)S(1)} %get-tuple-element.76), channel_id=1, source_target_pairs={{0,128},{16,144},{32,160},{48,176},{64,192},{80,208},{96,224},{112... | collective-permute-start | bytes 294920 | tf_op jit(solution)/shard_map/ppermute | solution.py:289
  92.3 1.6 %collective-permute-start.28 = (bf16[4,48,256]{2,1,0:T(8,128)(2,1)S(1)}, bf16[4,48,256]{2,1,0:T(8,128)(2,1)S(1)}, u32[]{:S(2)}, u32[]{:S(2)}) collective-permute-start(bf16[4,48,256]{2,1,0:T(8,128)(2,1)S(1)} %get-tuple-element.80), channel_id=1, source_target_pairs={{0,192},{16,208},{32,224},{48,240},{64,0},{80,16},{96,32},{112,48}... | collective-permute-start | bytes 294920 | tf_op jit(solution)/shard_map/ppermute | solution.py:289
  94.0 3.3 %corr.3 = (bf16[4,48,256]{2,1,0:T(8,128)(2,1)S(1)}, bf16[4,48,256]{2,1,0:T(8,128)(2,1)S(1)}, bf16[4,48,256]{2,1,0:T(8,128)(2,1)S(1)}, bf16[4,48,256]{2,1,0:T(8,128)(2,1)S(1)}) custom-call(bf16[2,48,1024]{2,1,0:T(8,128)(2,1)S(1)} %get-tuple-element.72.w0, bf16[2,48,1024]{2,1,0:T(8,128)(2,1)S(1)} %collective-permute-done.16.w1, ...), custom_call_target="tpu_custom_call" | custom-call | flops 4000000000 | bytes 65536 | tf_op jit(solution)/shard_map/corr/pallas_call | solution.py:250
  97.3 1.7 %collective-permute-start.33 = (bf16[4,48,256]{2,1,0:T(8,128)(2,1)S(1)}, bf16[4,48,256]{2,1,0:T(8,128)(2,1)S(1)}, u32[]{:S(2)}, u32[]{:S(2)}) collective-permute-start(bf16[4,48,256]{2,1,0:T(8,128)(2,1)S(1)} %get-tuple-element.85), channel_id=1, source_target_pairs={{0,128},{16,144},{32,160},{48,176},{64,192},{80,208},{96,224},{112... | collective-permute-start | bytes 294920 | tf_op jit(solution)/shard_map/ppermute | solution.py:289
  99.6 2.6 %collective-permute-start.35 = (bf16[4,48,256]{2,1,0:T(8,128)(2,1)S(1)}, bf16[4,48,256]{2,1,0:T(8,128)(2,1)S(1)}, u32[]{:S(2)}, u32[]{:S(2)}) collective-permute-start(bf16[4,48,256]{2,1,0:T(8,128)(2,1)S(1)} %get-tuple-element.87), channel_id=1, source_target_pairs={{0,192},{16,208},{32,224},{48,240},{64,0},{80,16},{96,32},{112,48}... | collective-permute-start | bytes 294920 | tf_op jit(solution)/shard_map/ppermute | solution.py:289
  102.3 2.3 %collective-permute-done.33.refs_5_ = bf16[4,48,256]{2,1,0:T(8,128)(2,1)S(1)} collective-permute-done((bf16[4,48,256]{2,1,0:T(8,128)(2,1)S(1)}, bf16[4,48,256]{2,1,0:T(8,128)(2,1)S(1)}, u32[]{:S(2)}, u32[]{:S(2)}) %collective-permute-start.33) | collective-permute-done | bytes 98336 | tf_op jit(solution)/shard_map/ppermute | solution.py:289
  106.0 1.8 %collective-permute-start.36 = (bf16[2,48,256]{2,1,0:T(8,128)(2,1)S(1)}, bf16[2,48,256]{2,1,0:T(8,128)(2,1)S(1)}, u32[]{:S(2)}, u32[]{:S(2)}) collective-permute-start(bf16[2,48,256]{2,1,0:T(8,128)(2,1)S(1)} %get-tuple-element.88), channel_id=1, source_target_pairs={{0,48},{16,32},{32,16},{48,0},{64,112},{80,96},{96,80},{112,64},{1... | collective-permute-start | bytes 147464 | tf_op jit(solution)/shard_map/ppermute | solution.py:289
  107.7 2.7 %collective-permute-start.38 = (bf16[2,48,256]{2,1,0:T(8,128)(2,1)S(1)}, bf16[2,48,256]{2,1,0:T(8,128)(2,1)S(1)}, u32[]{:S(2)}, u32[]{:S(2)}) collective-permute-start(bf16[2,48,256]{2,1,0:T(8,128)(2,1)S(1)} %get-tuple-element.90), channel_id=1, source_target_pairs={{0,16},{16,0},{32,48},{48,32},{64,80},{80,64},{96,112},{112,96},{1... | collective-permute-start | bytes 147464 | tf_op jit(solution)/shard_map/ppermute | solution.py:289
  110.6 1.6 %collective-permute-done.36.g3 = bf16[2,48,256]{2,1,0:T(8,128)(2,1)S(1)} collective-permute-done((bf16[2,48,256]{2,1,0:T(8,128)(2,1)S(1)}, bf16[2,48,256]{2,1,0:T(8,128)(2,1)S(1)}, u32[]{:S(2)}, u32[]{:S(2)}) %collective-permute-start.36) | collective-permute-done | bytes 49184 | tf_op jit(solution)/shard_map/ppermute | solution.py:289
  (75 shorter events, 25.9 us)
Async XLA Ops:
  2.1 8.9 %collective-permute-start = (bf16[96,256]{1,0:T(8,128)(2,1)S(1)}, bf16[96,256]{1,0:T(8,128)(2,1)S(1)}, u32[]{:S(2)}, u32[]{:S(2)}) collective-permute-start(bf16[96,256]{1,0:T(8,128)(2,1)S(1)} %spectra.1), channel_id=1, source_target_pairs={{0,48},{16,32},{32,16},{48,0},{64,112},{80,96},{96,80},{112,64},{1... | collective-permute-start | bytes 147464 | tf_op jit(solution)/shard_map/ppermute | solution.py:289
  6.8 5.0 %collective-permute-start.1 = (bf16[96,256]{1,0:T(8,128)(2,1)S(1)}, bf16[96,256]{1,0:T(8,128)(2,1)S(1)}, u32[]{:S(2)}, u32[]{:S(2)}) collective-permute-start(bf16[96,256]{1,0:T(8,128)(2,1)S(1)} %spectra.1), channel_id=1, source_target_pairs={{0,32},{16,48},{32,0},{48,16},{64,96},{80,112},{96,64},{112,80},{1... | collective-permute-start | bytes 147464 | tf_op jit(solution)/shard_map/ppermute | solution.py:289
  6.8 5.0 %collective-permute-start.2 = (bf16[96,256]{1,0:T(8,128)(2,1)S(1)}, bf16[96,256]{1,0:T(8,128)(2,1)S(1)}, u32[]{:S(2)}, u32[]{:S(2)}) collective-permute-start(bf16[96,256]{1,0:T(8,128)(2,1)S(1)} %spectra.1), channel_id=1, source_target_pairs={{0,16},{16,0},{32,48},{48,32},{64,80},{80,64},{96,112},{112,96},{1... | collective-permute-start | bytes 147464 | tf_op jit(solution)/shard_map/ppermute | solution.py:289
  11.8 9.4 %collective-permute-start.3 = (bf16[4,96,256]{2,1,0:T(8,128)(2,1)S(1)}, bf16[4,96,256]{2,1,0:T(8,128)(2,1)S(1)}, u32[]{:S(2)}, u32[]{:S(2)}) collective-permute-start(bf16[4,96,256]{2,1,0:T(8,128)(2,1)S(1)} %pad_maximum_fusion.f0), channel_id=1, source_target_pairs={{0,128},{16,144},{32,160},{48,176},{64,192},{80,208},{96,224},{112... | collective-permute-start | bytes 589832 | tf_op jit(solution)/shard_map/ppermute | solution.py:289
  14.9 8.7 %collective-permute-start.4 = (bf16[4,96,256]{2,1,0:T(8,128)(2,1)S(1)}, bf16[4,96,256]{2,1,0:T(8,128)(2,1)S(1)}, u32[]{:S(2)}, u32[]{:S(2)}) collective-permute-start(bf16[4,96,256]{2,1,0:T(8,128)(2,1)S(1)} %pad_maximum_fusion.f0), channel_id=1, source_target_pairs={{0,64},{16,80},{32,96},{48,112},{64,128},{80,144},{96,160},{112,17... | collective-permute-start | bytes 589832 | tf_op jit(solution)/shard_map/ppermute | solution.py:289
  15.5 8.1 %collective-permute-start.5 = (bf16[4,96,256]{2,1,0:T(8,128)(2,1)S(1)}, bf16[4,96,256]{2,1,0:T(8,128)(2,1)S(1)}, u32[]{:S(2)}, u32[]{:S(2)}) collective-permute-start(bf16[4,96,256]{2,1,0:T(8,128)(2,1)S(1)} %pad_maximum_fusion.f0), channel_id=1, source_target_pairs={{0,192},{16,208},{32,224},{48,240},{64,0},{80,16},{96,32},{112,48}... | collective-permute-start | bytes 589832 | tf_op jit(solution)/shard_map/ppermute | solution.py:289
  26.6 3.9 %collective-permute-start.6 = (bf16[4,2,48,1024]{3,2,1,0:T(8,128)(2,1)S(1)}, bf16[4,2,48,1024]{3,2,1,0:T(8,128)(2,1)S(1)}, u32[]{:S(2)}, u32[]{:S(2)}) collective-permute-start(bf16[4,2,48,1024]{3,2,1,0:T(8,128)(2,1)S(1)} %bitcast.76), channel_id=1, source_target_pairs={{0,1},{1,0},{2,3},{3,2},{4,5},{5,4},{6,7},{7,6},{8,9},{9,8},{10,11... | collective-permute-start | bytes 2359304 | tf_op jit(solution)/shard_map/ppermute | solution.py:289
  29.8 6.0 %collective-permute-start.10 = (bf16[4,2,48,1024]{3,2,1,0:T(8,128)(2,1)S(1)}, bf16[4,2,48,1024]{3,2,1,0:T(8,128)(2,1)S(1)}, u32[]{:S(2)}, u32[]{:S(2)}) collective-permute-start(bf16[4,2,48,1024]{3,2,1,0:T(8,128)(2,1)S(1)} %bitcast.75), channel_id=1, source_target_pairs={{0,1},{1,0},{2,3},{3,2},{4,5},{5,4},{6,7},{7,6},{8,9},{9,8},{10,11... | collective-permute-start | bytes 2359304 | tf_op jit(solution)/shard_map/ppermute | solution.py:289
  30.7 7.8 %collective-permute-start.7 = (bf16[2,48,1024]{2,1,0:T(8,128)(2,1)S(1)}, bf16[2,48,1024]{2,1,0:T(8,128)(2,1)S(1)}, u32[]{:S(2)}, u32[]{:S(2)}) collective-permute-start(bf16[2,48,1024]{2,1,0:T(8,128)(2,1)S(1)} %get-tuple-element.108), channel_id=1, source_target_pairs={{0,2},{1,3},{2,4},{3,5},{4,6},{5,7},{6,0},{7,1},{8,10},{9,11},{10,... | collective-permute-start | bytes 589832 | tf_op jit(solution)/shard_map/ppermute | solution.py:289
  32.4 9.3 %collective-permute-start.8 = (bf16[2,48,1024]{2,1,0:T(8,128)(2,1)S(1)}, bf16[2,48,1024]{2,1,0:T(8,128)(2,1)S(1)}, u32[]{:S(2)}, u32[]{:S(2)}) collective-permute-start(bf16[2,48,1024]{2,1,0:T(8,128)(2,1)S(1)} %get-tuple-element.107), channel_id=1, source_target_pairs={{0,4},{1,5},{2,6},{3,7},{4,0},{5,1},{6,2},{7,3},{8,12},{9,13},{10,... | collective-permute-start | bytes 589832 | tf_op jit(solution)/shard_map/ppermute | solution.py:289
  33.4 10.6 %collective-permute-start.9 = (bf16[2,48,1024]{2,1,0:T(8,128)(2,1)S(1)}, bf16[2,48,1024]{2,1,0:T(8,128)(2,1)S(1)}, u32[]{:S(2)}, u32[]{:S(2)}) collective-permute-start(bf16[2,48,1024]{2,1,0:T(8,128)(2,1)S(1)} %get-tuple-element.106), channel_id=1, source_target_pairs={{0,6},{1,7},{2,0},{3,1},{4,2},{5,3},{6,4},{7,5},{8,14},{9,15},{10,... | collective-permute-start | bytes 589832 | tf_op jit(solution)/shard_map/ppermute | solution.py:289
  44.0 10.8 %collective-permute-start.12 = (bf16[2,48,1024]{2,1,0:T(8,128)(2,1)S(1)}, bf16[2,48,1024]{2,1,0:T(8,128)(2,1)S(1)}, u32[]{:S(2)}, u32[]{:S(2)}) collective-permute-start(bf16[2,48,1024]{2,1,0:T(8,128)(2,1)S(1)} %get-tuple-element.60), channel_id=1, source_target_pairs={{0,2},{1,3},{2,4},{3,5},{4,6},{5,7},{6,0},{7,1},{8,10},{9,11},{10,... | collective-permute-start | bytes 589832 | tf_op jit(solution)/shard_map/ppermute | solution.py:289
  45.3 9.5 %collective-permute-start.13 = (bf16[2,48,1024]{2,1,0:T(8,128)(2,1)S(1)}, bf16[2,48,1024]{2,1,0:T(8,128)(2,1)S(1)}, u32[]{:S(2)}, u32[]{:S(2)}) collective-permute-start(bf16[2,48,1024]{2,1,0:T(8,128)(2,1)S(1)} %get-tuple-element.61), channel_id=1, source_target_pairs={{0,4},{1,5},{2,6},{3,7},{4,0},{5,1},{6,2},{7,3},{8,12},{9,13},{10,... | collective-permute-start | bytes 589832 | tf_op jit(solution)/shard_map/ppermute | solution.py:289
  46.8 9.6 %collective-permute-start.14 = (bf16[2,48,1024]{2,1,0:T(8,128)(2,1)S(1)}, bf16[2,48,1024]{2,1,0:T(8,128)(2,1)S(1)}, u32[]{:S(2)}, u32[]{:S(2)}) collective-permute-start(bf16[2,48,1024]{2,1,0:T(8,128)(2,1)S(1)} %get-tuple-element.62), channel_id=1, source_target_pairs={{0,6},{1,7},{2,0},{3,1},{4,2},{5,3},{6,4},{7,5},{8,14},{9,15},{10,... | collective-permute-start | bytes 589832 | tf_op jit(solution)/shard_map/ppermute | solution.py:289
  48.6 14.2 %collective-permute-start.11 = (bf16[2,48,1024]{2,1,0:T(8,128)(2,1)S(1)}, bf16[2,48,1024]{2,1,0:T(8,128)(2,1)S(1)}, u32[]{:S(2)}, u32[]{:S(2)}) collective-permute-start(bf16[2,48,1024]{2,1,0:T(8,128)(2,1)S(1)} %get-tuple-element.92), channel_id=1, source_target_pairs={{0,8},{1,9},{2,10},{3,11},{4,12},{5,13},{6,14},{7,15},{8,0},{9,1},... | collective-permute-start | bytes 589832 | tf_op jit(solution)/shard_map/ppermute | solution.py:289
  56.5 17.0 %collective-permute-start.15 = (bf16[2,48,1024]{2,1,0:T(8,128)(2,1)S(1)}, bf16[2,48,1024]{2,1,0:T(8,128)(2,1)S(1)}, u32[]{:S(2)}, u32[]{:S(2)}) collective-permute-start(bf16[2,48,1024]{2,1,0:T(8,128)(2,1)S(1)} %add_convert_fusion), channel_id=1, source_target_pairs={{0,8},{1,9},{2,10},{3,11},{4,12},{5,13},{6,14},{7,15},{8,0},{9,1},... | collective-permute-start | bytes 589832 | tf_op jit(solution)/shard_map/ppermute | solution.py:289
  64.4 12.4 %collective-permute-start.18 = (bf16[2,48,1024]{2,1,0:T(8,128)(2,1)S(1)}, bf16[2,48,1024]{2,1,0:T(8,128)(2,1)S(1)}, u32[]{:S(2)}, u32[]{:S(2)}) collective-permute-start(bf16[2,48,1024]{2,1,0:T(8,128)(2,1)S(1)} %get-tuple-element.73.w0), channel_id=1, source_target_pairs={{0,2},{1,3},{2,4},{3,5},{4,6},{5,7},{6,0},{7,1},{8,10},{9,11},{10,... | collective-permute-start | bytes 589832 | tf_op jit(solution)/shard_map/ppermute | solution.py:289
  65.7 11.6 %collective-permute-start.19 = (bf16[2,48,1024]{2,1,0:T(8,128)(2,1)S(1)}, bf16[2,48,1024]{2,1,0:T(8,128)(2,1)S(1)}, u32[]{:S(2)}, u32[]{:S(2)}) collective-permute-start(bf16[2,48,1024]{2,1,0:T(8,128)(2,1)S(1)} %get-tuple-element.73.w0), channel_id=1, source_target_pairs={{0,4},{1,5},{2,6},{3,7},{4,0},{5,1},{6,2},{7,3},{8,12},{9,13},{10,... | collective-permute-start | bytes 589832 | tf_op jit(solution)/shard_map/ppermute | solution.py:289
  68.0 9.4 %collective-permute-start.20 = (bf16[2,48,1024]{2,1,0:T(8,128)(2,1)S(1)}, bf16[2,48,1024]{2,1,0:T(8,128)(2,1)S(1)}, u32[]{:S(2)}, u32[]{:S(2)}) collective-permute-start(bf16[2,48,1024]{2,1,0:T(8,128)(2,1)S(1)} %get-tuple-element.73.w0), channel_id=1, source_target_pairs={{0,6},{1,7},{2,0},{3,1},{4,2},{5,3},{6,4},{7,5},{8,14},{9,15},{10,... | collective-permute-start | bytes 589832 | tf_op jit(solution)/shard_map/ppermute | solution.py:289
  77.8 12.6 %collective-permute-start.25 = (bf16[2,48,1024]{2,1,0:T(8,128)(2,1)S(1)}, bf16[2,48,1024]{2,1,0:T(8,128)(2,1)S(1)}, u32[]{:S(2)}, u32[]{:S(2)}) collective-permute-start(bf16[2,48,1024]{2,1,0:T(8,128)(2,1)S(1)} %get-tuple-element.72.w0), channel_id=1, source_target_pairs={{0,4},{1,5},{2,6},{3,7},{4,0},{5,1},{6,2},{7,3},{8,12},{9,13},{10,... | collective-permute-start | bytes 589832 | tf_op jit(solution)/shard_map/ppermute | solution.py:289
  78.6 10.2 %collective-permute-start.16 = (bf16[2,48,1024]{2,1,0:T(8,128)(2,1)S(1)}, bf16[2,48,1024]{2,1,0:T(8,128)(2,1)S(1)}, u32[]{:S(2)}, u32[]{:S(2)}) collective-permute-start(bf16[2,48,1024]{2,1,0:T(8,128)(2,1)S(1)} %get-tuple-element.72.w0), channel_id=1, source_target_pairs={{0,2},{1,3},{2,4},{3,5},{4,6},{5,7},{6,0},{7,1},{8,10},{9,11},{10,... | collective-permute-start | bytes 589832 | tf_op jit(solution)/shard_map/ppermute | solution.py:289
  79.0 11.4 %collective-permute-start.17 = (bf16[2,48,1024]{2,1,0:T(8,128)(2,1)S(1)}, bf16[2,48,1024]{2,1,0:T(8,128)(2,1)S(1)}, u32[]{:S(2)}, u32[]{:S(2)}) collective-permute-start(bf16[2,48,1024]{2,1,0:T(8,128)(2,1)S(1)} %get-tuple-element.72.w0), channel_id=1, source_target_pairs={{0,6},{1,7},{2,0},{3,1},{4,2},{5,3},{6,4},{7,5},{8,14},{9,15},{10,... | collective-permute-start | bytes 589832 | tf_op jit(solution)/shard_map/ppermute | solution.py:289
  84.0 6.9 %collective-permute-start.26 = (bf16[4,48,256]{2,1,0:T(8,128)(2,1)S(1)}, bf16[4,48,256]{2,1,0:T(8,128)(2,1)S(1)}, u32[]{:S(2)}, u32[]{:S(2)}) collective-permute-start(bf16[4,48,256]{2,1,0:T(8,128)(2,1)S(1)} %get-tuple-element.76), channel_id=1, source_target_pairs={{0,128},{16,144},{32,160},{48,176},{64,192},{80,208},{96,224},{112... | collective-permute-start | bytes 294920 | tf_op jit(solution)/shard_map/ppermute | solution.py:289
  86.2 6.2 %collective-permute-start.27 = (bf16[4,48,256]{2,1,0:T(8,128)(2,1)S(1)}, bf16[4,48,256]{2,1,0:T(8,128)(2,1)S(1)}, u32[]{:S(2)}, u32[]{:S(2)}) collective-permute-start(bf16[4,48,256]{2,1,0:T(8,128)(2,1)S(1)} %get-tuple-element.77), channel_id=1, source_target_pairs={{0,64},{16,80},{32,96},{48,112},{64,128},{80,144},{96,160},{112,17... | collective-permute-start | bytes 294920 | tf_op jit(solution)/shard_map/ppermute | solution.py:289
  88.8 5.1 %collective-permute-start.29 = (bf16[2,48,1024]{2,1,0:T(8,128)(2,1)S(1)}, bf16[2,48,1024]{2,1,0:T(8,128)(2,1)S(1)}, u32[]{:S(2)}, u32[]{:S(2)}) collective-permute-start(bf16[2,48,1024]{2,1,0:T(8,128)(2,1)S(1)} %get-tuple-element.72.w0), channel_id=1, source_target_pairs={{0,1},{1,0},{2,3},{3,2},{4,5},{5,4},{6,7},{7,6},{8,9},{9,8},{10,11... | collective-permute-start | bytes 589832 | tf_op jit(solution)/shard_map/ppermute | solution.py:289
  92.3 9.9 %collective-permute-start.28 = (bf16[4,48,256]{2,1,0:T(8,128)(2,1)S(1)}, bf16[4,48,256]{2,1,0:T(8,128)(2,1)S(1)}, u32[]{:S(2)}, u32[]{:S(2)}) collective-permute-start(bf16[4,48,256]{2,1,0:T(8,128)(2,1)S(1)} %get-tuple-element.80), channel_id=1, source_target_pairs={{0,192},{16,208},{32,224},{48,240},{64,0},{80,16},{96,32},{112,48}... | collective-permute-start | bytes 294920 | tf_op jit(solution)/shard_map/ppermute | solution.py:289
  97.3 7.2 %collective-permute-start.33 = (bf16[4,48,256]{2,1,0:T(8,128)(2,1)S(1)}, bf16[4,48,256]{2,1,0:T(8,128)(2,1)S(1)}, u32[]{:S(2)}, u32[]{:S(2)}) collective-permute-start(bf16[4,48,256]{2,1,0:T(8,128)(2,1)S(1)} %get-tuple-element.85), channel_id=1, source_target_pairs={{0,128},{16,144},{32,160},{48,176},{64,192},{80,208},{96,224},{112... | collective-permute-start | bytes 294920 | tf_op jit(solution)/shard_map/ppermute | solution.py:289
  99.0 6.8 %collective-permute-start.34 = (bf16[4,48,256]{2,1,0:T(8,128)(2,1)S(1)}, bf16[4,48,256]{2,1,0:T(8,128)(2,1)S(1)}, u32[]{:S(2)}, u32[]{:S(2)}) collective-permute-start(bf16[4,48,256]{2,1,0:T(8,128)(2,1)S(1)} %get-tuple-element.86), channel_id=1, source_target_pairs={{0,64},{16,80},{32,96},{48,112},{64,128},{80,144},{96,160},{112,17... | collective-permute-start | bytes 294920 | tf_op jit(solution)/shard_map/ppermute | solution.py:289
  99.6 6.3 %collective-permute-start.35 = (bf16[4,48,256]{2,1,0:T(8,128)(2,1)S(1)}, bf16[4,48,256]{2,1,0:T(8,128)(2,1)S(1)}, u32[]{:S(2)}, u32[]{:S(2)}) collective-permute-start(bf16[4,48,256]{2,1,0:T(8,128)(2,1)S(1)} %get-tuple-element.87), channel_id=1, source_target_pairs={{0,192},{16,208},{32,224},{48,240},{64,0},{80,16},{96,32},{112,48}... | collective-permute-start | bytes 294920 | tf_op jit(solution)/shard_map/ppermute | solution.py:289
  106.0 6.3 %collective-permute-start.36 = (bf16[2,48,256]{2,1,0:T(8,128)(2,1)S(1)}, bf16[2,48,256]{2,1,0:T(8,128)(2,1)S(1)}, u32[]{:S(2)}, u32[]{:S(2)}) collective-permute-start(bf16[2,48,256]{2,1,0:T(8,128)(2,1)S(1)} %get-tuple-element.88), channel_id=1, source_target_pairs={{0,48},{16,32},{32,16},{48,0},{64,112},{80,96},{96,80},{112,64},{1... | collective-permute-start | bytes 147464 | tf_op jit(solution)/shard_map/ppermute | solution.py:289
  107.7 5.6 %collective-permute-start.37 = (bf16[2,48,256]{2,1,0:T(8,128)(2,1)S(1)}, bf16[2,48,256]{2,1,0:T(8,128)(2,1)S(1)}, u32[]{:S(2)}, u32[]{:S(2)}) collective-permute-start(bf16[2,48,256]{2,1,0:T(8,128)(2,1)S(1)} %get-tuple-element.89), channel_id=1, source_target_pairs={{0,32},{16,48},{32,0},{48,16},{64,96},{80,112},{96,64},{112,80},{1... | collective-permute-start | bytes 147464 | tf_op jit(solution)/shard_map/ppermute | solution.py:289
  107.7 5.6 %collective-permute-start.38 = (bf16[2,48,256]{2,1,0:T(8,128)(2,1)S(1)}, bf16[2,48,256]{2,1,0:T(8,128)(2,1)S(1)}, u32[]{:S(2)}, u32[]{:S(2)}) collective-permute-start(bf16[2,48,256]{2,1,0:T(8,128)(2,1)S(1)} %get-tuple-element.90), channel_id=1, source_target_pairs={{0,16},{16,0},{32,48},{48,32},{64,80},{80,64},{96,112},{112,96},{1... | collective-permute-start | bytes 147464 | tf_op jit(solution)/shard_map/ppermute | solution.py:289
  (12 other events, 174.2 us)

commit v5 on v4

--- a/solution.py
+++ b/solution.py
@@ -237,7 +237,7 @@
 
     lax.fori_loop(0, 2, step, 0)
     for i in range(16):
-        other, d, e = i // 8, i // 2 % 4, i % 2
+        other, d, e = i // 8, (0, 2, 1, 3)[i // 2 % 4], i % 2
         yb = lax.rem(y + 4 - d, 4)
         xb = lax.rem(zh + e, 2) * 2 + yb // 2
         zb = lax.rem(yb, 2) * 2 + lax.rem(c + other, 2)
@@ -353,7 +353,7 @@
         return [(keep[d].astype(F32) + got[d].astype(F32)).astype(BF) for d in range(4)]
 
     def over_y(both):
-        return [both[0]] + [send(both[d], "rcv", to_y(d)) for d in (1, 2, 3)]
+        return [both[0]] + [send(both[d], "rcv", to_y(d)) for d in (2, 1, 3)]
 
     def half_sum(both):
         return ((both[0].astype(F32) + both[1].astype(F32)) + (both[2].astype(F32) + both[3].astype(F32))).astype(BF)
@@ -391,8 +391,8 @@
         return [back[0]] + [send(back[d], "src", to_x(d)) for d in (2, 1, 3)]
 
     parts_a = over_x(correlate(over_core(own_a), held))
-    own_b[1::2], parts_a[:1] = together(own_b[1::2], parts_a[:1])
-    own_b[2:3], parts_a[1:3] = together(own_b[2:3], parts_a[1:3])
+    own_b[2:], parts_a[:1] = together(own_b[2:], parts_a[:1])
+    own_b[1:2], parts_a[2:3] = together(own_b[1:2], parts_a[2:3])
     parts = parts_a + over_x(correlate(over_core(own_b), held))
 
     keep, *gives = call(

time: 116 us -> 115 us (level)
  transfers between devices with their start and end apart: 39 -> 39, of which waited for: 15 -> 16; matrix products, arithmetic and copies ran while one was open for 1% -> 1% of each run, Pallas kernels for 16% -> 16%
where the time goes in v5:
time: 115 us
  starting transfers between devices  57 us (50%)
  waiting for transfers between devices  31.4 us (27%)
  Pallas kernels  24 us (21%)
    ppermute x39, starting transfers between devices, send(): return lax.ppermute(value, axis, [(i, to(i)) for i in range(16)])  57 us
    ppermute x39, waiting for transfers between devices, send(): return lax.ppermute(value, axis, [(i, to(i)) for i in range(16)])  31.4 us
    pallas_call x2, Pallas kernels, correlate(): call(corr_kernel, [jax.ShapeDtypeStruct((4, ROWS, NR), BF)] * 4, 'corr',...  6.65 us
    pallas_call x2, Pallas kernels, convolve(): call(functools.partial(conv_kernel, chunk), [jax.ShapeDtypeStruct((8, 2,...  6.05 us
    pallas_call x1, Pallas kernels, on_device(): call(load_kernel, pltpu.VMEM((2, NF, NS, NR), BF), 'load', in_specs=[pl.B...  3.51 us
    pallas_call x2, Pallas kernels, window(): call(functools.partial(window_kernel, h), (jax.ShapeDtypeStruct((2, ROWS,...  3.28 us
  transfers between devices with their start and end apart: 39, of which 16 were waited for; matrix products, arithmetic and copies ran while one was open for 1% of the time, Pallas kernels for 16%

profile of v5, /device:TPU:8, one launch (start us, length us, event | category | flops | bytes accessed | tf_op | source)
XLA Modules:
  0.0 114.7 jit_solution(1443023819692230793)
XLA Ops:
  2.1 4.7 %collective-permute-start = (bf16[96,256]{1,0:T(8,128)(2,1)S(1)}, bf16[96,256]{1,0:T(8,128)(2,1)S(1)}, u32[]{:S(2)}, u32[]{:S(2)}) collective-permute-start(bf16[96,256]{1,0:T(8,128)(2,1)S(1)} %spectra.1), channel_id=1, source_target_pairs={{0,48},{16,32},{32,16},{48,0},{64,112},{80,96},{96,80},{112,64},{1... | collective-permute-start | bytes 147464 | tf_op jit(solution)/shard_map/ppermute | solution.py:289
  7.4 3.5 %load.1.r_ref = bf16[2,8,1024,256]{3,2,1,0:T(8,128)(2,1)S(1)} custom-call(bf16[2,8,1024,256]{3,2,1,0:T(8,128)(2,1)} %r_hbm.1), custom_call_target="tpu_custom_call" | custom-call | flops 3000000000 | bytes 65536 | tf_op jit(solution)/shard_map/load/pallas_call | solution.py:337
  11.8 3.1 %collective-permute-start.3 = (bf16[4,96,256]{2,1,0:T(8,128)(2,1)S(1)}, bf16[4,96,256]{2,1,0:T(8,128)(2,1)S(1)}, u32[]{:S(2)}, u32[]{:S(2)}) collective-permute-start(bf16[4,96,256]{2,1,0:T(8,128)(2,1)S(1)} %pad_maximum_fusion.f0), channel_id=1, source_target_pairs={{0,128},{16,144},{32,160},{48,176},{64,192},{80,208},{96,224},{112... | collective-permute-start | bytes 589832 | tf_op jit(solution)/shard_map/ppermute | solution.py:289
  15.5 2.6 %collective-permute-start.5 = (bf16[4,96,256]{2,1,0:T(8,128)(2,1)S(1)}, bf16[4,96,256]{2,1,0:T(8,128)(2,1)S(1)}, u32[]{:S(2)}, u32[]{:S(2)}) collective-permute-start(bf16[4,96,256]{2,1,0:T(8,128)(2,1)S(1)} %pad_maximum_fusion.f0), channel_id=1, source_target_pairs={{0,192},{16,208},{32,224},{48,240},{64,0},{80,16},{96,32},{112,48}... | collective-permute-start | bytes 589832 | tf_op jit(solution)/shard_map/ppermute | solution.py:289
  18.2 3.1 %collective-permute-done.3.f1 = bf16[4,96,256]{2,1,0:T(8,128)(2,1)S(1)} collective-permute-done((bf16[4,96,256]{2,1,0:T(8,128)(2,1)S(1)}, bf16[4,96,256]{2,1,0:T(8,128)(2,1)S(1)}, u32[]{:S(2)}, u32[]{:S(2)}) %collective-permute-start.3) | collective-permute-done | bytes 196640 | tf_op jit(solution)/shard_map/ppermute | solution.py:289
  21.2 2.3 %collective-permute-done.4.f2 = bf16[4,96,256]{2,1,0:T(8,128)(2,1)S(1)} collective-permute-done((bf16[4,96,256]{2,1,0:T(8,128)(2,1)S(1)}, bf16[4,96,256]{2,1,0:T(8,128)(2,1)S(1)}, u32[]{:S(2)}, u32[]{:S(2)}) %collective-permute-start.4) | collective-permute-done | bytes 196640 | tf_op jit(solution)/shard_map/ppermute | solution.py:289
  23.6 3.0 %conv0.1 = (bf16[8,2,24,1024]{3,2,1,0:T(8,128)(2,1)S(1)}, bf16[8,2,24,1024]{3,2,1,0:T(8,128)(2,1)S(1)}) custom-call(bf16[4,96,256]{2,1,0:T(8,128)(2,1)S(1)} %pad_maximum_fusion.f0, bf16[4,96,256]{2,1,0:T(8,128)(2,1)S(1)} %collective-permute-done.3.f1, bf16[4,96,256]{2,1,0:T(8,128)(2,1)S(1)} %collective-permute-done.4.f2, ...), custom_call_target="tpu_custom_call" | custom-call | flops 4000000000 | bytes 65536 | tf_op jit(solution)/shard_map/conv0/pallas_call | solution.py:170
  26.7 3.0 %conv1.1 = (bf16[8,2,24,1024]{3,2,1,0:T(8,128)(2,1)S(1)}, bf16[8,2,24,1024]{3,2,1,0:T(8,128)(2,1)S(1)}) custom-call(bf16[4,96,256]{2,1,0:T(8,128)(2,1)S(1)} %pad_maximum_fusion.f0, bf16[4,96,256]{2,1,0:T(8,128)(2,1)S(1)} %collective-permute-done.3.f1, bf16[4,96,256]{2,1,0:T(8,128)(2,1)S(1)} %collective-permute-done.4.f2, ...), custom_call_target="tpu_custom_call" | custom-call | flops 4000000000 | bytes 65536 | tf_op jit(solution)/shard_map/conv1/pallas_call | solution.py:170
  30.7 2.4 %collective-permute-start.7 = (bf16[2,48,1024]{2,1,0:T(8,128)(2,1)S(1)}, bf16[2,48,1024]{2,1,0:T(8,128)(2,1)S(1)}, u32[]{:S(2)}, u32[]{:S(2)}) collective-permute-start(bf16[2,48,1024]{2,1,0:T(8,128)(2,1)S(1)} %get-tuple-element.106), channel_id=1, source_target_pairs={{0,4},{1,5},{2,6},{3,7},{4,0},{5,1},{6,2},{7,3},{8,12},{9,13},{10,... | collective-permute-start | bytes 589832 | tf_op jit(solution)/shard_map/ppermute | solution.py:289
  33.1 2.0 %collective-permute-start.9 = (bf16[2,48,1024]{2,1,0:T(8,128)(2,1)S(1)}, bf16[2,48,1024]{2,1,0:T(8,128)(2,1)S(1)}, u32[]{:S(2)}, u32[]{:S(2)}) collective-permute-start(bf16[2,48,1024]{2,1,0:T(8,128)(2,1)S(1)} %get-tuple-element.104), channel_id=1, source_target_pairs={{0,6},{1,7},{2,0},{3,1},{4,2},{5,3},{6,4},{7,5},{8,14},{9,15},{10,... | collective-permute-start | bytes 589832 | tf_op jit(solution)/shard_map/ppermute | solution.py:289
  35.5 4.6 %collective-permute-done.7.p1 = bf16[2,48,1024]{2,1,0:T(8,128)(2,1)S(1)} collective-permute-done((bf16[2,48,1024]{2,1,0:T(8,128)(2,1)S(1)}, bf16[2,48,1024]{2,1,0:T(8,128)(2,1)S(1)}, u32[]{:S(2)}, u32[]{:S(2)}) %collective-permute-start.7) | collective-permute-done | bytes 196640 | tf_op jit(solution)/shard_map/ppermute | solution.py:289
  40.1 3.4 %collective-permute-done.8.p2 = bf16[2,48,1024]{2,1,0:T(8,128)(2,1)S(1)} collective-permute-done((bf16[2,48,1024]{2,1,0:T(8,128)(2,1)S(1)}, bf16[2,48,1024]{2,1,0:T(8,128)(2,1)S(1)}, u32[]{:S(2)}, u32[]{:S(2)}) %collective-permute-start.8) | collective-permute-done | bytes 196640 | tf_op jit(solution)/shard_map/ppermute | solution.py:289
  43.5 2.1 %collective-permute-start.12 = (bf16[2,48,1024]{2,1,0:T(8,128)(2,1)S(1)}, bf16[2,48,1024]{2,1,0:T(8,128)(2,1)S(1)}, u32[]{:S(2)}, u32[]{:S(2)}) collective-permute-start(bf16[2,48,1024]{2,1,0:T(8,128)(2,1)S(1)} %get-tuple-element.59), channel_id=1, source_target_pairs={{0,4},{1,5},{2,6},{3,7},{4,0},{5,1},{6,2},{7,3},{8,12},{9,13},{10,... | collective-permute-start | bytes 589832 | tf_op jit(solution)/shard_map/ppermute | solution.py:289
  45.7 2.0 %collective-permute-start.14 = (bf16[2,48,1024]{2,1,0:T(8,128)(2,1)S(1)}, bf16[2,48,1024]{2,1,0:T(8,128)(2,1)S(1)}, u32[]{:S(2)}, u32[]{:S(2)}) collective-permute-start(bf16[2,48,1024]{2,1,0:T(8,128)(2,1)S(1)} %get-tuple-element.61), channel_id=1, source_target_pairs={{0,6},{1,7},{2,0},{3,1},{4,2},{5,3},{6,4},{7,5},{8,14},{9,15},{10,... | collective-permute-start | bytes 589832 | tf_op jit(solution)/shard_map/ppermute | solution.py:289
  47.9 6.2 %collective-permute-start.11 = (bf16[2,48,1024]{2,1,0:T(8,128)(2,1)S(1)}, bf16[2,48,1024]{2,1,0:T(8,128)(2,1)S(1)}, u32[]{:S(2)}, u32[]{:S(2)}) collective-permute-start(bf16[2,48,1024]{2,1,0:T(8,128)(2,1)S(1)} %get-tuple-element.90), channel_id=1, source_target_pairs={{0,8},{1,9},{2,10},{3,11},{4,12},{5,13},{6,14},{7,15},{8,0},{9,1},... | collective-permute-start | bytes 589832 | tf_op jit(solution)/shard_map/ppermute | solution.py:289
  56.0 6.2 %collective-permute-start.15 = (bf16[2,48,1024]{2,1,0:T(8,128)(2,1)S(1)}, bf16[2,48,1024]{2,1,0:T(8,128)(2,1)S(1)}, u32[]{:S(2)}, u32[]{:S(2)}) collective-permute-start(bf16[2,48,1024]{2,1,0:T(8,128)(2,1)S(1)} %add_convert_fusion), channel_id=1, source_target_pairs={{0,8},{1,9},{2,10},{3,11},{4,12},{5,13},{6,14},{7,15},{8,0},{9,1},... | collective-permute-start | bytes 589832 | tf_op jit(solution)/shard_map/ppermute | solution.py:289
  62.2 1.6 %window0.1 = (bf16[2,48,1024]{2,1,0:T(8,128)(2,1)S(1)}, bf16[3,128,1024]{2,1,0:T(8,128)(2,1)S(1)}) custom-call(bf16[2,48,1024]{2,1,0:T(8,128)(2,1)S(1)} %get-tuple-element.91.p0, bf16[2,48,1024]{2,1,0:T(8,128)(2,1)S(1)} %collective-permute-done.7.p1, bf16[2,48,1024]{2,1,0:T(8,128)(2,1)S(1)} %collective-permute-done.8.p2, ...), custom_call_target="tpu_custom_call" | custom-call | flops 2000000000 | bytes 65536 | tf_op jit(solution)/shard_map/window0/pallas_call | solution.py:362
  63.9 2.0 %collective-permute-start.18 = (bf16[2,48,1024]{2,1,0:T(8,128)(2,1)S(1)}, bf16[2,48,1024]{2,1,0:T(8,128)(2,1)S(1)}, u32[]{:S(2)}, u32[]{:S(2)}) collective-permute-start(bf16[2,48,1024]{2,1,0:T(8,128)(2,1)S(1)} %get-tuple-element.72.w0), channel_id=1, source_target_pairs={{0,4},{1,5},{2,6},{3,7},{4,0},{5,1},{6,2},{7,3},{8,12},{9,13},{10,... | collective-permute-start | bytes 589832 | tf_op jit(solution)/shard_map/ppermute | solution.py:289
  65.9 2.0 %collective-permute-start.19 = (bf16[2,48,1024]{2,1,0:T(8,128)(2,1)S(1)}, bf16[2,48,1024]{2,1,0:T(8,128)(2,1)S(1)}, u32[]{:S(2)}, u32[]{:S(2)}) collective-permute-start(bf16[2,48,1024]{2,1,0:T(8,128)(2,1)S(1)} %get-tuple-element.72.w0), channel_id=1, source_target_pairs={{0,2},{1,3},{2,4},{3,5},{4,6},{5,7},{6,0},{7,1},{8,10},{9,11},{10,... | collective-permute-start | bytes 589832 | tf_op jit(solution)/shard_map/ppermute | solution.py:289
  67.9 2.9 %collective-permute-done.15.r_ref = bf16[2,48,1024]{2,1,0:T(8,128)(2,1)S(1)} collective-permute-done((bf16[2,48,1024]{2,1,0:T(8,128)(2,1)S(1)}, bf16[2,48,1024]{2,1,0:T(8,128)(2,1)S(1)}, u32[]{:S(2)}, u32[]{:S(2)}) %collective-permute-start.15) | collective-permute-done | bytes 196640 | tf_op jit(solution)/shard_map/ppermute | solution.py:289
  70.8 1.6 %window1.1 = (bf16[2,48,1024]{2,1,0:T(8,128)(2,1)S(1)}, bf16[3,128,1024]{2,1,0:T(8,128)(2,1)S(1)}) custom-call(bf16[2,48,1024]{2,1,0:T(8,128)(2,1)S(1)} %get-tuple-element.65.p0, bf16[2,48,1024]{2,1,0:T(8,128)(2,1)S(1)} %collective-permute-done.12.p1, bf16[2,48,1024]{2,1,0:T(8,128)(2,1)S(1)} %collective-permute-done.13.p2, ...), custom_call_target="tpu_custom_call" | custom-call | flops 2000000000 | bytes 65536 | tf_op jit(solution)/shard_map/window1/pallas_call | solution.py:362
  72.5 1.6 %flip.1 = bf16[6,1024,128]{2,1,0:T(8,128)(2,1)} custom-call(bf16[3,128,1024]{2,1,0:T(8,128)(2,1)S(1)} %get-tuple-element.64.a_ref, bf16[3,128,1024]{2,1,0:T(8,128)(2,1)S(1)} %get-tuple-element.69.b_ref), custom_call_target="tpu_custom_call" | custom-call | flops 2000000000 | bytes 65536 | tf_op jit(solution)/shard_map/flip/pallas_call | solution.py:381
  79.8 3.3 %corr.2 = (bf16[4,48,256]{2,1,0:T(8,128)(2,1)S(1)}, bf16[4,48,256]{2,1,0:T(8,128)(2,1)S(1)}, bf16[4,48,256]{2,1,0:T(8,128)(2,1)S(1)}, bf16[4,48,256]{2,1,0:T(8,128)(2,1)S(1)}) custom-call(bf16[2,48,1024]{2,1,0:T(8,128)(2,1)S(1)} %get-tuple-element.72.w0, bf16[2,48,1024]{2,1,0:T(8,128)(2,1)S(1)} %collective-permute-done.18.w1, ...), custom_call_target="tpu_custom_call" | custom-call | flops 4000000000 | bytes 65536 | tf_op jit(solution)/shard_map/corr/pallas_call | solution.py:250
  84.7 3.7 %collective-permute-done.16.w2 = bf16[2,48,1024]{2,1,0:T(8,128)(2,1)S(1)} collective-permute-done((bf16[2,48,1024]{2,1,0:T(8,128)(2,1)S(1)}, bf16[2,48,1024]{2,1,0:T(8,128)(2,1)S(1)}, u32[]{:S(2)}, u32[]{:S(2)}) %collective-permute-start.16) | collective-permute-done | bytes 196640 | tf_op jit(solution)/shard_map/ppermute | solution.py:289
  89.9 2.1 %collective-permute-start.25 = (bf16[4,48,256]{2,1,0:T(8,128)(2,1)S(1)}, bf16[4,48,256]{2,1,0:T(8,128)(2,1)S(1)}, u32[]{:S(2)}, u32[]{:S(2)}) collective-permute-start(bf16[4,48,256]{2,1,0:T(8,128)(2,1)S(1)} %get-tuple-element.75), channel_id=1, source_target_pairs={{0,128},{16,144},{32,160},{48,176},{64,192},{80,208},{96,224},{112... | collective-permute-start | bytes 294920 | tf_op jit(solution)/shard_map/ppermute | solution.py:289
  92.0 2.1 %collective-permute-start.28 = (bf16[4,48,256]{2,1,0:T(8,128)(2,1)S(1)}, bf16[4,48,256]{2,1,0:T(8,128)(2,1)S(1)}, u32[]{:S(2)}, u32[]{:S(2)}) collective-permute-start(bf16[4,48,256]{2,1,0:T(8,128)(2,1)S(1)} %get-tuple-element.78), channel_id=1, source_target_pairs={{0,192},{16,208},{32,224},{48,240},{64,0},{80,16},{96,32},{112,48}... | collective-permute-start | bytes 294920 | tf_op jit(solution)/shard_map/ppermute | solution.py:289
  94.0 3.3 %corr.3 = (bf16[4,48,256]{2,1,0:T(8,128)(2,1)S(1)}, bf16[4,48,256]{2,1,0:T(8,128)(2,1)S(1)}, bf16[4,48,256]{2,1,0:T(8,128)(2,1)S(1)}, bf16[4,48,256]{2,1,0:T(8,128)(2,1)S(1)}) custom-call(bf16[2,48,1024]{2,1,0:T(8,128)(2,1)S(1)} %get-tuple-element.71.w0, bf16[2,48,1024]{2,1,0:T(8,128)(2,1)S(1)} %collective-permute-done.26.w1, ...), custom_call_target="tpu_custom_call" | custom-call | flops 4000000000 | bytes 65536 | tf_op jit(solution)/shard_map/corr/pallas_call | solution.py:250
  98.9 3.2 %collective-permute-start.35 = (bf16[4,48,256]{2,1,0:T(8,128)(2,1)S(1)}, bf16[4,48,256]{2,1,0:T(8,128)(2,1)S(1)}, u32[]{:S(2)}, u32[]{:S(2)}) collective-permute-start(bf16[4,48,256]{2,1,0:T(8,128)(2,1)S(1)} %get-tuple-element.85), channel_id=1, source_target_pairs={{0,192},{16,208},{32,224},{48,240},{64,0},{80,16},{96,32},{112,48}... | collective-permute-start | bytes 294920 | tf_op jit(solution)/shard_map/ppermute | solution.py:289
  102.2 2.4 %collective-permute-done.33.refs_5_ = bf16[4,48,256]{2,1,0:T(8,128)(2,1)S(1)} collective-permute-done((bf16[4,48,256]{2,1,0:T(8,128)(2,1)S(1)}, bf16[4,48,256]{2,1,0:T(8,128)(2,1)S(1)}, u32[]{:S(2)}, u32[]{:S(2)}) %collective-permute-start.33) | collective-permute-done | bytes 98336 | tf_op jit(solution)/shard_map/ppermute | solution.py:289
  105.8 2.0 %collective-permute-start.36 = (bf16[2,48,256]{2,1,0:T(8,128)(2,1)S(1)}, bf16[2,48,256]{2,1,0:T(8,128)(2,1)S(1)}, u32[]{:S(2)}, u32[]{:S(2)}) collective-permute-start(bf16[2,48,256]{2,1,0:T(8,128)(2,1)S(1)} %get-tuple-element.86), channel_id=1, source_target_pairs={{0,48},{16,32},{32,16},{48,0},{64,112},{80,96},{96,80},{112,64},{1... | collective-permute-start | bytes 147464 | tf_op jit(solution)/shard_map/ppermute | solution.py:289
  107.8 2.5 %collective-permute-start.38 = (bf16[2,48,256]{2,1,0:T(8,128)(2,1)S(1)}, bf16[2,48,256]{2,1,0:T(8,128)(2,1)S(1)}, u32[]{:S(2)}, u32[]{:S(2)}) collective-permute-start(bf16[2,48,256]{2,1,0:T(8,128)(2,1)S(1)} %get-tuple-element.88), channel_id=1, source_target_pairs={{0,16},{16,0},{32,48},{48,32},{64,80},{80,64},{96,112},{112,96},{1... | collective-permute-start | bytes 147464 | tf_op jit(solution)/shard_map/ppermute | solution.py:289
  110.4 1.6 %collective-permute-done.36.g3 = bf16[2,48,256]{2,1,0:T(8,128)(2,1)S(1)} collective-permute-done((bf16[2,48,256]{2,1,0:T(8,128)(2,1)S(1)}, bf16[2,48,256]{2,1,0:T(8,128)(2,1)S(1)}, u32[]{:S(2)}, u32[]{:S(2)}) %collective-permute-start.36) | collective-permute-done | bytes 49184 | tf_op jit(solution)/shard_map/ppermute | solution.py:289
  (75 shorter events, 21.2 us)
Async XLA Ops:
  2.1 8.9 %collective-permute-start = (bf16[96,256]{1,0:T(8,128)(2,1)S(1)}, bf16[96,256]{1,0:T(8,128)(2,1)S(1)}, u32[]{:S(2)}, u32[]{:S(2)}) collective-permute-start(bf16[96,256]{1,0:T(8,128)(2,1)S(1)} %spectra.1), channel_id=1, source_target_pairs={{0,48},{16,32},{32,16},{48,0},{64,112},{80,96},{96,80},{112,64},{1... | collective-permute-start | bytes 147464 | tf_op jit(solution)/shard_map/ppermute | solution.py:289
  6.8 5.0 %collective-permute-start.1 = (bf16[96,256]{1,0:T(8,128)(2,1)S(1)}, bf16[96,256]{1,0:T(8,128)(2,1)S(1)}, u32[]{:S(2)}, u32[]{:S(2)}) collective-permute-start(bf16[96,256]{1,0:T(8,128)(2,1)S(1)} %spectra.1), channel_id=1, source_target_pairs={{0,32},{16,48},{32,0},{48,16},{64,96},{80,112},{96,64},{112,80},{1... | collective-permute-start | bytes 147464 | tf_op jit(solution)/shard_map/ppermute | solution.py:289
  6.8 5.0 %collective-permute-start.2 = (bf16[96,256]{1,0:T(8,128)(2,1)S(1)}, bf16[96,256]{1,0:T(8,128)(2,1)S(1)}, u32[]{:S(2)}, u32[]{:S(2)}) collective-permute-start(bf16[96,256]{1,0:T(8,128)(2,1)S(1)} %spectra.1), channel_id=1, source_target_pairs={{0,16},{16,0},{32,48},{48,32},{64,80},{80,64},{96,112},{112,96},{1... | collective-permute-start | bytes 147464 | tf_op jit(solution)/shard_map/ppermute | solution.py:289
  11.8 9.4 %collective-permute-start.3 = (bf16[4,96,256]{2,1,0:T(8,128)(2,1)S(1)}, bf16[4,96,256]{2,1,0:T(8,128)(2,1)S(1)}, u32[]{:S(2)}, u32[]{:S(2)}) collective-permute-start(bf16[4,96,256]{2,1,0:T(8,128)(2,1)S(1)} %pad_maximum_fusion.f0), channel_id=1, source_target_pairs={{0,128},{16,144},{32,160},{48,176},{64,192},{80,208},{96,224},{112... | collective-permute-start | bytes 589832 | tf_op jit(solution)/shard_map/ppermute | solution.py:289
  14.9 8.7 %collective-permute-start.4 = (bf16[4,96,256]{2,1,0:T(8,128)(2,1)S(1)}, bf16[4,96,256]{2,1,0:T(8,128)(2,1)S(1)}, u32[]{:S(2)}, u32[]{:S(2)}) collective-permute-start(bf16[4,96,256]{2,1,0:T(8,128)(2,1)S(1)} %pad_maximum_fusion.f0), channel_id=1, source_target_pairs={{0,64},{16,80},{32,96},{48,112},{64,128},{80,144},{96,160},{112,17... | collective-permute-start | bytes 589832 | tf_op jit(solution)/shard_map/ppermute | solution.py:289
  15.5 8.1 %collective-permute-start.5 = (bf16[4,96,256]{2,1,0:T(8,128)(2,1)S(1)}, bf16[4,96,256]{2,1,0:T(8,128)(2,1)S(1)}, u32[]{:S(2)}, u32[]{:S(2)}) collective-permute-start(bf16[4,96,256]{2,1,0:T(8,128)(2,1)S(1)} %pad_maximum_fusion.f0), channel_id=1, source_target_pairs={{0,192},{16,208},{32,224},{48,240},{64,0},{80,16},{96,32},{112,48}... | collective-permute-start | bytes 589832 | tf_op jit(solution)/shard_map/ppermute | solution.py:289
  29.8 5.4 %collective-permute-start.10 = (bf16[4,2,48,1024]{3,2,1,0:T(8,128)(2,1)S(1)}, bf16[4,2,48,1024]{3,2,1,0:T(8,128)(2,1)S(1)}, u32[]{:S(2)}, u32[]{:S(2)}) collective-permute-start(bf16[4,2,48,1024]{3,2,1,0:T(8,128)(2,1)S(1)} %bitcast.75), channel_id=1, source_target_pairs={{0,1},{1,0},{2,3},{3,2},{4,5},{5,4},{6,7},{7,6},{8,9},{9,8},{10,11... | collective-permute-start | bytes 2359304 | tf_op jit(solution)/shard_map/ppermute | solution.py:289
  30.7 9.4 %collective-permute-start.7 = (bf16[2,48,1024]{2,1,0:T(8,128)(2,1)S(1)}, bf16[2,48,1024]{2,1,0:T(8,128)(2,1)S(1)}, u32[]{:S(2)}, u32[]{:S(2)}) collective-permute-start(bf16[2,48,1024]{2,1,0:T(8,128)(2,1)S(1)} %get-tuple-element.106), channel_id=1, source_target_pairs={{0,4},{1,5},{2,6},{3,7},{4,0},{5,1},{6,2},{7,3},{8,12},{9,13},{10,... | collective-permute-start | bytes 589832 | tf_op jit(solution)/shard_map/ppermute | solution.py:289
  33.1 10.4 %collective-permute-start.8 = (bf16[2,48,1024]{2,1,0:T(8,128)(2,1)S(1)}, bf16[2,48,1024]{2,1,0:T(8,128)(2,1)S(1)}, u32[]{:S(2)}, u32[]{:S(2)}) collective-permute-start(bf16[2,48,1024]{2,1,0:T(8,128)(2,1)S(1)} %get-tuple-element.105), channel_id=1, source_target_pairs={{0,2},{1,3},{2,4},{3,5},{4,6},{5,7},{6,0},{7,1},{8,10},{9,11},{10,... | collective-permute-start | bytes 589832 | tf_op jit(solution)/shard_map/ppermute | solution.py:289
  33.1 10.4 %collective-permute-start.9 = (bf16[2,48,1024]{2,1,0:T(8,128)(2,1)S(1)}, bf16[2,48,1024]{2,1,0:T(8,128)(2,1)S(1)}, u32[]{:S(2)}, u32[]{:S(2)}) collective-permute-start(bf16[2,48,1024]{2,1,0:T(8,128)(2,1)S(1)} %get-tuple-element.104), channel_id=1, source_target_pairs={{0,6},{1,7},{2,0},{3,1},{4,2},{5,3},{6,4},{7,5},{8,14},{9,15},{10,... | collective-permute-start | bytes 589832 | tf_op jit(solution)/shard_map/ppermute | solution.py:289
  43.5 10.6 %collective-permute-start.12 = (bf16[2,48,1024]{2,1,0:T(8,128)(2,1)S(1)}, bf16[2,48,1024]{2,1,0:T(8,128)(2,1)S(1)}, u32[]{:S(2)}, u32[]{:S(2)}) collective-permute-start(bf16[2,48,1024]{2,1,0:T(8,128)(2,1)S(1)} %get-tuple-element.59), channel_id=1, source_target_pairs={{0,4},{1,5},{2,6},{3,7},{4,0},{5,1},{6,2},{7,3},{8,12},{9,13},{10,... | collective-permute-start | bytes 589832 | tf_op jit(solution)/shard_map/ppermute | solution.py:289
  45.7 8.9 %collective-permute-start.13 = (bf16[2,48,1024]{2,1,0:T(8,128)(2,1)S(1)}, bf16[2,48,1024]{2,1,0:T(8,128)(2,1)S(1)}, u32[]{:S(2)}, u32[]{:S(2)}) collective-permute-start(bf16[2,48,1024]{2,1,0:T(8,128)(2,1)S(1)} %get-tuple-element.60), channel_id=1, source_target_pairs={{0,2},{1,3},{2,4},{3,5},{4,6},{5,7},{6,0},{7,1},{8,10},{9,11},{10,... | collective-permute-start | bytes 589832 | tf_op jit(solution)/shard_map/ppermute | solution.py:289
  45.7 10.2 %collective-permute-start.14 = (bf16[2,48,1024]{2,1,0:T(8,128)(2,1)S(1)}, bf16[2,48,1024]{2,1,0:T(8,128)(2,1)S(1)}, u32[]{:S(2)}, u32[]{:S(2)}) collective-permute-start(bf16[2,48,1024]{2,1,0:T(8,128)(2,1)S(1)} %get-tuple-element.61), channel_id=1, source_target_pairs={{0,6},{1,7},{2,0},{3,1},{4,2},{5,3},{6,4},{7,5},{8,14},{9,15},{10,... | collective-permute-start | bytes 589832 | tf_op jit(solution)/shard_map/ppermute | solution.py:289
  47.9 14.4 %collective-permute-start.11 = (bf16[2,48,1024]{2,1,0:T(8,128)(2,1)S(1)}, bf16[2,48,1024]{2,1,0:T(8,128)(2,1)S(1)}, u32[]{:S(2)}, u32[]{:S(2)}) collective-permute-start(bf16[2,48,1024]{2,1,0:T(8,128)(2,1)S(1)} %get-tuple-element.90), channel_id=1, source_target_pairs={{0,8},{1,9},{2,10},{3,11},{4,12},{5,13},{6,14},{7,15},{8,0},{9,1},... | collective-permute-start | bytes 589832 | tf_op jit(solution)/shard_map/ppermute | solution.py:289
  56.0 14.8 %collective-permute-start.15 = (bf16[2,48,1024]{2,1,0:T(8,128)(2,1)S(1)}, bf16[2,48,1024]{2,1,0:T(8,128)(2,1)S(1)}, u32[]{:S(2)}, u32[]{:S(2)}) collective-permute-start(bf16[2,48,1024]{2,1,0:T(8,128)(2,1)S(1)} %add_convert_fusion), channel_id=1, source_target_pairs={{0,8},{1,9},{2,10},{3,11},{4,12},{5,13},{6,14},{7,15},{8,0},{9,1},... | collective-permute-start | bytes 589832 | tf_op jit(solution)/shard_map/ppermute | solution.py:289
  63.9 10.2 %collective-permute-start.18 = (bf16[2,48,1024]{2,1,0:T(8,128)(2,1)S(1)}, bf16[2,48,1024]{2,1,0:T(8,128)(2,1)S(1)}, u32[]{:S(2)}, u32[]{:S(2)}) collective-permute-start(bf16[2,48,1024]{2,1,0:T(8,128)(2,1)S(1)} %get-tuple-element.72.w0), channel_id=1, source_target_pairs={{0,4},{1,5},{2,6},{3,7},{4,0},{5,1},{6,2},{7,3},{8,12},{9,13},{10,... | collective-permute-start | bytes 589832 | tf_op jit(solution)/shard_map/ppermute | solution.py:289
  65.9 8.9 %collective-permute-start.19 = (bf16[2,48,1024]{2,1,0:T(8,128)(2,1)S(1)}, bf16[2,48,1024]{2,1,0:T(8,128)(2,1)S(1)}, u32[]{:S(2)}, u32[]{:S(2)}) collective-permute-start(bf16[2,48,1024]{2,1,0:T(8,128)(2,1)S(1)} %get-tuple-element.72.w0), channel_id=1, source_target_pairs={{0,2},{1,3},{2,4},{3,5},{4,6},{5,7},{6,0},{7,1},{8,10},{9,11},{10,... | collective-permute-start | bytes 589832 | tf_op jit(solution)/shard_map/ppermute | solution.py:289
  67.9 8.4 %collective-permute-start.20 = (bf16[2,48,1024]{2,1,0:T(8,128)(2,1)S(1)}, bf16[2,48,1024]{2,1,0:T(8,128)(2,1)S(1)}, u32[]{:S(2)}, u32[]{:S(2)}) collective-permute-start(bf16[2,48,1024]{2,1,0:T(8,128)(2,1)S(1)} %get-tuple-element.72.w0), channel_id=1, source_target_pairs={{0,6},{1,7},{2,0},{3,1},{4,2},{5,3},{6,4},{7,5},{8,14},{9,15},{10,... | collective-permute-start | bytes 589832 | tf_op jit(solution)/shard_map/ppermute | solution.py:289
  74.8 5.0 %collective-permute-start.23 = (bf16[2,48,1024]{2,1,0:T(8,128)(2,1)S(1)}, bf16[2,48,1024]{2,1,0:T(8,128)(2,1)S(1)}, u32[]{:S(2)}, u32[]{:S(2)}) collective-permute-start(bf16[2,48,1024]{2,1,0:T(8,128)(2,1)S(1)} %collective-permute-done.19.w2), channel_id=1, source_target_pairs={{0,1},{1,0},{2,3},{3,2},{4,5},{5,4},{6,7},{7,6},{8,9},{9,8},{10,11... | collective-permute-start | bytes 589832 | tf_op jit(solution)/shard_map/ppermute | solution.py:289
  76.2 13.5 %collective-permute-start.26 = (bf16[2,48,1024]{2,1,0:T(8,128)(2,1)S(1)}, bf16[2,48,1024]{2,1,0:T(8,128)(2,1)S(1)}, u32[]{:S(2)}, u32[]{:S(2)}) collective-permute-start(bf16[2,48,1024]{2,1,0:T(8,128)(2,1)S(1)} %get-tuple-element.71.w0), channel_id=1, source_target_pairs={{0,4},{1,5},{2,6},{3,7},{4,0},{5,1},{6,2},{7,3},{8,12},{9,13},{10,... | collective-permute-start | bytes 589832 | tf_op jit(solution)/shard_map/ppermute | solution.py:289
  77.8 10.7 %collective-permute-start.16 = (bf16[2,48,1024]{2,1,0:T(8,128)(2,1)S(1)}, bf16[2,48,1024]{2,1,0:T(8,128)(2,1)S(1)}, u32[]{:S(2)}, u32[]{:S(2)}) collective-permute-start(bf16[2,48,1024]{2,1,0:T(8,128)(2,1)S(1)} %get-tuple-element.71.w0), channel_id=1, source_target_pairs={{0,2},{1,3},{2,4},{3,5},{4,6},{5,7},{6,0},{7,1},{8,10},{9,11},{10,... | collective-permute-start | bytes 589832 | tf_op jit(solution)/shard_map/ppermute | solution.py:289
  78.9 10.4 %collective-permute-start.17 = (bf16[2,48,1024]{2,1,0:T(8,128)(2,1)S(1)}, bf16[2,48,1024]{2,1,0:T(8,128)(2,1)S(1)}, u32[]{:S(2)}, u32[]{:S(2)}) collective-permute-start(bf16[2,48,1024]{2,1,0:T(8,128)(2,1)S(1)} %get-tuple-element.71.w0), channel_id=1, source_target_pairs={{0,6},{1,7},{2,0},{3,1},{4,2},{5,3},{6,4},{7,5},{8,14},{9,15},{10,... | collective-permute-start | bytes 589832 | tf_op jit(solution)/shard_map/ppermute | solution.py:289
  83.2 6.6 %collective-permute-start.27 = (bf16[4,48,256]{2,1,0:T(8,128)(2,1)S(1)}, bf16[4,48,256]{2,1,0:T(8,128)(2,1)S(1)}, u32[]{:S(2)}, u32[]{:S(2)}) collective-permute-start(bf16[4,48,256]{2,1,0:T(8,128)(2,1)S(1)} %get-tuple-element.76), channel_id=1, source_target_pairs={{0,64},{16,80},{32,96},{48,112},{64,128},{80,144},{96,160},{112,17... | collective-permute-start | bytes 294920 | tf_op jit(solution)/shard_map/ppermute | solution.py:289
  84.7 7.2 %collective-permute-start.29 = (bf16[2,48,1024]{2,1,0:T(8,128)(2,1)S(1)}, bf16[2,48,1024]{2,1,0:T(8,128)(2,1)S(1)}, u32[]{:S(2)}, u32[]{:S(2)}) collective-permute-start(bf16[2,48,1024]{2,1,0:T(8,128)(2,1)S(1)} %get-tuple-element.71.w0), channel_id=1, source_target_pairs={{0,1},{1,0},{2,3},{3,2},{4,5},{5,4},{6,7},{7,6},{8,9},{9,8},{10,11... | collective-permute-start | bytes 589832 | tf_op jit(solution)/shard_map/ppermute | solution.py:289
  89.9 12.3 %collective-permute-start.25 = (bf16[4,48,256]{2,1,0:T(8,128)(2,1)S(1)}, bf16[4,48,256]{2,1,0:T(8,128)(2,1)S(1)}, u32[]{:S(2)}, u32[]{:S(2)}) collective-permute-start(bf16[4,48,256]{2,1,0:T(8,128)(2,1)S(1)} %get-tuple-element.75), channel_id=1, source_target_pairs={{0,128},{16,144},{32,160},{48,176},{64,192},{80,208},{96,224},{112... | collective-permute-start | bytes 294920 | tf_op jit(solution)/shard_map/ppermute | solution.py:289
  92.0 10.2 %collective-permute-start.28 = (bf16[4,48,256]{2,1,0:T(8,128)(2,1)S(1)}, bf16[4,48,256]{2,1,0:T(8,128)(2,1)S(1)}, u32[]{:S(2)}, u32[]{:S(2)}) collective-permute-start(bf16[4,48,256]{2,1,0:T(8,128)(2,1)S(1)} %get-tuple-element.78), channel_id=1, source_target_pairs={{0,192},{16,208},{32,224},{48,240},{64,0},{80,16},{96,32},{112,48}... | collective-permute-start | bytes 294920 | tf_op jit(solution)/shard_map/ppermute | solution.py:289
  97.4 7.2 %collective-permute-start.33 = (bf16[4,48,256]{2,1,0:T(8,128)(2,1)S(1)}, bf16[4,48,256]{2,1,0:T(8,128)(2,1)S(1)}, u32[]{:S(2)}, u32[]{:S(2)}) collective-permute-start(bf16[4,48,256]{2,1,0:T(8,128)(2,1)S(1)} %get-tuple-element.83), channel_id=1, source_target_pairs={{0,128},{16,144},{32,160},{48,176},{64,192},{80,208},{96,224},{112... | collective-permute-start | bytes 294920 | tf_op jit(solution)/shard_map/ppermute | solution.py:289
  98.9 6.7 %collective-permute-start.34 = (bf16[4,48,256]{2,1,0:T(8,128)(2,1)S(1)}, bf16[4,48,256]{2,1,0:T(8,128)(2,1)S(1)}, u32[]{:S(2)}, u32[]{:S(2)}) collective-permute-start(bf16[4,48,256]{2,1,0:T(8,128)(2,1)S(1)} %get-tuple-element.84), channel_id=1, source_target_pairs={{0,64},{16,80},{32,96},{48,112},{64,128},{80,144},{96,160},{112,17... | collective-permute-start | bytes 294920 | tf_op jit(solution)/shard_map/ppermute | solution.py:289
  98.9 6.7 %collective-permute-start.35 = (bf16[4,48,256]{2,1,0:T(8,128)(2,1)S(1)}, bf16[4,48,256]{2,1,0:T(8,128)(2,1)S(1)}, u32[]{:S(2)}, u32[]{:S(2)}) collective-permute-start(bf16[4,48,256]{2,1,0:T(8,128)(2,1)S(1)} %get-tuple-element.85), channel_id=1, source_target_pairs={{0,192},{16,208},{32,224},{48,240},{64,0},{80,16},{96,32},{112,48}... | collective-permute-start | bytes 294920 | tf_op jit(solution)/shard_map/ppermute | solution.py:289
  105.8 6.2 %collective-permute-start.36 = (bf16[2,48,256]{2,1,0:T(8,128)(2,1)S(1)}, bf16[2,48,256]{2,1,0:T(8,128)(2,1)S(1)}, u32[]{:S(2)}, u32[]{:S(2)}) collective-permute-start(bf16[2,48,256]{2,1,0:T(8,128)(2,1)S(1)} %get-tuple-element.86), channel_id=1, source_target_pairs={{0,48},{16,32},{32,16},{48,0},{64,112},{80,96},{96,80},{112,64},{1... | collective-permute-start | bytes 147464 | tf_op jit(solution)/shard_map/ppermute | solution.py:289
  107.8 5.4 %collective-permute-start.37 = (bf16[2,48,256]{2,1,0:T(8,128)(2,1)S(1)}, bf16[2,48,256]{2,1,0:T(8,128)(2,1)S(1)}, u32[]{:S(2)}, u32[]{:S(2)}) collective-permute-start(bf16[2,48,256]{2,1,0:T(8,128)(2,1)S(1)} %get-tuple-element.87), channel_id=1, source_target_pairs={{0,32},{16,48},{32,0},{48,16},{64,96},{80,112},{96,64},{112,80},{1... | collective-permute-start | bytes 147464 | tf_op jit(solution)/shard_map/ppermute | solution.py:289
  107.8 5.4 %collective-permute-start.38 = (bf16[2,48,256]{2,1,0:T(8,128)(2,1)S(1)}, bf16[2,48,256]{2,1,0:T(8,128)(2,1)S(1)}, u32[]{:S(2)}, u32[]{:S(2)}) collective-permute-start(bf16[2,48,256]{2,1,0:T(8,128)(2,1)S(1)} %get-tuple-element.88), channel_id=1, source_target_pairs={{0,16},{16,0},{32,48},{48,32},{64,80},{80,64},{96,112},{112,96},{1... | collective-permute-start | bytes 147464 | tf_op jit(solution)/shard_map/ppermute | solution.py:289
  (12 other events, 184.3 us)

commit v6 on v5

--- a/solution.py
+++ b/solution.py
@@ -334,6 +334,10 @@
         focusing, jnp.asarray(trace_table())
     )
     near = [send(spectra, "src", to_zl(d)) for d in (3, 2, 1)]
+    stack = jnp.stack([*near, spectra])
+    [reflection], [stack] = together([reflection], [stack])
+    pieces = [stack] + [send(stack, "src", to_x(d)) for d in (2, 1, 3)]
+
     held = call(
         load_kernel,
         pltpu.VMEM((2, NF, NS, NR), BF),
@@ -344,10 +348,6 @@
         cost_estimate=cost(3),
         mib=50,
     )(reflection)
-    near, [spectra, held] = together(near, [spectra, held])
-    stack = jnp.stack([*near, spectra])
-    pieces = [stack] + [send(stack, "src", to_x(d)) for d in (2, 1, 3)]
-
     def summed(give, keep):
         got = send(give, "rcv", to_core)
         return [(keep[d].astype(F32) + got[d].astype(F32)).astype(BF) for d in range(4)]

time: 115 us -> 115 us (level)
  no operation moved by 1% of the time
where the time goes in v6:
time: 115 us
  starting transfers between devices  57 us (50%)
  waiting for transfers between devices  31.4 us (27%)
  Pallas kernels  24 us (21%)
    ppermute x39, starting transfers between devices, send(): return lax.ppermute(value, axis, [(i, to(i)) for i in range(16)])  57 us
    ppermute x39, waiting for transfers between devices, send(): return lax.ppermute(value, axis, [(i, to(i)) for i in range(16)])  31.4 us
    pallas_call x2, Pallas kernels, correlate(): call(corr_kernel, [jax.ShapeDtypeStruct((4, ROWS, NR), BF)] * 4, 'corr',...  6.65 us
    pallas_call x2, Pallas kernels, convolve(): call(functools.partial(conv_kernel, chunk), [jax.ShapeDtypeStruct((8, 2,...  6.05 us
    pallas_call x1, Pallas kernels, on_device(): call(load_kernel, pltpu.VMEM((2, NF, NS, NR), BF), 'load', in_specs=[pl.B...  3.51 us
    pallas_call x2, Pallas kernels, window(): call(functools.partial(window_kernel, h), (jax.ShapeDtypeStruct((2, ROWS,...  3.28 us
  transfers between devices with their start and end apart: 39, of which 16 were waited for; matrix products, arithmetic and copies ran while one was open for 1% of the time, Pallas kernels for 16%

profile of v6, /device:TPU:8, one launch (start us, length us, event | category | flops | bytes accessed | tf_op | source)
XLA Modules:
  0.0 114.7 jit_solution(7716643816255691899)
XLA Ops:
  2.1 4.7 %collective-permute-start = (bf16[96,256]{1,0:T(8,128)(2,1)S(1)}, bf16[96,256]{1,0:T(8,128)(2,1)S(1)}, u32[]{:S(2)}, u32[]{:S(2)}) collective-permute-start(bf16[96,256]{1,0:T(8,128)(2,1)S(1)} %spectra.1), channel_id=1, source_target_pairs={{0,48},{16,32},{32,16},{48,0},{64,112},{80,96},{96,80},{112,64},{1... | collective-permute-start | bytes 147464 | tf_op jit(solution)/shard_map/ppermute | solution.py:289
  7.4 1.8 %collective-permute-done = bf16[96,256]{1,0:T(8,128)(2,1)S(1)} collective-permute-done((bf16[96,256]{1,0:T(8,128)(2,1)S(1)}, bf16[96,256]{1,0:T(8,128)(2,1)S(1)}, u32[]{:S(2)}, u32[]{:S(2)}) %collective-permute-start) | collective-permute-done | bytes 49184 | tf_op jit(solution)/shard_map/ppermute | solution.py:289
  9.2 2.5 %collective-permute-done.1 = bf16[96,256]{1,0:T(8,128)(2,1)S(1)} collective-permute-done((bf16[96,256]{1,0:T(8,128)(2,1)S(1)}, bf16[96,256]{1,0:T(8,128)(2,1)S(1)}, u32[]{:S(2)}, u32[]{:S(2)}) %collective-permute-start.1) | collective-permute-done | bytes 49184 | tf_op jit(solution)/shard_map/ppermute | solution.py:289
  11.8 3.1 %collective-permute-start.3 = (bf16[4,96,256]{2,1,0:T(8,128)(2,1)S(1)}, bf16[4,96,256]{2,1,0:T(8,128)(2,1)S(1)}, u32[]{:S(2)}, u32[]{:S(2)}) collective-permute-start(bf16[4,96,256]{2,1,0:T(8,128)(2,1)S(1)} %pad_maximum_fusion.f0), channel_id=1, source_target_pairs={{0,128},{16,144},{32,160},{48,176},{64,192},{80,208},{96,224},{112... | collective-permute-start | bytes 589832 | tf_op jit(solution)/shard_map/ppermute | solution.py:289
  15.5 2.6 %collective-permute-start.5 = (bf16[4,96,256]{2,1,0:T(8,128)(2,1)S(1)}, bf16[4,96,256]{2,1,0:T(8,128)(2,1)S(1)}, u32[]{:S(2)}, u32[]{:S(2)}) collective-permute-start(bf16[4,96,256]{2,1,0:T(8,128)(2,1)S(1)} %pad_maximum_fusion.f0), channel_id=1, source_target_pairs={{0,192},{16,208},{32,224},{48,240},{64,0},{80,16},{96,32},{112,48}... | collective-permute-start | bytes 589832 | tf_op jit(solution)/shard_map/ppermute | solution.py:289
  18.2 3.5 %load.1.r_ref = bf16[2,8,1024,256]{3,2,1,0:T(8,128)(2,1)S(1)} custom-call(bf16[2,8,1024,256]{3,2,1,0:T(8,128)(2,1)} %r_hbm), custom_call_target="tpu_custom_call" | custom-call | flops 3000000000 | bytes 65536 | tf_op jit(solution)/shard_map/load/pallas_call | solution.py:341
  21.7 1.9 %collective-permute-done.4.f2 = bf16[4,96,256]{2,1,0:T(8,128)(2,1)S(1)} collective-permute-done((bf16[4,96,256]{2,1,0:T(8,128)(2,1)S(1)}, bf16[4,96,256]{2,1,0:T(8,128)(2,1)S(1)}, u32[]{:S(2)}, u32[]{:S(2)}) %collective-permute-start.4) | collective-permute-done | bytes 196640 | tf_op jit(solution)/shard_map/ppermute | solution.py:289
  23.6 3.0 %conv0.1 = (bf16[8,2,24,1024]{3,2,1,0:T(8,128)(2,1)S(1)}, bf16[8,2,24,1024]{3,2,1,0:T(8,128)(2,1)S(1)}) custom-call(bf16[4,96,256]{2,1,0:T(8,128)(2,1)S(1)} %pad_maximum_fusion.f0, bf16[4,96,256]{2,1,0:T(8,128)(2,1)S(1)} %collective-permute-done.3.f1, bf16[4,96,256]{2,1,0:T(8,128)(2,1)S(1)} %collective-permute-done.4.f2, ...), custom_call_target="tpu_custom_call" | custom-call | flops 4000000000 | bytes 65536 | tf_op jit(solution)/shard_map/conv0/pallas_call | solution.py:170
  26.7 3.0 %conv1.1 = (bf16[8,2,24,1024]{3,2,1,0:T(8,128)(2,1)S(1)}, bf16[8,2,24,1024]{3,2,1,0:T(8,128)(2,1)S(1)}) custom-call(bf16[4,96,256]{2,1,0:T(8,128)(2,1)S(1)} %pad_maximum_fusion.f0, bf16[4,96,256]{2,1,0:T(8,128)(2,1)S(1)} %collective-permute-done.3.f1, bf16[4,96,256]{2,1,0:T(8,128)(2,1)S(1)} %collective-permute-done.4.f2, ...), custom_call_target="tpu_custom_call" | custom-call | flops 4000000000 | bytes 65536 | tf_op jit(solution)/shard_map/conv1/pallas_call | solution.py:170
  30.8 2.4 %collective-permute-start.7 = (bf16[2,48,1024]{2,1,0:T(8,128)(2,1)S(1)}, bf16[2,48,1024]{2,1,0:T(8,128)(2,1)S(1)}, u32[]{:S(2)}, u32[]{:S(2)}) collective-permute-start(bf16[2,48,1024]{2,1,0:T(8,128)(2,1)S(1)} %get-tuple-element.100), channel_id=1, source_target_pairs={{0,4},{1,5},{2,6},{3,7},{4,0},{5,1},{6,2},{7,3},{8,12},{9,13},{10,... | collective-permute-start | bytes 589832 | tf_op jit(solution)/shard_map/ppermute | solution.py:289
  33.1 2.0 %collective-permute-start.9 = (bf16[2,48,1024]{2,1,0:T(8,128)(2,1)S(1)}, bf16[2,48,1024]{2,1,0:T(8,128)(2,1)S(1)}, u32[]{:S(2)}, u32[]{:S(2)}) collective-permute-start(bf16[2,48,1024]{2,1,0:T(8,128)(2,1)S(1)} %get-tuple-element.98), channel_id=1, source_target_pairs={{0,6},{1,7},{2,0},{3,1},{4,2},{5,3},{6,4},{7,5},{8,14},{9,15},{10,... | collective-permute-start | bytes 589832 | tf_op jit(solution)/shard_map/ppermute | solution.py:289
  35.5 4.6 %collective-permute-done.7.p1 = bf16[2,48,1024]{2,1,0:T(8,128)(2,1)S(1)} collective-permute-done((bf16[2,48,1024]{2,1,0:T(8,128)(2,1)S(1)}, bf16[2,48,1024]{2,1,0:T(8,128)(2,1)S(1)}, u32[]{:S(2)}, u32[]{:S(2)}) %collective-permute-start.7) | collective-permute-done | bytes 196640 | tf_op jit(solution)/shard_map/ppermute | solution.py:289
  40.2 3.4 %collective-permute-done.8.p2 = bf16[2,48,1024]{2,1,0:T(8,128)(2,1)S(1)} collective-permute-done((bf16[2,48,1024]{2,1,0:T(8,128)(2,1)S(1)}, bf16[2,48,1024]{2,1,0:T(8,128)(2,1)S(1)}, u32[]{:S(2)}, u32[]{:S(2)}) %collective-permute-start.8) | collective-permute-done | bytes 196640 | tf_op jit(solution)/shard_map/ppermute | solution.py:289
  43.5 2.1 %collective-permute-start.12 = (bf16[2,48,1024]{2,1,0:T(8,128)(2,1)S(1)}, bf16[2,48,1024]{2,1,0:T(8,128)(2,1)S(1)}, u32[]{:S(2)}, u32[]{:S(2)}) collective-permute-start(bf16[2,48,1024]{2,1,0:T(8,128)(2,1)S(1)} %get-tuple-element.53), channel_id=1, source_target_pairs={{0,4},{1,5},{2,6},{3,7},{4,0},{5,1},{6,2},{7,3},{8,12},{9,13},{10,... | collective-permute-start | bytes 589832 | tf_op jit(solution)/shard_map/ppermute | solution.py:289
  45.7 2.0 %collective-permute-start.14 = (bf16[2,48,1024]{2,1,0:T(8,128)(2,1)S(1)}, bf16[2,48,1024]{2,1,0:T(8,128)(2,1)S(1)}, u32[]{:S(2)}, u32[]{:S(2)}) collective-permute-start(bf16[2,48,1024]{2,1,0:T(8,128)(2,1)S(1)} %get-tuple-element.55), channel_id=1, source_target_pairs={{0,6},{1,7},{2,0},{3,1},{4,2},{5,3},{6,4},{7,5},{8,14},{9,15},{10,... | collective-permute-start | bytes 589832 | tf_op jit(solution)/shard_map/ppermute | solution.py:289
  47.9 6.2 %collective-permute-start.11 = (bf16[2,48,1024]{2,1,0:T(8,128)(2,1)S(1)}, bf16[2,48,1024]{2,1,0:T(8,128)(2,1)S(1)}, u32[]{:S(2)}, u32[]{:S(2)}) collective-permute-start(bf16[2,48,1024]{2,1,0:T(8,128)(2,1)S(1)} %get-tuple-element.84), channel_id=1, source_target_pairs={{0,8},{1,9},{2,10},{3,11},{4,12},{5,13},{6,14},{7,15},{8,0},{9,1},... | collective-permute-start | bytes 589832 | tf_op jit(solution)/shard_map/ppermute | solution.py:289
  56.1 6.2 %collective-permute-start.15 = (bf16[2,48,1024]{2,1,0:T(8,128)(2,1)S(1)}, bf16[2,48,1024]{2,1,0:T(8,128)(2,1)S(1)}, u32[]{:S(2)}, u32[]{:S(2)}) collective-permute-start(bf16[2,48,1024]{2,1,0:T(8,128)(2,1)S(1)} %add_convert_fusion), channel_id=1, source_target_pairs={{0,8},{1,9},{2,10},{3,11},{4,12},{5,13},{6,14},{7,15},{8,0},{9,1},... | collective-permute-start | bytes 589832 | tf_op jit(solution)/shard_map/ppermute | solution.py:289
  62.3 1.6 %window0.1 = (bf16[2,48,1024]{2,1,0:T(8,128)(2,1)S(1)}, bf16[3,128,1024]{2,1,0:T(8,128)(2,1)S(1)}) custom-call(bf16[2,48,1024]{2,1,0:T(8,128)(2,1)S(1)} %get-tuple-element.85.p0, bf16[2,48,1024]{2,1,0:T(8,128)(2,1)S(1)} %collective-permute-done.7.p1, bf16[2,48,1024]{2,1,0:T(8,128)(2,1)S(1)} %collective-permute-done.8.p2, ...), custom_call_target="tpu_custom_call" | custom-call | flops 2000000000 | bytes 65536 | tf_op jit(solution)/shard_map/window0/pallas_call | solution.py:362
  63.9 2.0 %collective-permute-start.18 = (bf16[2,48,1024]{2,1,0:T(8,128)(2,1)S(1)}, bf16[2,48,1024]{2,1,0:T(8,128)(2,1)S(1)}, u32[]{:S(2)}, u32[]{:S(2)}) collective-permute-start(bf16[2,48,1024]{2,1,0:T(8,128)(2,1)S(1)} %get-tuple-element.66.w0), channel_id=1, source_target_pairs={{0,4},{1,5},{2,6},{3,7},{4,0},{5,1},{6,2},{7,3},{8,12},{9,13},{10,... | collective-permute-start | bytes 589832 | tf_op jit(solution)/shard_map/ppermute | solution.py:289
  65.9 2.0 %collective-permute-start.19 = (bf16[2,48,1024]{2,1,0:T(8,128)(2,1)S(1)}, bf16[2,48,1024]{2,1,0:T(8,128)(2,1)S(1)}, u32[]{:S(2)}, u32[]{:S(2)}) collective-permute-start(bf16[2,48,1024]{2,1,0:T(8,128)(2,1)S(1)} %get-tuple-element.66.w0), channel_id=1, source_target_pairs={{0,2},{1,3},{2,4},{3,5},{4,6},{5,7},{6,0},{7,1},{8,10},{9,11},{10,... | collective-permute-start | bytes 589832 | tf_op jit(solution)/shard_map/ppermute | solution.py:289
  67.9 3.0 %collective-permute-done.15.r_ref = bf16[2,48,1024]{2,1,0:T(8,128)(2,1)S(1)} collective-permute-done((bf16[2,48,1024]{2,1,0:T(8,128)(2,1)S(1)}, bf16[2,48,1024]{2,1,0:T(8,128)(2,1)S(1)}, u32[]{:S(2)}, u32[]{:S(2)}) %collective-permute-start.15) | collective-permute-done | bytes 196640 | tf_op jit(solution)/shard_map/ppermute | solution.py:289
  70.9 1.6 %window1.1 = (bf16[2,48,1024]{2,1,0:T(8,128)(2,1)S(1)}, bf16[3,128,1024]{2,1,0:T(8,128)(2,1)S(1)}) custom-call(bf16[2,48,1024]{2,1,0:T(8,128)(2,1)S(1)} %get-tuple-element.59.p0, bf16[2,48,1024]{2,1,0:T(8,128)(2,1)S(1)} %collective-permute-done.12.p1, bf16[2,48,1024]{2,1,0:T(8,128)(2,1)S(1)} %collective-permute-done.13.p2, ...), custom_call_target="tpu_custom_call" | custom-call | flops 2000000000 | bytes 65536 | tf_op jit(solution)/shard_map/window1/pallas_call | solution.py:362
  72.6 1.6 %flip.1 = bf16[6,1024,128]{2,1,0:T(8,128)(2,1)} custom-call(bf16[3,128,1024]{2,1,0:T(8,128)(2,1)S(1)} %get-tuple-element.58.a_ref, bf16[3,128,1024]{2,1,0:T(8,128)(2,1)S(1)} %get-tuple-element.63.b_ref), custom_call_target="tpu_custom_call" | custom-call | flops 2000000000 | bytes 65536 | tf_op jit(solution)/shard_map/flip/pallas_call | solution.py:381
  79.8 3.3 %corr.2 = (bf16[4,48,256]{2,1,0:T(8,128)(2,1)S(1)}, bf16[4,48,256]{2,1,0:T(8,128)(2,1)S(1)}, bf16[4,48,256]{2,1,0:T(8,128)(2,1)S(1)}, bf16[4,48,256]{2,1,0:T(8,128)(2,1)S(1)}) custom-call(bf16[2,48,1024]{2,1,0:T(8,128)(2,1)S(1)} %get-tuple-element.66.w0, bf16[2,48,1024]{2,1,0:T(8,128)(2,1)S(1)} %collective-permute-done.18.w1, ...), custom_call_target="tpu_custom_call" | custom-call | flops 4000000000 | bytes 65536 | tf_op jit(solution)/shard_map/corr/pallas_call | solution.py:250
  84.7 3.7 %collective-permute-done.16.w2 = bf16[2,48,1024]{2,1,0:T(8,128)(2,1)S(1)} collective-permute-done((bf16[2,48,1024]{2,1,0:T(8,128)(2,1)S(1)}, bf16[2,48,1024]{2,1,0:T(8,128)(2,1)S(1)}, u32[]{:S(2)}, u32[]{:S(2)}) %collective-permute-start.16) | collective-permute-done | bytes 196640 | tf_op jit(solution)/shard_map/ppermute | solution.py:289
  89.9 2.1 %collective-permute-start.25 = (bf16[4,48,256]{2,1,0:T(8,128)(2,1)S(1)}, bf16[4,48,256]{2,1,0:T(8,128)(2,1)S(1)}, u32[]{:S(2)}, u32[]{:S(2)}) collective-permute-start(bf16[4,48,256]{2,1,0:T(8,128)(2,1)S(1)} %get-tuple-element.69), channel_id=1, source_target_pairs={{0,128},{16,144},{32,160},{48,176},{64,192},{80,208},{96,224},{112... | collective-permute-start | bytes 294920 | tf_op jit(solution)/shard_map/ppermute | solution.py:289
  92.0 2.1 %collective-permute-start.28 = (bf16[4,48,256]{2,1,0:T(8,128)(2,1)S(1)}, bf16[4,48,256]{2,1,0:T(8,128)(2,1)S(1)}, u32[]{:S(2)}, u32[]{:S(2)}) collective-permute-start(bf16[4,48,256]{2,1,0:T(8,128)(2,1)S(1)} %get-tuple-element.72), channel_id=1, source_target_pairs={{0,192},{16,208},{32,224},{48,240},{64,0},{80,16},{96,32},{112,48}... | collective-permute-start | bytes 294920 | tf_op jit(solution)/shard_map/ppermute | solution.py:289
  94.1 3.3 %corr.3 = (bf16[4,48,256]{2,1,0:T(8,128)(2,1)S(1)}, bf16[4,48,256]{2,1,0:T(8,128)(2,1)S(1)}, bf16[4,48,256]{2,1,0:T(8,128)(2,1)S(1)}, bf16[4,48,256]{2,1,0:T(8,128)(2,1)S(1)}) custom-call(bf16[2,48,1024]{2,1,0:T(8,128)(2,1)S(1)} %get-tuple-element.65.w0, bf16[2,48,1024]{2,1,0:T(8,128)(2,1)S(1)} %collective-permute-done.26.w1, ...), custom_call_target="tpu_custom_call" | custom-call | flops 4000000000 | bytes 65536 | tf_op jit(solution)/shard_map/corr/pallas_call | solution.py:250
  98.9 3.2 %collective-permute-start.35 = (bf16[4,48,256]{2,1,0:T(8,128)(2,1)S(1)}, bf16[4,48,256]{2,1,0:T(8,128)(2,1)S(1)}, u32[]{:S(2)}, u32[]{:S(2)}) collective-permute-start(bf16[4,48,256]{2,1,0:T(8,128)(2,1)S(1)} %get-tuple-element.79), channel_id=1, source_target_pairs={{0,192},{16,208},{32,224},{48,240},{64,0},{80,16},{96,32},{112,48}... | collective-permute-start | bytes 294920 | tf_op jit(solution)/shard_map/ppermute | solution.py:289
  102.2 2.4 %collective-permute-done.33.refs_5_ = bf16[4,48,256]{2,1,0:T(8,128)(2,1)S(1)} collective-permute-done((bf16[4,48,256]{2,1,0:T(8,128)(2,1)S(1)}, bf16[4,48,256]{2,1,0:T(8,128)(2,1)S(1)}, u32[]{:S(2)}, u32[]{:S(2)}) %collective-permute-start.33) | collective-permute-done | bytes 98336 | tf_op jit(solution)/shard_map/ppermute | solution.py:289
  105.8 2.0 %collective-permute-start.36 = (bf16[2,48,256]{2,1,0:T(8,128)(2,1)S(1)}, bf16[2,48,256]{2,1,0:T(8,128)(2,1)S(1)}, u32[]{:S(2)}, u32[]{:S(2)}) collective-permute-start(bf16[2,48,256]{2,1,0:T(8,128)(2,1)S(1)} %get-tuple-element.80), channel_id=1, source_target_pairs={{0,48},{16,32},{32,16},{48,0},{64,112},{80,96},{96,80},{112,64},{1... | collective-permute-start | bytes 147464 | tf_op jit(solution)/shard_map/ppermute | solution.py:289
  107.8 2.5 %collective-permute-start.38 = (bf16[2,48,256]{2,1,0:T(8,128)(2,1)S(1)}, bf16[2,48,256]{2,1,0:T(8,128)(2,1)S(1)}, u32[]{:S(2)}, u32[]{:S(2)}) collective-permute-start(bf16[2,48,256]{2,1,0:T(8,128)(2,1)S(1)} %get-tuple-element.82), channel_id=1, source_target_pairs={{0,16},{16,0},{32,48},{48,32},{64,80},{80,64},{96,112},{112,96},{1... | collective-permute-start | bytes 147464 | tf_op jit(solution)/shard_map/ppermute | solution.py:289
  (75 shorter events, 21.9 us)
Async XLA Ops:
  2.1 7.2 %collective-permute-start = (bf16[96,256]{1,0:T(8,128)(2,1)S(1)}, bf16[96,256]{1,0:T(8,128)(2,1)S(1)}, u32[]{:S(2)}, u32[]{:S(2)}) collective-permute-start(bf16[96,256]{1,0:T(8,128)(2,1)S(1)} %spectra.1), channel_id=1, source_target_pairs={{0,48},{16,32},{32,16},{48,0},{64,112},{80,96},{96,80},{112,64},{1... | collective-permute-start | bytes 147464 | tf_op jit(solution)/shard_map/ppermute | solution.py:289
  6.8 5.0 %collective-permute-start.1 = (bf16[96,256]{1,0:T(8,128)(2,1)S(1)}, bf16[96,256]{1,0:T(8,128)(2,1)S(1)}, u32[]{:S(2)}, u32[]{:S(2)}) collective-permute-start(bf16[96,256]{1,0:T(8,128)(2,1)S(1)} %spectra.1), channel_id=1, source_target_pairs={{0,32},{16,48},{32,0},{48,16},{64,96},{80,112},{96,64},{112,80},{1... | collective-permute-start | bytes 147464 | tf_op jit(solution)/shard_map/ppermute | solution.py:289
  6.8 5.0 %collective-permute-start.2 = (bf16[96,256]{1,0:T(8,128)(2,1)S(1)}, bf16[96,256]{1,0:T(8,128)(2,1)S(1)}, u32[]{:S(2)}, u32[]{:S(2)}) collective-permute-start(bf16[96,256]{1,0:T(8,128)(2,1)S(1)} %spectra.1), channel_id=1, source_target_pairs={{0,16},{16,0},{32,48},{48,32},{64,80},{80,64},{96,112},{112,96},{1... | collective-permute-start | bytes 147464 | tf_op jit(solution)/shard_map/ppermute | solution.py:289
  11.8 9.9 %collective-permute-start.3 = (bf16[4,96,256]{2,1,0:T(8,128)(2,1)S(1)}, bf16[4,96,256]{2,1,0:T(8,128)(2,1)S(1)}, u32[]{:S(2)}, u32[]{:S(2)}) collective-permute-start(bf16[4,96,256]{2,1,0:T(8,128)(2,1)S(1)} %pad_maximum_fusion.f0), channel_id=1, source_target_pairs={{0,128},{16,144},{32,160},{48,176},{64,192},{80,208},{96,224},{112... | collective-permute-start | bytes 589832 | tf_op jit(solution)/shard_map/ppermute | solution.py:289
  14.9 8.7 %collective-permute-start.4 = (bf16[4,96,256]{2,1,0:T(8,128)(2,1)S(1)}, bf16[4,96,256]{2,1,0:T(8,128)(2,1)S(1)}, u32[]{:S(2)}, u32[]{:S(2)}) collective-permute-start(bf16[4,96,256]{2,1,0:T(8,128)(2,1)S(1)} %pad_maximum_fusion.f0), channel_id=1, source_target_pairs={{0,64},{16,80},{32,96},{48,112},{64,128},{80,144},{96,160},{112,17... | collective-permute-start | bytes 589832 | tf_op jit(solution)/shard_map/ppermute | solution.py:289
  15.5 8.1 %collective-permute-start.5 = (bf16[4,96,256]{2,1,0:T(8,128)(2,1)S(1)}, bf16[4,96,256]{2,1,0:T(8,128)(2,1)S(1)}, u32[]{:S(2)}, u32[]{:S(2)}) collective-permute-start(bf16[4,96,256]{2,1,0:T(8,128)(2,1)S(1)} %pad_maximum_fusion.f0), channel_id=1, source_target_pairs={{0,192},{16,208},{32,224},{48,240},{64,0},{80,16},{96,32},{112,48}... | collective-permute-start | bytes 589832 | tf_op jit(solution)/shard_map/ppermute | solution.py:289
  29.8 5.4 %collective-permute-start.10 = (bf16[4,2,48,1024]{3,2,1,0:T(8,128)(2,1)S(1)}, bf16[4,2,48,1024]{3,2,1,0:T(8,128)(2,1)S(1)}, u32[]{:S(2)}, u32[]{:S(2)}) collective-permute-start(bf16[4,2,48,1024]{3,2,1,0:T(8,128)(2,1)S(1)} %bitcast.75), channel_id=1, source_target_pairs={{0,1},{1,0},{2,3},{3,2},{4,5},{5,4},{6,7},{7,6},{8,9},{9,8},{10,11... | collective-permute-start | bytes 2359304 | tf_op jit(solution)/shard_map/ppermute | solution.py:289
  30.8 9.4 %collective-permute-start.7 = (bf16[2,48,1024]{2,1,0:T(8,128)(2,1)S(1)}, bf16[2,48,1024]{2,1,0:T(8,128)(2,1)S(1)}, u32[]{:S(2)}, u32[]{:S(2)}) collective-permute-start(bf16[2,48,1024]{2,1,0:T(8,128)(2,1)S(1)} %get-tuple-element.100), channel_id=1, source_target_pairs={{0,4},{1,5},{2,6},{3,7},{4,0},{5,1},{6,2},{7,3},{8,12},{9,13},{10,... | collective-permute-start | bytes 589832 | tf_op jit(solution)/shard_map/ppermute | solution.py:289
  33.1 10.4 %collective-permute-start.8 = (bf16[2,48,1024]{2,1,0:T(8,128)(2,1)S(1)}, bf16[2,48,1024]{2,1,0:T(8,128)(2,1)S(1)}, u32[]{:S(2)}, u32[]{:S(2)}) collective-permute-start(bf16[2,48,1024]{2,1,0:T(8,128)(2,1)S(1)} %get-tuple-element.99), channel_id=1, source_target_pairs={{0,2},{1,3},{2,4},{3,5},{4,6},{5,7},{6,0},{7,1},{8,10},{9,11},{10,... | collective-permute-start | bytes 589832 | tf_op jit(solution)/shard_map/ppermute | solution.py:289
  33.1 10.4 %collective-permute-start.9 = (bf16[2,48,1024]{2,1,0:T(8,128)(2,1)S(1)}, bf16[2,48,1024]{2,1,0:T(8,128)(2,1)S(1)}, u32[]{:S(2)}, u32[]{:S(2)}) collective-permute-start(bf16[2,48,1024]{2,1,0:T(8,128)(2,1)S(1)} %get-tuple-element.98), channel_id=1, source_target_pairs={{0,6},{1,7},{2,0},{3,1},{4,2},{5,3},{6,4},{7,5},{8,14},{9,15},{10,... | collective-permute-start | bytes 589832 | tf_op jit(solution)/shard_map/ppermute | solution.py:289
  43.5 10.6 %collective-permute-start.12 = (bf16[2,48,1024]{2,1,0:T(8,128)(2,1)S(1)}, bf16[2,48,1024]{2,1,0:T(8,128)(2,1)S(1)}, u32[]{:S(2)}, u32[]{:S(2)}) collective-permute-start(bf16[2,48,1024]{2,1,0:T(8,128)(2,1)S(1)} %get-tuple-element.53), channel_id=1, source_target_pairs={{0,4},{1,5},{2,6},{3,7},{4,0},{5,1},{6,2},{7,3},{8,12},{9,13},{10,... | collective-permute-start | bytes 589832 | tf_op jit(solution)/shard_map/ppermute | solution.py:289
  45.7 8.9 %collective-permute-start.13 = (bf16[2,48,1024]{2,1,0:T(8,128)(2,1)S(1)}, bf16[2,48,1024]{2,1,0:T(8,128)(2,1)S(1)}, u32[]{:S(2)}, u32[]{:S(2)}) collective-permute-start(bf16[2,48,1024]{2,1,0:T(8,128)(2,1)S(1)} %get-tuple-element.54), channel_id=1, source_target_pairs={{0,2},{1,3},{2,4},{3,5},{4,6},{5,7},{6,0},{7,1},{8,10},{9,11},{10,... | collective-permute-start | bytes 589832 | tf_op jit(solution)/shard_map/ppermute | solution.py:289
  45.7 10.2 %collective-permute-start.14 = (bf16[2,48,1024]{2,1,0:T(8,128)(2,1)S(1)}, bf16[2,48,1024]{2,1,0:T(8,128)(2,1)S(1)}, u32[]{:S(2)}, u32[]{:S(2)}) collective-permute-start(bf16[2,48,1024]{2,1,0:T(8,128)(2,1)S(1)} %get-tuple-element.55), channel_id=1, source_target_pairs={{0,6},{1,7},{2,0},{3,1},{4,2},{5,3},{6,4},{7,5},{8,14},{9,15},{10,... | collective-permute-start | bytes 589832 | tf_op jit(solution)/shard_map/ppermute | solution.py:289
  47.9 14.4 %collective-permute-start.11 = (bf16[2,48,1024]{2,1,0:T(8,128)(2,1)S(1)}, bf16[2,48,1024]{2,1,0:T(8,128)(2,1)S(1)}, u32[]{:S(2)}, u32[]{:S(2)}) collective-permute-start(bf16[2,48,1024]{2,1,0:T(8,128)(2,1)S(1)} %get-tuple-element.84), channel_id=1, source_target_pairs={{0,8},{1,9},{2,10},{3,11},{4,12},{5,13},{6,14},{7,15},{8,0},{9,1},... | collective-permute-start | bytes 589832 | tf_op jit(solution)/shard_map/ppermute | solution.py:289
  56.1 14.9 %collective-permute-start.15 = (bf16[2,48,1024]{2,1,0:T(8,128)(2,1)S(1)}, bf16[2,48,1024]{2,1,0:T(8,128)(2,1)S(1)}, u32[]{:S(2)}, u32[]{:S(2)}) collective-permute-start(bf16[2,48,1024]{2,1,0:T(8,128)(2,1)S(1)} %add_convert_fusion), channel_id=1, source_target_pairs={{0,8},{1,9},{2,10},{3,11},{4,12},{5,13},{6,14},{7,15},{8,0},{9,1},... | collective-permute-start | bytes 589832 | tf_op jit(solution)/shard_map/ppermute | solution.py:289
  63.9 10.3 %collective-permute-start.18 = (bf16[2,48,1024]{2,1,0:T(8,128)(2,1)S(1)}, bf16[2,48,1024]{2,1,0:T(8,128)(2,1)S(1)}, u32[]{:S(2)}, u32[]{:S(2)}) collective-permute-start(bf16[2,48,1024]{2,1,0:T(8,128)(2,1)S(1)} %get-tuple-element.66.w0), channel_id=1, source_target_pairs={{0,4},{1,5},{2,6},{3,7},{4,0},{5,1},{6,2},{7,3},{8,12},{9,13},{10,... | collective-permute-start | bytes 589832 | tf_op jit(solution)/shard_map/ppermute | solution.py:289
  65.9 8.9 %collective-permute-start.19 = (bf16[2,48,1024]{2,1,0:T(8,128)(2,1)S(1)}, bf16[2,48,1024]{2,1,0:T(8,128)(2,1)S(1)}, u32[]{:S(2)}, u32[]{:S(2)}) collective-permute-start(bf16[2,48,1024]{2,1,0:T(8,128)(2,1)S(1)} %get-tuple-element.66.w0), channel_id=1, source_target_pairs={{0,2},{1,3},{2,4},{3,5},{4,6},{5,7},{6,0},{7,1},{8,10},{9,11},{10,... | collective-permute-start | bytes 589832 | tf_op jit(solution)/shard_map/ppermute | solution.py:289
  67.9 8.4 %collective-permute-start.20 = (bf16[2,48,1024]{2,1,0:T(8,128)(2,1)S(1)}, bf16[2,48,1024]{2,1,0:T(8,128)(2,1)S(1)}, u32[]{:S(2)}, u32[]{:S(2)}) collective-permute-start(bf16[2,48,1024]{2,1,0:T(8,128)(2,1)S(1)} %get-tuple-element.66.w0), channel_id=1, source_target_pairs={{0,6},{1,7},{2,0},{3,1},{4,2},{5,3},{6,4},{7,5},{8,14},{9,15},{10,... | collective-permute-start | bytes 589832 | tf_op jit(solution)/shard_map/ppermute | solution.py:289
  74.9 5.0 %collective-permute-start.23 = (bf16[2,48,1024]{2,1,0:T(8,128)(2,1)S(1)}, bf16[2,48,1024]{2,1,0:T(8,128)(2,1)S(1)}, u32[]{:S(2)}, u32[]{:S(2)}) collective-permute-start(bf16[2,48,1024]{2,1,0:T(8,128)(2,1)S(1)} %collective-permute-done.19.w2), channel_id=1, source_target_pairs={{0,1},{1,0},{2,3},{3,2},{4,5},{5,4},{6,7},{7,6},{8,9},{9,8},{10,11... | collective-permute-start | bytes 589832 | tf_op jit(solution)/shard_map/ppermute | solution.py:289
  76.2 13.5 %collective-permute-start.26 = (bf16[2,48,1024]{2,1,0:T(8,128)(2,1)S(1)}, bf16[2,48,1024]{2,1,0:T(8,128)(2,1)S(1)}, u32[]{:S(2)}, u32[]{:S(2)}) collective-permute-start(bf16[2,48,1024]{2,1,0:T(8,128)(2,1)S(1)} %get-tuple-element.65.w0), channel_id=1, source_target_pairs={{0,4},{1,5},{2,6},{3,7},{4,0},{5,1},{6,2},{7,3},{8,12},{9,13},{10,... | collective-permute-start | bytes 589832 | tf_op jit(solution)/shard_map/ppermute | solution.py:289
  77.8 10.7 %collective-permute-start.16 = (bf16[2,48,1024]{2,1,0:T(8,128)(2,1)S(1)}, bf16[2,48,1024]{2,1,0:T(8,128)(2,1)S(1)}, u32[]{:S(2)}, u32[]{:S(2)}) collective-permute-start(bf16[2,48,1024]{2,1,0:T(8,128)(2,1)S(1)} %get-tuple-element.65.w0), channel_id=1, source_target_pairs={{0,2},{1,3},{2,4},{3,5},{4,6},{5,7},{6,0},{7,1},{8,10},{9,11},{10,... | collective-permute-start | bytes 589832 | tf_op jit(solution)/shard_map/ppermute | solution.py:289
  78.9 10.4 %collective-permute-start.17 = (bf16[2,48,1024]{2,1,0:T(8,128)(2,1)S(1)}, bf16[2,48,1024]{2,1,0:T(8,128)(2,1)S(1)}, u32[]{:S(2)}, u32[]{:S(2)}) collective-permute-start(bf16[2,48,1024]{2,1,0:T(8,128)(2,1)S(1)} %get-tuple-element.65.w0), channel_id=1, source_target_pairs={{0,6},{1,7},{2,0},{3,1},{4,2},{5,3},{6,4},{7,5},{8,14},{9,15},{10,... | collective-permute-start | bytes 589832 | tf_op jit(solution)/shard_map/ppermute | solution.py:289
  83.2 6.6 %collective-permute-start.27 = (bf16[4,48,256]{2,1,0:T(8,128)(2,1)S(1)}, bf16[4,48,256]{2,1,0:T(8,128)(2,1)S(1)}, u32[]{:S(2)}, u32[]{:S(2)}) collective-permute-start(bf16[4,48,256]{2,1,0:T(8,128)(2,1)S(1)} %get-tuple-element.70), channel_id=1, source_target_pairs={{0,64},{16,80},{32,96},{48,112},{64,128},{80,144},{96,160},{112,17... | collective-permute-start | bytes 294920 | tf_op jit(solution)/shard_map/ppermute | solution.py:289
  84.7 7.2 %collective-permute-start.29 = (bf16[2,48,1024]{2,1,0:T(8,128)(2,1)S(1)}, bf16[2,48,1024]{2,1,0:T(8,128)(2,1)S(1)}, u32[]{:S(2)}, u32[]{:S(2)}) collective-permute-start(bf16[2,48,1024]{2,1,0:T(8,128)(2,1)S(1)} %get-tuple-element.65.w0), channel_id=1, source_target_pairs={{0,1},{1,0},{2,3},{3,2},{4,5},{5,4},{6,7},{7,6},{8,9},{9,8},{10,11... | collective-permute-start | bytes 589832 | tf_op jit(solution)/shard_map/ppermute | solution.py:289
  89.9 12.3 %collective-permute-start.25 = (bf16[4,48,256]{2,1,0:T(8,128)(2,1)S(1)}, bf16[4,48,256]{2,1,0:T(8,128)(2,1)S(1)}, u32[]{:S(2)}, u32[]{:S(2)}) collective-permute-start(bf16[4,48,256]{2,1,0:T(8,128)(2,1)S(1)} %get-tuple-element.69), channel_id=1, source_target_pairs={{0,128},{16,144},{32,160},{48,176},{64,192},{80,208},{96,224},{112... | collective-permute-start | bytes 294920 | tf_op jit(solution)/shard_map/ppermute | solution.py:289
  92.0 10.2 %collective-permute-start.28 = (bf16[4,48,256]{2,1,0:T(8,128)(2,1)S(1)}, bf16[4,48,256]{2,1,0:T(8,128)(2,1)S(1)}, u32[]{:S(2)}, u32[]{:S(2)}) collective-permute-start(bf16[4,48,256]{2,1,0:T(8,128)(2,1)S(1)} %get-tuple-element.72), channel_id=1, source_target_pairs={{0,192},{16,208},{32,224},{48,240},{64,0},{80,16},{96,32},{112,48}... | collective-permute-start | bytes 294920 | tf_op jit(solution)/shard_map/ppermute | solution.py:289
  97.4 7.2 %collective-permute-start.33 = (bf16[4,48,256]{2,1,0:T(8,128)(2,1)S(1)}, bf16[4,48,256]{2,1,0:T(8,128)(2,1)S(1)}, u32[]{:S(2)}, u32[]{:S(2)}) collective-permute-start(bf16[4,48,256]{2,1,0:T(8,128)(2,1)S(1)} %get-tuple-element.77), channel_id=1, source_target_pairs={{0,128},{16,144},{32,160},{48,176},{64,192},{80,208},{96,224},{112... | collective-permute-start | bytes 294920 | tf_op jit(solution)/shard_map/ppermute | solution.py:289
  98.9 6.7 %collective-permute-start.34 = (bf16[4,48,256]{2,1,0:T(8,128)(2,1)S(1)}, bf16[4,48,256]{2,1,0:T(8,128)(2,1)S(1)}, u32[]{:S(2)}, u32[]{:S(2)}) collective-permute-start(bf16[4,48,256]{2,1,0:T(8,128)(2,1)S(1)} %get-tuple-element.78), channel_id=1, source_target_pairs={{0,64},{16,80},{32,96},{48,112},{64,128},{80,144},{96,160},{112,17... | collective-permute-start | bytes 294920 | tf_op jit(solution)/shard_map/ppermute | solution.py:289
  98.9 6.7 %collective-permute-start.35 = (bf16[4,48,256]{2,1,0:T(8,128)(2,1)S(1)}, bf16[4,48,256]{2,1,0:T(8,128)(2,1)S(1)}, u32[]{:S(2)}, u32[]{:S(2)}) collective-permute-start(bf16[4,48,256]{2,1,0:T(8,128)(2,1)S(1)} %get-tuple-element.79), channel_id=1, source_target_pairs={{0,192},{16,208},{32,224},{48,240},{64,0},{80,16},{96,32},{112,48}... | collective-permute-start | bytes 294920 | tf_op jit(solution)/shard_map/ppermute | solution.py:289
  105.8 6.2 %collective-permute-start.36 = (bf16[2,48,256]{2,1,0:T(8,128)(2,1)S(1)}, bf16[2,48,256]{2,1,0:T(8,128)(2,1)S(1)}, u32[]{:S(2)}, u32[]{:S(2)}) collective-permute-start(bf16[2,48,256]{2,1,0:T(8,128)(2,1)S(1)} %get-tuple-element.80), channel_id=1, source_target_pairs={{0,48},{16,32},{32,16},{48,0},{64,112},{80,96},{96,80},{112,64},{1... | collective-permute-start | bytes 147464 | tf_op jit(solution)/shard_map/ppermute | solution.py:289
  107.8 5.4 %collective-permute-start.37 = (bf16[2,48,256]{2,1,0:T(8,128)(2,1)S(1)}, bf16[2,48,256]{2,1,0:T(8,128)(2,1)S(1)}, u32[]{:S(2)}, u32[]{:S(2)}) collective-permute-start(bf16[2,48,256]{2,1,0:T(8,128)(2,1)S(1)} %get-tuple-element.81), channel_id=1, source_target_pairs={{0,32},{16,48},{32,0},{48,16},{64,96},{80,112},{96,64},{112,80},{1... | collective-permute-start | bytes 147464 | tf_op jit(solution)/shard_map/ppermute | solution.py:289
  107.8 5.4 %collective-permute-start.38 = (bf16[2,48,256]{2,1,0:T(8,128)(2,1)S(1)}, bf16[2,48,256]{2,1,0:T(8,128)(2,1)S(1)}, u32[]{:S(2)}, u32[]{:S(2)}) collective-permute-start(bf16[2,48,256]{2,1,0:T(8,128)(2,1)S(1)} %get-tuple-element.82), channel_id=1, source_target_pairs={{0,16},{16,0},{32,48},{48,32},{64,80},{80,64},{96,112},{112,96},{1... | collective-permute-start | bytes 147464 | tf_op jit(solution)/shard_map/ppermute | solution.py:289
  (12 other events, 184.2 us)
